TPU v7x, 256 devices: a whole 4x4x8 slice. The times are simulated.
256 devices in a mesh: nodes: 64 (over x, z, core), mp: 4 (over y).
Axes of the slice: x: 4, y: 4, z: 8, core: 2. Of those that a mesh axis runs over, the one named last changes fastest.
Arguments:
- tokens: bfloat16 [2048, 64, 768], P('nodes'), may hold values from -32 to 32
- w_query: bfloat16 [768, 768], P('mp'), may hold values from -0.5 to 0.5
- w_key: bfloat16 [768, 768], P('mp'), may hold values from -0.5 to 0.5
- w_value: bfloat16 [768, 768], P('mp'), may hold values from -0.21875 to 0.21875
- grad_out: bfloat16 [2048, 12, 4096], P('nodes', 'mp'), may hold values from -6 to 6
- owned_cls: bfloat16 [768, 131072], P('mp', 'nodes'), may hold values from -24 to 24
- send_rows: int32 [64, 64, 32], P('nodes'), may hold values from 0 to 2047
- neigh_slot: int32 [2048, 2, 32], P('nodes'), may hold values from 0 to 2047
- neigh_count: int32 [2048, 2], P('nodes'), may hold values from 1 to 32
Outputs:
- context: bfloat16 [2048, 12, 4096], P('nodes', 'mp')
- grad_query: float32 [768, 768], P('mp')
- grad_key: float32 [768, 768], P('mp')
- grad_value: float32 [768, 768], P('mp')
- grad_cls: float32 [768, 131072], P('mp', 'nodes')
Inputs may be any that keep to these rules, and one draw needn't show every extreme that they name: send_rows[o, r, :] are rows of owner o's own block; rows may repeat. `neigh_slot`: entries with k >= neigh_count[c, t] are not used.
All inputs are finite; a program needn't handle non-finite values.
Results may differ from a plain program's by a relative error of at most 0.012.
The roundings to bfloat16 on the way count: a program that leaves them out, or rounds other values in their place, can miss the bound.
Values may be sent and summed in bfloat16 or wider, within the bound.
No kernel may reach another device: no remote copies, remote signals or barrier semaphores. Data moves between devices by JAX's collectives and lax.ppermute only.
A program may use at most 128 MiB of HBM per device.

v0:
```python
import math

import jax
import jax.numpy as jnp
from jax import lax
from jax.sharding import PartitionSpec as P

HD = 64


def widen_columns(features):
    return lax.all_gather(features, "mp", axis=0, tiled=True)


def local_attend(tokens, virtual, w_query, w_key, w_value, grad_out):
    centres, length, model_width = tokens.shape
    local_width = w_query.shape[0]
    head_count = local_width // HD
    type_count = virtual.shape[1]
    span = type_count + length
    key_input = jnp.concatenate([virtual, tokens], axis=1)
    flat_tokens = tokens.reshape(-1, model_width)
    flat_keys = key_input.reshape(-1, model_width)
    queries = (
        jnp.einsum("nd,od->no", flat_tokens, w_query, preferred_element_type=jnp.float32)
        .astype(jnp.bfloat16)
        .reshape(centres, length, head_count, HD)
    )
    keys = (
        jnp.einsum("nd,od->no", flat_keys, w_key, preferred_element_type=jnp.float32)
        .astype(jnp.bfloat16)
        .reshape(centres, span, head_count, HD)
    )
    values = (
        jnp.einsum("nd,od->no", flat_keys, w_value, preferred_element_type=jnp.float32)
        .astype(jnp.bfloat16)
        .reshape(centres, span, head_count, HD)
    )
    score_scale = 1.0 / math.sqrt(HD)
    scores = (
        jnp.einsum("clhe,cmhe->chlm", queries, keys, preferred_element_type=jnp.float32)
        * score_scale
    )
    attn_probs = jax.nn.softmax(scores, axis=-1)
    probs_low = attn_probs.astype(jnp.bfloat16)
    context = jnp.einsum(
        "chlm,cmhe->chle", probs_low, values, preferred_element_type=jnp.float32
    ).astype(jnp.bfloat16)
    grad_heads = grad_out.reshape(centres, head_count, length, HD)
    prob_grads = jnp.einsum(
        "chle,cmhe->chlm", grad_heads, values, preferred_element_type=jnp.float32
    )
    value_grads = jnp.einsum(
        "chlm,chle->cmhe", probs_low, grad_heads, preferred_element_type=jnp.float32
    ).astype(jnp.bfloat16)
    score_grads = (
        attn_probs
        * (prob_grads - jnp.sum(prob_grads * attn_probs, axis=-1, keepdims=True))
        * score_scale
    )
    score_low = score_grads.astype(jnp.bfloat16)
    query_grads = jnp.einsum(
        "chlm,cmhe->clhe", score_low, keys, preferred_element_type=jnp.float32
    ).astype(jnp.bfloat16)
    key_grads = jnp.einsum(
        "chlm,clhe->cmhe", score_low, queries, preferred_element_type=jnp.float32
    ).astype(jnp.bfloat16)
    part_query = jnp.einsum(
        "no,nd->od",
        query_grads.reshape(-1, local_width),
        flat_tokens,
        preferred_element_type=jnp.float32,
    )
    part_key = jnp.einsum(
        "no,nd->od",
        key_grads.reshape(-1, local_width),
        flat_keys,
        preferred_element_type=jnp.float32,
    )
    part_value = jnp.einsum(
        "no,nd->od",
        value_grads.reshape(-1, local_width),
        flat_keys,
        preferred_element_type=jnp.float32,
    )
    virtual_key = key_grads[:, :type_count].reshape(-1, local_width)
    virtual_value = value_grads[:, :type_count].reshape(-1, local_width)
    virtual_grads = jnp.einsum(
        "no,od->dn", virtual_key, w_key, preferred_element_type=jnp.float32
    ) + jnp.einsum("no,od->dn", virtual_value, w_value, preferred_element_type=jnp.float32)
    return (
        context.reshape(centres, head_count, length * HD),
        part_query,
        part_key,
        part_value,
        virtual_grads,
    )


def body(tokens, w_query, w_key, w_value, grad_out, owned_cls, send_rows, neigh_slot, neigh_count):
    centres = tokens.shape[0]
    model_width = tokens.shape[2]
    local_width = owned_cls.shape[0]
    own_rows = owned_cls.shape[1]
    type_count = neigh_slot.shape[1]
    slot_width = neigh_slot.shape[2]
    send_flat = send_rows[0].reshape(-1)
    outgoing = jnp.take(owned_cls, send_flat, axis=1)
    fetched = lax.all_to_all(outgoing, "nodes", split_axis=1, concat_axis=1, tiled=True)
    slots_total = fetched.shape[1]
    pairs = centres * type_count
    counts = neigh_count.reshape(-1).astype(jnp.float32)
    live_mask = lax.broadcasted_iota(jnp.int32, neigh_slot.shape, 2) < neigh_count[:, :, None]
    live_float = live_mask.astype(jnp.float32).reshape(-1)
    pair_index = lax.broadcasted_iota(jnp.int32, (pairs, slot_width), 0).reshape(-1)
    mixing = (
        jnp.zeros((pairs, slots_total), jnp.float32)
        .at[pair_index, neigh_slot.reshape(-1)]
        .add(live_float)
    )
    mixing_low = mixing.astype(jnp.bfloat16)
    full_table = widen_columns(fetched)
    summed = jnp.einsum("dr,nr->dn", full_table, mixing_low, preferred_element_type=jnp.float32)
    virtual_cols = (summed / counts[None, :]).astype(jnp.bfloat16)
    virtual = virtual_cols.T.reshape(centres, type_count, model_width)
    context, part_query, part_key, part_value, virtual_grads = local_attend(
        tokens, virtual, w_query, w_key, w_value, grad_out
    )
    summed_weights = lax.psum((part_query, part_key, part_value), "nodes")
    shared_grad = (
        lax.psum_scatter(
            virtual_grads.astype(jnp.bfloat16), "mp", scatter_dimension=0, tiled=True
        ).astype(jnp.float32)
        / counts[None, :]
    )
    slot_grads = jnp.dot(
        shared_grad, mixing, precision=lax.Precision.HIGHEST, preferred_element_type=jnp.float32
    )
    returned = lax.all_to_all(
        slot_grads.astype(jnp.bfloat16), "nodes", split_axis=1, concat_axis=1, tiled=True
    ).astype(slot_grads.dtype)
    grad_cls = jnp.zeros((local_width, own_rows), jnp.float32).at[:, send_flat].add(returned)
    return (context, summed_weights[0], summed_weights[1], summed_weights[2], grad_cls)


def solution(mesh):
    in_specs = (
        P("nodes", None, None),
        P("mp", None),
        P("mp", None),
        P("mp", None),
        P("nodes", "mp", None),
        P("mp", "nodes"),
        P("nodes", None, None),
        P("nodes", None, None),
        P("nodes", None),
    )
    out_specs = (
        P("nodes", "mp", None),
        P("mp", None),
        P("mp", None),
        P("mp", None),
        P("mp", "nodes"),
    )
    return jax.shard_map(body, mesh=mesh, in_specs=in_specs, out_specs=out_specs, check_vma=False)
```

profile of v0, /device:TPU:8, one launch (start us, length us, event | category | flops | bytes accessed | tf_op | source)
XLA Modules:
  0.0 523.2 jit_solution(8477868783395647791)
XLA Ops:
  7.2 0.8 copy.74
  8.1 0.7 compare_and_fusion
  8.8 1.4 copy.75
  10.3 0.1 copy.73
  10.4 7.5 %gather_fusion = bf16[2048,192]{1,0:T(8,128)(2,1)S(1)} fusion(bf16[192,2048]{0,1:T(8,128)(2,1)S(1)} %copy.75, s32[2048]{0:T(1024)S(1)} %broadcast_clamp_fusion), kind=kCustom, calls=%fused_computation | custom fusion | bytes 1581056 | tf_op jit(solution)/shard_map/jit(_take)/gather | solution.py:108
  18.0 0.4 broadcast_select_fusion
  18.5 40.3 %all_to_all.18 = bf16[192,64,32]{0,2,1:T(8,128)(2,1)} all-to-all(bf16[192,64,32]{0,2,1:T(8,128)(2,1)S(1)} %broadcast_select_fusion), channel_id=1, replica_groups=mesh['nodes'=64,'mp'=4] {'nodes'}, dimensions={1} | all-to-all | bytes 1572864 | tf_op jit(solution)/shard_map/all_to_all | solution.py:109
  58.7 2.2 copy.76
  61.1 0.1 reshape.177
  61.3 0.1 compare_convert_fusion
  61.6 0.1 and_reduce_fusion
  61.7 12.3 %scatter_custom_fusion.1 = f32[131072]{0:T(1024)} fusion(s32[2048]{0:T(1024)S(1)} %broadcast_select_fusion.1, f32[2048]{0:T(1024)S(1)} %reshape.213, f32[]{:T(128)} %constant.8.clone.1), kind=kCustom, calls=%fused_computation.49 | custom fusion | flops 2048 | bytes 524292
  74.0 1.9 reshape.192
  76.0 0.1 convert_element_type.83
  76.1 3.0 convolution_convert_fusion.2
  79.1 3.4 reshape.175
  82.6 3.5 reshape.183
  86.0 13.8 %all-gather.2.cloned.1.call-done = bf16[768,2048]{1,0:T(8,128)(2,1)} async-done(((bf16[192,2048]{1,0:T(8,128)(2,1)}), bf16[768,2048]{1,0:T(8,128)(2,1)}) %all-gather.2.cloned.1.call-update) | async-done | bytes 3145744 | tf_op jit(solution)/shard_map/all_gather | solution.py:12
  99.9 3.1 fusion.24
  103.0 0.7 reshape.178
  103.7 4.6 pad_maximum_fusion
  108.3 3.1 reshape.179
  111.4 3.1 convolution_convert_fusion
  114.5 6.8 %reshape.181 = bf16[32,66,3,64]{1,0,3,2:T(8,128)(2,1)} reshape(bf16[2112,192]{0,1:T(8,128)(2,1)} %convolution_convert_fusion) | data formatting | bytes 1622016 | tf_op jit(solution)/shard_map/reshape | solution.py:37
  121.3 2.1 convolution_convert_fusion.1
  123.5 7.0 %reshape.180 = bf16[32,66,3,64]{1,0,3,2:T(8,128)(2,1)} reshape(bf16[2112,192]{0,1:T(8,128)(2,1)} %convolution_convert_fusion.1) | data formatting | bytes 1622016 | tf_op jit(solution)/shard_map/reshape | solution.py:32
  130.4 3.4 fusion.14
  133.9 3.2 fusion.49
  137.2 0.9 copy-done.4
  138.1 2.7 fusion.18
  140.7 39.7 %fusion.10 = bf16[32,64,3,64]{1,3,2,0:T(8,128)(2,1)} fusion(f32[32,3,66,64]{2,3,1,0:T(8,128)} %fusion.18, bf16[32,66,3,64]{1,0,3,2:T(8,128)(2,1)} %reshape.180, f32[32,3,64,66]{3,2,1,0:T(8,128)} %get-tuple-element.29, f32[32,3,64]{2,1,0:T(4,128)} %get-tuple-element.28), kind=kOutput, calls=%fused_computation.26 | convolution fusion | flops 55142464 | bytes 4866048 | tf_op jit(solution)/shard_map/chlm,cmhe->clhe/dot_general | solution.py:62
  180.5 40.3 %fusion.11 = bf16[32,66,3,64]{1,3,2,0:T(8,128)(2,1)} fusion(f32[32,3,66,64]{2,3,1,0:T(8,128)} %fusion.18, bf16[32,64,3,64]{1,0,3,2:T(8,128)(2,1)} %reshape.175, f32[32,3,64,66]{3,2,1,0:T(8,128)} %get-tuple-element.29, f32[32,3,64]{2,1,0:T(4,128)} %get-tuple-element.28), kind=kOutput, calls=%fused_computation.27 | convolution fusion | flops 55154752 | bytes 4866048 | tf_op jit(solution)/shard_map/chlm,clhe->cmhe/dot_general | solution.py:65
  220.7 15.9 %fusion.12 = bf16[32,66,3,64]{1,3,2,0:T(8,128)(2,1)} fusion(bf16[32,3,64,64]{3,2,0,1:T(8,128)(2,1)} %reshape.183, f32[32,3,64]{2,1,0:T(4,128)} %get-tuple-element.28, f32[32,3,64,66]{3,2,1,0:T(8,128)} %copy-done.2), kind=kOutput, calls=%fused_computation.28 | convolution fusion | flops 54343744 | bytes 3244032 | tf_op jit(solution)/shard_map/chlm,chle->cmhe/dot_general | solution.py:53
  236.6 3.6 copy.85
  240.2 3.5 reshape.184
  243.7 3.6 copy.87
  247.3 4.2 reshape.185
  251.4 3.6 copy.89
  255.0 4.2 reshape.186
  259.2 2.7 copy.90
  261.8 1.6 reshape.187
  263.4 1.6 fusion.53
  265.0 2.8 copy.91
  267.8 1.6 reshape.188
  269.4 1.9 fusion.26
  271.2 1.7 copy.97
  272.9 2.8 fusion.51
  275.8 19.8 %reduce-scatter.4.cloned.1.call-done = bf16[192,64]{1,0:T(8,128)(2,1)} async-done(((bf16[768,64]{1,0:T(8,128)(2,1)}), bf16[192,64]{1,0:T(8,128)(2,1)}) %reduce-scatter.4.cloned.1.call-update) | async-done | bytes 24592
  295.5 1.5 copy.98
  297.0 3.4 convolution_convert_fusion.3
  300.5 2.2 copy.92
  302.7 10.7 %all-to-all-start.1 = ((bf16[192,64,32]{0,2,1:T(8,128)(2,1)}), bf16[192,64,32]{0,2,1:T(8,128)(2,1)}, u32[]{:S(2)}, u32[]{:S(2)}) async-start(bf16[192,64,32]{0,2,1:T(8,128)(2,1)} %bitcast.91), calls=%async_computation.1 | async-start | bytes 2097152 | tf_op jit(solution)/shard_map/all_to_all | solution.py:139
  313.5 3.8 fusion.50
  317.3 1.7 fusion.52
  319.0 14.1 %convolution_convert_fusion.7 = bf16[32,3,64,64]{3,2,1,0:T(8,128)(2,1)S(1)} fusion(bf16[32,66,3,64]{1,0,3,2:T(8,128)(2,1)} %reshape.181, f32[32,3,64]{2,1,0:T(4,128)} %get-tuple-element.28, f32[32,3,64,66]{3,2,1,0:T(8,128)} %copy-done.2), kind=kOutput, calls=%fused_computation.23 | convolution fusion | flops 54331456 | bytes 3244032 | tf_op jit(solution)/shard_map/chlm,cmhe->chle/dot_general | solution.py:46
  333.1 1.4 reshape.217
  334.5 1.5 copy.95
  336.0 5.9 %all-to-all-done.1 = bf16[192,64,32]{0,2,1:T(8,128)(2,1)} async-done(((bf16[192,64,32]{0,2,1:T(8,128)(2,1)}), bf16[192,64,32]{0,2,1:T(8,128)(2,1)}, u32[]{:S(2)}, u32[]{:S(2)}) %all-to-all-start.1) | async-done | bytes 786464 | tf_op jit(solution)/shard_map/all_to_all | solution.py:139
  341.8 11.4 %scatter_custom_fusion = f32[192,2048]{0,1:T(8,128)S(1)} fusion(s32[2048]{0:T(1024)S(1)} %bitcast.95, bf16[192,2048]{0,1:T(8,128)(2,1)} %bitcast.16, f32[]{:T(128)} %constant.8.clone.1), kind=kCustom, calls=%fused_computation.19 | custom fusion | flops 786432 | bytes 2359300 | tf_op jit(solution)/shard_map/scatter-add | solution.py:142
  353.3 1.7 copy.93
  355.0 155.8 %all-reduce.3.cloned.1.call-done = (f32[192,768]{1,0:T(8,128)}, f32[192,768]{1,0:T(8,128)}, f32[192,768]{1,0:T(8,128)}) async-done(((f32[192,768]{1,0:T(8,128)}, f32[192,768]{1,0:T(8,128)}, f32[192,768]{1,0:T(8,128)}), (f32[192,768]{1,0:T(8,128)}, f32[192,768]{1,0:T(8,128)}, f32[192,768]{1,0:T(8,128)})) %all-reduce.3.cloned.1.call-update) | async-done | bytes 1769488 | tf_op jit(solution)/shard_map/psum | solution.py:129
  510.7 1.9 copy.118
  512.7 1.9 copy.119
  514.6 1.9 copy.120
  (37 shorter events, 0.8 us)
Async XLA Ops:
  7.2 114.2 %copy-start = (bf16[192,768]{1,0:T(8,128)(2,1)S(1)}, bf16[192,768]{1,0:T(8,128)(2,1)}, u32[]{:S(2)}) copy-start(bf16[192,768]{1,0:T(8,128)(2,1)} %param.11) | copy-start | bytes 884740
  7.2 92.7 %all-gather.2.cloned.1.call-start = ((), (), s32[]{:S(2)}) async-start(), calls=%async_computation.3 | async-start | bytes 3932160 | tf_op jit(solution)/shard_map/all_gather | solution.py:12
  17.9 43.0 %copy-start.7 = (s32[32,2]{0,1:T(2,128)S(1)}, s32[32,2]{0,1:T(2,128)}, u32[]{:S(2)}) copy-start(s32[32,2]{0,1:T(2,128)} %param.17) | copy-start | bytes 772
  18.0 43.1 %copy-start.6 = (s32[32,2,32]{2,1,0:T(2,128)S(1)}, s32[32,2,32]{2,1,0:T(2,128)}, u32[]{:S(2)}) copy-start(s32[32,2,32]{2,1,0:T(2,128)} %param.16) | copy-start | bytes 24580
  18.0 43.5 %copy-start.8 = (s32[2]{0:T(128)S(1)}, s32[2]{0:T(128)}, u32[]{:S(2)}) copy-start(s32[2]{0:T(128)} %constant.34) | copy-start | bytes 28
  18.0 43.6 %copy-start.9 = (s32[2]{0:T(128)S(1)}, s32[2]{0:T(128)}, u32[]{:S(2)}) copy-start(s32[2]{0:T(128)} %constant.37) | copy-start | bytes 28
  18.5 57.7 %copy-start.1 = (bf16[32,64,768]{2,1,0:T(8,128)(2,1)S(1)}, bf16[32,64,768]{2,1,0:T(8,128)(2,1)}, u32[]{:S(2)}) copy-start(bf16[32,64,768]{2,1,0:T(8,128)(2,1)} %param.9) | copy-start | bytes 9437188
  60.9 234.6 %reduce-scatter.4.cloned.1.call-start = ((), (), s32[]{:S(2)}) async-start(), calls=%async_computation.4 | async-start | bytes 245760
  133.9 3.3 copy-start.2
  133.9 3.3 copy-start.3
  133.9 4.2 copy-start.4
  302.7 39.1 %all-to-all-start.1 = ((bf16[192,64,32]{0,2,1:T(8,128)(2,1)}), bf16[192,64,32]{0,2,1:T(8,128)(2,1)}, u32[]{:S(2)}, u32[]{:S(2)}) async-start(bf16[192,64,32]{0,2,1:T(8,128)(2,1)} %bitcast.91), calls=%async_computation.1 | async-start | bytes 2097152 | tf_op jit(solution)/shard_map/all_to_all | solution.py:139
  313.4 197.3 %all-reduce.3.cloned.1.call-start = ((), (), s32[]{:S(2)}) async-start(), calls=%async_computation.5 | async-start | bytes 3538944 | tf_op jit(solution)/shard_map/psum | solution.py:129
  313.5 3.8 copy-start.5
Sparse Core Ops, SparseCore 0:
  61.0 38.7 all-gather.1
  273.1 22.4 reduce-scatter.3
  319.1 191.5 all-reduce.2
where the time goes:
time: 528 us; the launch traced here: 523 us
  waiting for transfers between devices  195 us (37%)
  matrix products  143 us (27%)
  local copies, waits for them, and re-layouts  86.9 us (16%)
  blocking collectives  40.3 us (8%)
  other arithmetic  33.1 us (6%)
  between operations  14.3 us (3%)
  starting transfers between devices  10.8 us (2%)
    psum x1, waiting for transfers between devices, body(): summed_weights = lax.psum((part_query, part_key, part_value), 'nodes')  156 us
    dot_general x1, matrix products, local_attend(): jnp.einsum('chlm,clhe->cmhe', score_low, queries, preferred_element_type=...  40.3 us
    all_to_all x1, blocking collectives, body(): lax.all_to_all(outgoing, 'nodes', split_axis=1, concat_axis=1, tiled=True)  40.3 us
    dot_general x1, matrix products, local_attend(): jnp.einsum('chlm,cmhe->clhe', score_low, keys, preferred_element_type=jnp...  39.7 us
    unnamed x4, waiting for transfers between devices  19.8 us
    dot_general x1, matrix products, local_attend(): jnp.einsum('chlm,chle->cmhe', probs_low, grad_heads, preferred_element_ty...  15.9 us
    dot_general x1, matrix products, local_attend(): jnp.einsum('chlm,cmhe->chle', probs_low, values, preferred_element_type=j...  14.1 us
    unnamed x29, local copies, waits for them, and re-layouts  14 us
  transfers between devices with their start and end apart: 4, of which 4 were waited for; matrix products, arithmetic and copies ran while one was open for 12% of the time, Pallas kernels for 0%

commit v1 on v0

v1 whole, which is shorter than its diff:
```python
import jax
import jax.numpy as jnp
from jax import lax
from jax.experimental import pallas as pl
from jax.experimental.pallas import tpu as pltpu
from jax.sharding import PartitionSpec as P

HD = 64
BF = jnp.bfloat16
F32 = jnp.float32
CHIPS = 32
CENTRES = 32
GROUP = 4
VMEM_LIMIT = 60 * 1024 * 1024

XZ_GROUPS = [[chip * 2 + core for chip in range(CHIPS)] for core in range(2)]
CORE_SWAP = [(dev, dev ^ 1) for dev in range(2 * CHIPS)]


def nt(a, b):
    return lax.dot_general(a, b, (((1,), (1,)), ((), ())), preferred_element_type=F32)


def nn(a, b):
    return lax.dot_general(a, b, (((1,), (0,)), ((), ())), preferred_element_type=F32)


def tn(a, b):
    return lax.dot_general(a, b, (((0,), (0,)), ((), ())), preferred_element_type=F32)


def core_swap(x):
    return lax.ppermute(x, "nodes", CORE_SWAP)


def chip_exchange(x):
    return lax.all_to_all(
        x, "nodes", split_axis=0, concat_axis=0, tiled=True, axis_index_groups=XZ_GROUPS
    )


def gather_kernel(index_ref, table_ref, out_ref):
    rows = table_ref.shape[1]
    row = lax.broadcasted_iota(jnp.int32, (rows, 256), 0)
    select = jnp.where(row == index_ref[0], 1.0, 0.0).astype(BF)
    picked = nn(table_ref[...], select)
    turned = picked.T.astype(BF)
    for chip in range(4):
        own = turned[32 * chip : 32 * chip + 32]
        other = turned[128 + 32 * chip : 160 + 32 * chip]
        out_ref[chip, 0:32, :] = own[:, 0:128]
        out_ref[chip, 32:64, :] = other[:, 0:128]
        out_ref[chip, 64:96, 0:64] = own[:, 128:192]
        out_ref[chip, 64:96, 64:128] = other[:, 128:192]


def gather_rows(index, table):
    rows = table.shape[1]
    return pl.pallas_call(
        gather_kernel,
        out_shape=jax.ShapeDtypeStruct((CHIPS, 96, 128), BF),
        grid=(8,),
        in_specs=[
            pl.BlockSpec((1, 1, 256), lambda i: (i, 0, 0)),
            pl.BlockSpec((192, rows), lambda i: (0, 0)),
        ],
        out_specs=pl.BlockSpec((4, 96, 128), lambda i: (i, 0, 0)),
        compiler_params=pltpu.CompilerParams(vmem_limit_bytes=VMEM_LIMIT),
        name="gather_rows",
    )(index, table)


def mixing_kernel(key_ref, out_ref):
    for block in range(8):
        slot = lax.broadcasted_iota(jnp.int32, (128, 128), 0) + 128 * block
        total = jnp.zeros((128, 128), F32)
        for k in range(32):
            total = total + jnp.where(slot == key_ref[k : k + 1, :], 1.0, 0.0)
        out_ref[128 * block : 128 * block + 128, :] = total.astype(BF)


def make_mixing(keys):
    return pl.pallas_call(
        mixing_kernel,
        out_shape=jax.ShapeDtypeStruct((1024, 128), BF),
        name="make_mixing",
    )(keys)


def virtual_kernel(rows_ref, mix_ref, own_ref, other_ref):
    mix = mix_ref[...]
    first = tn(mix, rows_ref[:, 0:32, :].reshape(1024, 128))
    second = tn(mix, rows_ref[:, 32:64, :].reshape(1024, 128))
    both = tn(mix, rows_ref[:, 64:96, :].reshape(1024, 128))
    own_ref[:, 0:128] = first[0:64]
    own_ref[:, 128:192] = both[0:64, 0:64]
    other_ref[:, 0:128] = second[64:128]
    other_ref[:, 128:192] = both[64:128, 64:128]


def mix_rows(rows, mix):
    part = jax.ShapeDtypeStruct((64, 192), F32)
    return pl.pallas_call(virtual_kernel, out_shape=(part, part), name="mix_rows")(rows, mix)


def attend_kernel(
    place_ref, tok_ref, grad_ref, virt_ref, wq_ref, wk_ref, wv_ref, wk4_ref, wv4_ref,
    ctx_ref, dw_ref, vg0_ref, vg1_ref, vg2_ref, vg3_ref,
    acc_ref, kvirt_ref, vvirt_ref, dkvirt_ref, dvvirt_ref,
):
    step = pl.program_id(0)
    width = 192

    @pl.when(step == 0)
    def _():
        acc_ref[...] = jnp.zeros_like(acc_ref)
        row = lax.broadcasted_iota(jnp.int32, (512, 64), 0)
        pair = lax.broadcasted_iota(jnp.int32, (512, 64), 1)
        spread = jnp.where((row // 16 == pair // 2) & (row % 16 == pair % 2), 1.0, 0.0).astype(BF)
        virt = virt_ref[...]
        kvirt_ref[...] = nn(spread, nt(virt, wk_ref[...]).astype(BF)).astype(BF)
        vvirt_ref[...] = nn(spread, nt(virt, wv_ref[...]).astype(BF)).astype(BF)

    tok = tok_ref[...]
    queries = nt(tok, wq_ref[...]).astype(BF)
    keys = nt(tok, wk_ref[...]).astype(BF)
    values = nt(tok, wv_ref[...]).astype(BF)
    head_row = lax.broadcasted_iota(jnp.int32, (width, width), 0) // HD
    head_col = lax.broadcasted_iota(jnp.int32, (width, width), 1) // HD
    blocks = jnp.where(head_row == head_col, 1.0, 0.0).astype(BF)
    valid = lax.broadcasted_iota(jnp.int32, (80, width), 0) < 66
    lane = lax.broadcasted_iota(jnp.int32, (HD, width), 1)

    def heads_of(full):
        return jnp.where(
            lane < 64, full[0:64], jnp.where(lane < 128, full[64:128], full[128:192])
        )

    dqs, dks, dvs = [], [], []
    for i in range(GROUP):
        at = pl.multiple_of((step * GROUP + i) * 16, 16)
        span = slice(64 * i, 64 * i + 64)
        key = jnp.concatenate([keys[span], kvirt_ref[pl.ds(at, 16), :]], axis=0)
        value = jnp.concatenate([values[span], vvirt_ref[pl.ds(at, 16), :]], axis=0)
        query = queries[span]
        grad = grad_ref[span, :]
        query_blocks = jnp.concatenate([query, query, query], axis=0) * blocks
        grad_blocks = jnp.concatenate([grad, grad, grad], axis=0) * blocks
        scores = jnp.where(valid, nt(key, query_blocks) * 0.125, -1e30)
        top = jnp.max(scores, axis=0, keepdims=True)
        powers = jnp.exp(scores - top)
        powers = jnp.where(valid, powers, 0.0)
        probs = powers * (1.0 / jnp.sum(powers, axis=0, keepdims=True))
        low = probs.astype(BF)
        prob_grads = nt(value, grad_blocks)
        inner = jnp.sum(prob_grads * probs, axis=0, keepdims=True)
        score_low = (probs * (prob_grads - inner) * 0.125).astype(BF)
        ctx_ref[span, :] = heads_of(tn(low, value)).astype(BF)
        dq = heads_of(tn(score_low, key)).astype(BF)
        dv = nn(low, grad_blocks).astype(BF)
        dk = nn(score_low, query_blocks).astype(BF)
        dkvirt_ref[pl.ds(at, 16), :] = dk[64:80]
        dvvirt_ref[pl.ds(at, 16), :] = dv[64:80]
        dqs.append(dq)
        dks.append(dk[0:64])
        dvs.append(dv[0:64])
    acc_ref[0:192, :] += tn(jnp.concatenate(dqs, axis=0), tok)
    acc_ref[192:384, :] += tn(jnp.concatenate(dks, axis=0), tok)
    acc_ref[384:576, :] += tn(jnp.concatenate(dvs, axis=0), tok)

    @pl.when(step == pl.num_programs(0) - 1)
    def _():
        pair = lax.broadcasted_iota(jnp.int32, (64, 512), 0)
        row = lax.broadcasted_iota(jnp.int32, (64, 512), 1)
        collect = jnp.where((row // 16 == pair // 2) & (row % 16 == pair % 2), 1.0, 0.0).astype(BF)
        dk = nn(collect, dkvirt_ref[...]).astype(BF)
        dv = nn(collect, dvvirt_ref[...]).astype(BF)
        virt = virt_ref[...]
        acc_ref[192:384, :] += tn(dk, virt)
        acc_ref[384:576, :] += tn(dv, virt)
        own = place_ref[0]
        for d, ref in enumerate((vg0_ref, vg1_ref, vg2_ref, vg3_ref)):
            at = (own + d) % 4
            ref[...] = (nn(dk, wk4_ref[at]) + nn(dv, wv4_ref[at])).astype(ref.dtype)
        for core in range(2):
            @pl.when(place_ref[1] == core)
            def _():
                for t in range(3):
                    keep = 3 * core + t
                    give = 3 * (1 - core) + t
                    dw_ref[0, t] = acc_ref[:, 128 * keep : 128 * keep + 128]
                    dw_ref[1, t] = acc_ref[:, 128 * give : 128 * give + 128]


def attend(place, tokens, grads, virtual, wq, wk, wv, wk4, wv4):
    rows = 64 * GROUP
    steps = CENTRES // GROUP
    fixed2 = lambda i: (0, 0)
    fixed3 = lambda i: (0, 0, 0)
    out_shape = (
        jax.ShapeDtypeStruct((2048, 192), BF),
        jax.ShapeDtypeStruct((2, 3, 576, 128), F32),
        jax.ShapeDtypeStruct((64, 192), F32),
        jax.ShapeDtypeStruct((64, 192), BF),
        jax.ShapeDtypeStruct((64, 192), BF),
        jax.ShapeDtypeStruct((64, 192), BF),
    )
    small = pl.BlockSpec((64, 192), fixed2)
    weight = pl.BlockSpec((192, 768), fixed2)
    return pl.pallas_call(
        attend_kernel,
        out_shape=out_shape,
        grid=(steps,),
        in_specs=[
            pl.BlockSpec(memory_space=pltpu.SMEM),
            pl.BlockSpec((rows, 768), lambda i: (i, 0)),
            pl.BlockSpec((rows, 192), lambda i: (i, 0)),
            pl.BlockSpec((64, 768), fixed2),
            weight, weight, weight,
            pl.BlockSpec((4, 192, 192), fixed3),
            pl.BlockSpec((4, 192, 192), fixed3),
        ],
        out_specs=(
            pl.BlockSpec((rows, 192), lambda i: (i, 0)),
            pl.BlockSpec((2, 3, 576, 128), lambda i: (0, 0, 0, 0)),
            small, small, small, small,
        ),
        scratch_shapes=[
            pltpu.VMEM((576, 768), F32),
            pltpu.VMEM((512, 192), BF),
            pltpu.VMEM((512, 192), BF),
            pltpu.VMEM((512, 192), BF),
            pltpu.VMEM((512, 192), BF),
        ],
        compiler_params=pltpu.CompilerParams(vmem_limit_bytes=VMEM_LIMIT),
        name="attend",
    )(place, tokens, grads, virtual, wq, wk, wv, wk4, wv4)


def spread_kernel(own_ref, other_ref, mix_ref, weights_ref, out_ref):
    mix = mix_ref[...]
    zeros = jnp.zeros((64, 192), BF)

    def split(x):
        high = x.astype(BF)
        return high, (x - high.astype(F32)).astype(BF)

    own_high, own_low = split(own_ref[...])
    other_high, other_low = split(other_ref[...])
    stack = lambda a, b: jnp.concatenate([a, b], axis=0)
    own = nn(mix, stack(own_high, zeros)) + nn(mix, stack(own_low, zeros))
    other = nn(mix, stack(zeros, other_high)) + nn(mix, stack(zeros, other_low))
    own = own.astype(BF)
    other = other.astype(BF)
    out_ref[:, 0:32, :] = own[:, 0:128].reshape(CHIPS, 32, 128)
    out_ref[:, 32:64, :] = other[:, 0:128].reshape(CHIPS, 32, 128)
    out_ref[:, 64:96, 0:64] = own[:, 128:192].reshape(CHIPS, 32, 64)
    out_ref[:, 64:96, 64:128] = other[:, 128:192].reshape(CHIPS, 32, 64)
    total = weights_ref[0].astype(F32)
    for chip in range(1, CHIPS):
        total = total + weights_ref[chip].astype(F32)
    total = total.astype(BF)
    for chip in range(CHIPS):
        out_ref[chip, 96:160, :] = total


def spread(own, other, mix, weights):
    return pl.pallas_call(
        spread_kernel,
        out_shape=jax.ShapeDtypeStruct((CHIPS, 160, 128), BF),
        name="spread",
    )(own, other, mix, weights)


def scatter_kernel(index_ref, rows_ref, out_ref, turned_ref):
    step = pl.program_id(0)

    @pl.when(step == 0)
    def _():
        for g in range(8):
            chips = slice(4 * g, 4 * g + 4)
            first = rows_ref[chips, 0:32, :].reshape(128, 128).astype(F32).T.astype(BF)
            second = rows_ref[chips, 32:64, :].reshape(128, 128).astype(F32).T.astype(BF)
            both = rows_ref[chips, 64:96, :].reshape(128, 128).astype(F32).T.astype(BF)
            lanes = slice(256 * g, 256 * g + 128)
            more = slice(256 * g + 128, 256 * g + 256)
            turned_ref[0:128, lanes] = first
            turned_ref[128:192, lanes] = both[0:64]
            turned_ref[0:128, more] = second
            turned_ref[128:192, more] = both[64:128]

    row = lax.broadcasted_iota(jnp.int32, (256, 2048), 0) + 256 * step
    select = jnp.where(row == index_ref[...], 1.0, 0.0).astype(BF)
    out_ref[...] = nt(turned_ref[...], select)


def scatter_rows(index, rows):
    return pl.pallas_call(
        scatter_kernel,
        out_shape=jax.ShapeDtypeStruct((192, 2048), F32),
        grid=(8,),
        in_specs=[
            pl.BlockSpec((1, 2048), lambda i: (0, 0)),
            pl.BlockSpec((CHIPS, 96, 128), lambda i: (0, 0, 0)),
        ],
        out_specs=pl.BlockSpec((192, 256), lambda i: (0, i)),
        scratch_shapes=[pltpu.VMEM((192, 2048), BF)],
        compiler_params=pltpu.CompilerParams(vmem_limit_bytes=VMEM_LIMIT),
        name="scatter_rows",
    )(index, rows)


def body(tokens, w_query, w_key, w_value, grad_out, owned_cls, send_rows, neigh_slot, neigh_count):
    core = lax.axis_index("nodes") % 2
    own_mp = lax.axis_index("mp")
    place = jnp.stack([own_mp, core]).astype(jnp.int32)

    asked = send_rows.reshape(8, 4, 2, 32)
    asked = jnp.where(core == 0, asked, asked[:, :, ::-1])
    index = asked.transpose(0, 2, 1, 3).reshape(8, 1, 256)
    sent = gather_rows(index, owned_cls)

    slots = neigh_slot.reshape(64, 32)
    counts = neigh_count.reshape(64, 1)
    position = lax.broadcasted_iota(jnp.int32, (64, 32), 1)
    slots = jnp.where(position < counts, slots, -1)
    all_slots = jnp.concatenate([slots, core_swap(slots)], axis=0)
    here = (all_slots >= 0) & (((all_slots >> 5) & 1) == core)
    keys = jnp.where(here, (all_slots >> 6) * 32 + (all_slots & 31), -1).T
    mix = make_mixing(keys)

    heads = grad_out.reshape(32, 3, 64, 64).transpose(0, 2, 1, 3).reshape(2048, 192)
    wk4 = w_key.reshape(192, 4, 192).transpose(1, 0, 2)
    wv4 = w_value.reshape(192, 4, 192).transpose(1, 0, 2)

    fetched = chip_exchange(sent)
    own_part, other_part = mix_rows(fetched, mix)
    divisor = counts.astype(F32)
    local = ((own_part + core_swap(other_part)) / divisor).astype(BF)
    virtual = lax.all_gather(local, "mp", axis=1, tiled=True)

    ctx, dw, vg0, vg1, vg2, vg3 = attend(
        place, tokens.reshape(2048, 768), heads, virtual, w_query, w_key, w_value, wk4, wv4
    )
    context = ctx.reshape(32, 64, 3, 64).transpose(0, 2, 1, 3).reshape(32, 3, 4096)

    around = lambda x, d: lax.ppermute(x, "mp", [(i, (i + d) % 4) for i in range(4)])
    moved = [around(vg, d + 1) for d, vg in enumerate((vg1, vg2, vg3))]
    half = dw[0] + core_swap(dw[1])
    half = half.astype(BF).reshape(1728, 128)
    padded = jnp.pad(half, ((0, 2048 - 1728), (0, 0))).reshape(CHIPS, 64, 128)
    pieces = chip_exchange(padded)

    shared = (vg0 + moved[0].astype(F32) + moved[1].astype(F32) + moved[2].astype(F32)) / divisor
    other_shared = core_swap(shared)
    outgoing = spread(shared, other_shared, mix, pieces)
    arrived = chip_exchange(outgoing)

    mine = arrived[:, 96:160].reshape(2048, 128)[:1728]
    theirs = core_swap(mine)
    grad_cls = scatter_rows(index.reshape(1, 2048), arrived)
    first = jnp.where(core == 0, mine, theirs).reshape(3, 576, 128)
    second = jnp.where(core == 0, theirs, mine).reshape(3, 576, 128)
    grads = jnp.concatenate([first, second], axis=0).transpose(1, 0, 2).reshape(576, 768).astype(F32)
    return (context, grads[0:192], grads[192:384], grads[384:576], grad_cls)


def solution(mesh):
    in_specs = (
        P("nodes", None, None),
        P("mp", None),
        P("mp", None),
        P("mp", None),
        P("nodes", "mp", None),
        P("mp", "nodes"),
        P("nodes", None, None),
        P("nodes", None, None),
        P("nodes", None),
    )
    out_specs = (
        P("nodes", "mp", None),
        P("mp", None),
        P("mp", None),
        P("mp", None),
        P("mp", "nodes"),
    )
    return jax.shard_map(body, mesh=mesh, in_specs=in_specs, out_specs=out_specs, check_vma=False)
```

time: 528 us -> 185 us (0.35)
  waiting for transfers between devices: 195 us -> 31.7 us
  matrix products: 143 us -> 0 us
  local copies, waits for them, and re-layouts: 86.9 us -> 27.7 us
  Pallas kernels: 0 us -> 45.3 us
  other arithmetic: 33.1 us -> 2.77 us
  between operations: 14.3 us -> 0.98 us
  blocking collectives: 40.3 us -> 53 us
  starting transfers between devices: 10.8 us -> 21.4 us
    psum x1 -> x0, waiting for transfers between devices: 156 us -> none  [body(): summed_weights = lax.psum((part_query, part_key, part_value), 'nodes')]
    dot_general x16 -> x0, matrix products: 143 us -> none  [the longest x1 40.3 us: local_attend(): jnp.einsum('chlm,clhe->cmhe', score_low, queries, preferred_element_type=...]
    pallas_call x0 -> x6, Pallas kernels: none -> 45.3 us  [the longest x1 23.5 us: attend(): pl.pallas_call(attend_kernel, out_shape=out_shape, grid=(steps,), in_spec...]
    reshape x15 -> x10, local copies, waits for them, and re-layouts: 42.4 us -> 13.8 us  [the longest x4 6.48 us: body(): grad_out.reshape(32, 3, 64, 64).transpose(0, 2, 1, 3).reshape(2048, 192)]
    all_to_all x1 -> x2, waiting for transfers between devices: 5.85 us -> 26.4 us  [chip_exchange(): lax.all_to_all(x, 'nodes', split_axis=0, concat_axis=0, tiled=True, axis_...]
    unnamed x4 -> x0, waiting for transfers between devices: 19.8 us -> none
    all_gather x1 -> x0, waiting for transfers between devices: 13.8 us -> none  [widen_columns(): return lax.all_gather(features, 'mp', axis=0, tiled=True)]
    convert_element_type x7 -> x0, local copies, waits for them, and re-layouts: 13.2 us -> none  [the longest x1 3.56 us: local_attend(): query_grads = jnp.einsum('chlm,cmhe->clhe', score_low, keys, preferred_el...]
  transfers between devices with their start and end apart: 4 -> 10, of which waited for: 4 -> 6; matrix products, arithmetic and copies ran while one was open for 12% -> 11% of each run, Pallas kernels for 0% -> 5%
where the time goes in v1:
time: 185 us; the launch traced here: 183 us
  blocking collectives  53 us (29%)
  Pallas kernels  45.3 us (24%)
  waiting for transfers between devices  31.7 us (17%)
  local copies, waits for them, and re-layouts  27.7 us (15%)
  starting transfers between devices  21.4 us (12%)
  other arithmetic  2.77 us (1%)
    all_to_all x1, blocking collectives, chip_exchange(): lax.all_to_all(x, 'nodes', split_axis=0, concat_axis=0, tiled=True, axis_...  40.7 us
    all_to_all x2, waiting for transfers between devices, chip_exchange(): lax.all_to_all(x, 'nodes', split_axis=0, concat_axis=0, tiled=True, axis_...  26.4 us
    pallas_call x1, Pallas kernels, attend(): pl.pallas_call(attend_kernel, out_shape=out_shape, grid=(steps,), in_spec...  23.5 us
    all_to_all x2, starting transfers between devices, chip_exchange(): lax.all_to_all(x, 'nodes', split_axis=0, concat_axis=0, tiled=True, axis_...  16.2 us
    all_gather x1, blocking collectives, body(): virtual = lax.all_gather(local, 'mp', axis=1, tiled=True)  12.3 us
    pallas_call x1, Pallas kernels, scatter_rows(): pl.pallas_call(scatter_kernel, out_shape=jax.ShapeDtypeStruct((192, 2048)...  6.67 us
    pallas_call x1, Pallas kernels, gather_rows(): pl.pallas_call(gather_kernel, out_shape=jax.ShapeDtypeStruct((CHIPS, 96,...  6.67 us
    reshape x4, local copies, waits for them, and re-layouts, body(): grad_out.reshape(32, 3, 64, 64).transpose(0, 2, 1, 3).reshape(2048, 192)  6.48 us
  transfers between devices with their start and end apart: 10, of which 6 were waited for; matrix products, arithmetic and copies ran while one was open for 11% of the time, Pallas kernels for 5%

profile of v1, /device:TPU:8, one launch (start us, length us, event | category | flops | bytes accessed | tf_op | source)
XLA Modules:
  0.0 182.8 jit_solution(3534959614309661022)
XLA Ops:
  0.7 0.8 copy.49
  1.5 0.1 rev.3
  1.6 0.7 reshape.72.index_ref
  2.3 6.7 %gather_rows.1 = bf16[32,96,128]{2,1,0:T(8,128)(2,1)} custom-call(s32[8,1,256]{2,1,0:T(1,128)} %reshape.72.index_ref, bf16[192,2048]{1,0:T(8,128)(2,1)} %table_ref.1), custom_call_target="tpu_custom_call" | custom-call | tf_op jit(solution)/shard_map/gather_rows/pallas_call | solution.py:59
  9.0 11.3 %all-to-all-start = ((bf16[32,96,128]{2,1,0:T(8,128)(2,1)}), bf16[32,96,128]{2,1,0:T(8,128)(2,1)S(1)}, u32[]{:S(2)}, u32[]{:S(2)}) async-start(bf16[32,96,128]{2,1,0:T(8,128)(2,1)} %gather_rows.1), calls=%async_computation | async-start | bytes 1572864 | tf_op jit(solution)/shard_map/all_to_all | solution.py:37
  20.3 0.1 copy.51
  20.4 0.1 lt.17
  20.5 0.1 copy.52
  20.6 0.1 collective-permute-start
  20.7 0.4 reshape.75
  21.1 0.4 reshape.74
  21.4 1.0 copy_bitcast_fusion.3
  22.4 0.0 collective-permute-done
  22.4 0.7 select_bitcast_fusion.1.key_ref
  23.1 3.1 %make_mixing.1.mix_ref = bf16[1024,128]{1,0:T(8,128)(2,1)} custom-call(s32[32,128]{1,0:T(8,128)} %select_bitcast_fusion.1.key_ref), custom_call_target="tpu_custom_call" | custom-call | tf_op jit(solution)/shard_map/make_mixing/pallas_call | solution.py:83
  26.2 17.4 %all-to-all-done.rows_ref = bf16[32,96,128]{2,1,0:T(8,128)(2,1)S(1)} async-done(((bf16[32,96,128]{2,1,0:T(8,128)(2,1)}), bf16[32,96,128]{2,1,0:T(8,128)(2,1)S(1)}, u32[]{:S(2)}, u32[]{:S(2)}) %all-to-all-start) | async-done | bytes 786464 | tf_op jit(solution)/shard_map/all_to_all | solution.py:37
  43.7 0.9 copy-done.1
  44.5 2.3 %mix_rows.1 = (f32[64,192]{1,0:T(8,128)}, f32[64,192]{1,0:T(8,128)}) custom-call(bf16[32,96,128]{2,1,0:T(8,128)(2,1)} %copy-done.1, bf16[1024,128]{1,0:T(8,128)(2,1)} %make_mixing.1.mix_ref), custom_call_target="tpu_custom_call" | custom-call | tf_op jit(solution)/shard_map/mix_rows/pallas_call | solution.py:103
  46.8 0.0 collective-permute-start.1
  46.8 0.6 pad_add_fusion.1.place_ref
  47.4 2.5 %reshape.69 = bf16[32,3,64,64]{3,2,0,1:T(8,128)(2,1)S(1)} reshape(bf16[32,3,4096]{2,0,1:T(8,128)(2,1)} %param.13) | data formatting | bytes 1572864 | tf_op jit(solution)/shard_map/reshape | solution.py:332
  50.0 1.4 copy.48
  51.4 1.3 reshape.70
  52.7 1.3 copy.56.grad_ref
  54.0 0.0 collective-permute-done.1
  54.0 0.1 fusion.1
  54.1 12.3 %all-gather = bf16[4,192,64]{1,2,0:T(8,128)(2,1)S(1)} all-gather(bf16[1,192,64]{1,2,0:T(8,128)(2,1)S(1)} %fusion.1), channel_id=1, replica_groups=mesh['nodes'=64,'mp'=4] {'mp'}, dimensions={0}, use_global_device_ids=true | all-gather | bytes 122880 | tf_op jit(solution)/shard_map/all_gather | solution.py:340
  66.3 0.1 copy.53
  66.4 0.8 reshape.83
  67.2 23.5 %attend.1 = (bf16[2048,192]{1,0:T(8,128)(2,1)}, f32[2,3,576,128]{3,2,1,0:T(8,128)}, f32[64,192]{1,0:T(8,128)}, bf16[64,192]{1,0:T(8,128)(2,1)}, bf16[64,192]{1,0:T(8,128)(2,1)}, /*index=5*/bf16[64,192]{1,0:T(8,128)(2,1)}) custom-call(s32[2]{0:T(128)} %pad_add_fusion.1.place_ref, bf16[2048,768]{1,0:T(8,128)(2,1)} %bitcast.66, ...), custom_call_target="tpu_custom_call" | custom-call | tf_op jit(solution)/shard_map/attend/pallas_call | solution.py:210
  90.7 1.4 slice_bitcast_fusion
  92.1 0.1 collective-permute-start.6
  92.2 2.4 %collective-permute-done.6 = f32[3,576,128]{2,1,0:T(8,128)S(1)} collective-permute-done((f32[3,576,128]{2,1,0:T(8,128)S(1)}, f32[3,576,128]{2,1,0:T(8,128)S(1)}, u32[]{:S(2)}, u32[]{:S(2)}) %collective-permute-start.6) | collective-permute-done | bytes 884768 | tf_op jit(solution)/shard_map/ppermute | solution.py:33
  94.6 0.1 fusion
  94.7 0.8 pad.4
  95.6 4.9 %all-to-all-start.1 = ((bf16[32,64,128]{2,1,0:T(8,128)(2,1)}), bf16[32,64,128]{2,1,0:T(8,128)(2,1)S(1)}, u32[]{:S(2)}, u32[]{:S(2)}) async-start(bf16[32,64,128]{2,1,0:T(8,128)(2,1)} %bitcast.17), calls=%async_computation.1 | async-start | bytes 1048576 | tf_op jit(solution)/shard_map/all_to_all | solution.py:37
  100.5 0.8 collective-permute-start.4
  101.3 1.5 collective-permute-start.3
  102.8 2.5 %collective-permute-start.2 = (bf16[64,192]{1,0:T(8,128)(2,1)S(1)}, bf16[64,192]{1,0:T(8,128)(2,1)S(1)}, u32[]{:S(2)}, u32[]{:S(2)}) collective-permute-start(bf16[64,192]{1,0:T(8,128)(2,1)S(1)} %copy-done.13), channel_id=1, source_target_pairs={{0,1},{1,2},{2,3},{3,0},{4,5},{5,6},{6,7},{7,4},{8,9},{9,10},{10,1... | collective-permute-start | bytes 73736 | tf_op jit(solution)/shard_map/ppermute | solution.py:347
  105.3 0.0 collective-permute-done.4
  105.3 1.4 collective-permute-done.3
  106.7 0.2 collective-permute-done.2
  106.9 0.1 add_divide_fusion.own_ref
  107.0 0.0 copy-start.7
  107.0 0.1 collective-permute-start.5
  107.1 1.2 collective-permute-done.5.other_ref
  108.4 9.0 %all-to-all-done.1.weights_ref = bf16[32,64,128]{2,1,0:T(8,128)(2,1)S(1)} async-done(((bf16[32,64,128]{2,1,0:T(8,128)(2,1)}), bf16[32,64,128]{2,1,0:T(8,128)(2,1)S(1)}, u32[]{:S(2)}, u32[]{:S(2)}) %all-to-all-start.1) | async-done | bytes 524320 | tf_op jit(solution)/shard_map/all_to_all | solution.py:37
  117.3 0.8 copy-done.2
  118.1 3.0 %spread.1 = bf16[32,160,128]{2,1,0:T(8,128)(2,1)} custom-call(f32[64,192]{1,0:T(8,128)} %copy-done.7, f32[64,192]{1,0:T(8,128)} %copy-done.9, bf16[1024,128]{1,0:T(8,128)(2,1)} %make_mixing.1.mix_ref, bf16[32,64,128]{2,1,0:T(8,128)(2,1)} %copy-done.2), custom_call_target="tpu_custom_call" | custom-call | tf_op jit(solution)/shard_map/spread/pallas_call | solution.py:268
  121.2 40.7 %all_to_all.15.rows_ref = bf16[32,160,128]{2,1,0:T(8,128)(2,1)S(1)} all-to-all(bf16[32,160,128]{2,1,0:T(8,128)(2,1)} %spread.1), channel_id=1, replica_groups={{0,8,16,24,32,40,48,56,64,72,80,88,96,104,112,120,128,136,144,152,160,1..., dimensions={0} | all-to-all | bytes 2621440 | tf_op jit(solution)/shard_map/all_to_all | solution.py:37
  161.9 0.1 collective-permute-start.7
  162.0 0.9 reshape_reshape.3.index_ref
  162.9 1.2 copy.57
  164.1 2.7 %reshape.76 = bf16[32,64,3,64]{1,0,3,2:T(8,128)(2,1)S(1)} reshape(bf16[2048,192]{0,1:T(8,128)(2,1)} %copy.57) | data formatting | bytes 1572864 | tf_op jit(solution)/shard_map/reshape | solution.py:345
  166.8 2.2 %copy.58 = bf16[32,3,64,64]{3,2,0,1:T(8,128)(2,1)} copy(bf16[32,3,64,64]{2,0,3,1:T(8,128)(2,1)S(1)} %bitcast.65) | data formatting | bytes 1572864 | tf_op jit(solution)/shard_map/transpose | solution.py:345
  169.0 3.2 %reshape.77 = bf16[32,3,4096]{2,0,1:T(8,128)(2,1)} reshape(bf16[32,3,64,64]{3,2,0,1:T(8,128)(2,1)} %copy.58) | data formatting | bytes 1572864 | tf_op jit(solution)/shard_map/reshape | solution.py:345
  172.2 6.7 %scatter_rows.1 = f32[192,2048]{1,0:T(8,128)} custom-call(s32[1,2048]{1,0:T(1,128)} %reshape_reshape.3.index_ref, bf16[32,160,128]{2,1,0:T(8,128)(2,1)} %copy-done), custom_call_target="tpu_custom_call" | custom-call | tf_op jit(solution)/shard_map/scatter_rows/pallas_call | solution.py:298
  178.9 0.0 collective-permute-done.7
  178.9 1.1 broadcast_select_fusion.1
  179.9 0.1 convert_bitcast_fusion
  180.1 0.2 slice_bitcast_fusion.1
  180.2 0.9 copy.73
  181.1 0.9 copy.72
  181.9 0.9 copy.71
  (34 shorter events, 0.1 us)
Async XLA Ops:
  0.6 19.7 %copy-start.12 = (s32[32,2]{0,1:T(2,128)S(1)}, s32[32,2]{0,1:T(2,128)}, u32[]{:S(2)}) copy-start(s32[32,2]{0,1:T(2,128)} %param.17) | copy-start | bytes 772
  0.6 19.9 %copy-start.11 = (s32[32,2,32]{2,1,0:T(2,128)S(1)}, s32[32,2,32]{2,1,0:T(2,128)}, u32[]{:S(2)}) copy-start(s32[32,2,32]{2,1,0:T(2,128)} %param.16) | copy-start | bytes 24580
  1.5 19.2 %copy-start.5 = (bf16[192,768]{1,0:T(8,128)(2,1)S(1)}, bf16[192,768]{1,0:T(8,128)(2,1)}, u32[]{:S(2)}) copy-start(bf16[192,768]{1,0:T(8,128)(2,1)} %wv_ref.1) | copy-start | bytes 884740
  2.3 18.8 %copy-start.4 = (bf16[192,768]{1,0:T(8,128)(2,1)S(1)}, bf16[192,768]{1,0:T(8,128)(2,1)}, u32[]{:S(2)}) copy-start(bf16[192,768]{1,0:T(8,128)(2,1)} %wk_ref.1) | copy-start | bytes 884740
  9.0 34.7 %all-to-all-start = ((bf16[32,96,128]{2,1,0:T(8,128)(2,1)}), bf16[32,96,128]{2,1,0:T(8,128)(2,1)S(1)}, u32[]{:S(2)}, u32[]{:S(2)}) async-start(bf16[32,96,128]{2,1,0:T(8,128)(2,1)} %gather_rows.1), calls=%async_computation | async-start | bytes 1572864 | tf_op jit(solution)/shard_map/all_to_all | solution.py:37
  20.6 1.8 %collective-permute-start = (s32[64,32]{0,1:T(8,128)S(1)}, s32[64,32]{0,1:T(8,128)S(1)}, u32[]{:S(2)}, u32[]{:S(2)}) collective-permute-start(s32[64,32]{0,1:T(8,128)S(1)} %fusion.2), channel_id=1, source_target_pairs={{0,4},{4,0},{8,12},{12,8},{16,20},{20,16},{24,28},{28,24},{32,36},... | collective-permute-start | bytes 24584 | tf_op jit(solution)/shard_map/ppermute | solution.py:33
  43.7 0.9 copy-start.1
  46.8 7.1 %collective-permute-start.1 = (f32[64,192]{1,0:T(8,128)}, f32[64,192]{1,0:T(8,128)S(1)}, u32[]{:S(2)}, u32[]{:S(2)}) collective-permute-start(f32[64,192]{1,0:T(8,128)} %get-tuple-element.14), channel_id=1, source_target_pairs={{0,4},{4,0},{8,12},{12,8},{16,20},{20,16},{24,28},{28,24},{32,36},... | collective-permute-start | bytes 147464 | tf_op jit(solution)/shard_map/ppermute | solution.py:33
  51.4 2.6 %copy-start.10 = (f32[64,192]{1,0:T(8,128)S(1)}, f32[64,192]{1,0:T(8,128)}, u32[]{:S(2)}) copy-start(f32[64,192]{1,0:T(8,128)} %get-tuple-element.13) | copy-start | bytes 147460
  90.7 3.9 %copy-start.3 = (f32[2,3,576,128]{3,2,1,0:T(8,128)S(1)}, f32[2,3,576,128]{3,2,1,0:T(8,128)}, u32[]{:S(2)}) copy-start(f32[2,3,576,128]{3,2,1,0:T(8,128)} %get-tuple-element.20) | copy-start | bytes 5308420
  92.1 8.4 %copy-start.15 = (bf16[64,192]{1,0:T(8,128)(2,1)S(1)}, bf16[64,192]{1,0:T(8,128)(2,1)}, u32[]{:S(2)}) copy-start(bf16[64,192]{1,0:T(8,128)(2,1)} %get-tuple-element.19) | copy-start | bytes 73732
  92.1 9.2 %copy-start.14 = (bf16[64,192]{1,0:T(8,128)(2,1)S(1)}, bf16[64,192]{1,0:T(8,128)(2,1)}, u32[]{:S(2)}) copy-start(bf16[64,192]{1,0:T(8,128)(2,1)} %get-tuple-element.18) | copy-start | bytes 73732
  92.1 10.7 %copy-start.13 = (bf16[64,192]{1,0:T(8,128)(2,1)S(1)}, bf16[64,192]{1,0:T(8,128)(2,1)}, u32[]{:S(2)}) copy-start(bf16[64,192]{1,0:T(8,128)(2,1)} %get-tuple-element.17) | copy-start | bytes 73732
  92.1 14.8 %copy-start.8 = (f32[64,192]{1,0:T(8,128)S(1)}, f32[64,192]{1,0:T(8,128)}, u32[]{:S(2)}) copy-start(f32[64,192]{1,0:T(8,128)} %get-tuple-element.16) | copy-start | bytes 147460
  92.1 2.5 %collective-permute-start.6 = (f32[3,576,128]{2,1,0:T(8,128)S(1)}, f32[3,576,128]{2,1,0:T(8,128)S(1)}, u32[]{:S(2)}, u32[]{:S(2)}) collective-permute-start(f32[3,576,128]{2,1,0:T(8,128)S(1)} %slice_bitcast_fusion), channel_id=1, source_target_pairs={{0,4},{4,0},{8,12},{12,8},{16,20},{20,16},{24,28},{28,24},{32,36},... | collective-permute-start | bytes 2654216 | tf_op jit(solution)/shard_map/ppermute | solution.py:33
  95.6 21.8 %all-to-all-start.1 = ((bf16[32,64,128]{2,1,0:T(8,128)(2,1)}), bf16[32,64,128]{2,1,0:T(8,128)(2,1)S(1)}, u32[]{:S(2)}, u32[]{:S(2)}) async-start(bf16[32,64,128]{2,1,0:T(8,128)(2,1)} %bitcast.17), calls=%async_computation.1 | async-start | bytes 1048576 | tf_op jit(solution)/shard_map/all_to_all | solution.py:37
  100.5 4.8 %collective-permute-start.4 = (bf16[64,192]{1,0:T(8,128)(2,1)S(1)}, bf16[64,192]{1,0:T(8,128)(2,1)S(1)}, u32[]{:S(2)}, u32[]{:S(2)}) collective-permute-start(bf16[64,192]{1,0:T(8,128)(2,1)S(1)} %copy-done.15), channel_id=1, source_target_pairs={{0,3},{1,0},{2,1},{3,2},{4,7},{5,4},{6,5},{7,6},{8,11},{9,8},{10,9... | collective-permute-start | bytes 73736 | tf_op jit(solution)/shard_map/ppermute | solution.py:347
  101.3 5.4 %collective-permute-start.3 = (bf16[64,192]{1,0:T(8,128)(2,1)S(1)}, bf16[64,192]{1,0:T(8,128)(2,1)S(1)}, u32[]{:S(2)}, u32[]{:S(2)}) collective-permute-start(bf16[64,192]{1,0:T(8,128)(2,1)S(1)} %copy-done.14), channel_id=1, source_target_pairs={{0,2},{1,3},{2,0},{3,1},{4,6},{5,7},{6,4},{7,5},{8,10},{9,11},{10,... | collective-permute-start | bytes 73736 | tf_op jit(solution)/shard_map/ppermute | solution.py:347
  102.8 4.2 %collective-permute-start.2 = (bf16[64,192]{1,0:T(8,128)(2,1)S(1)}, bf16[64,192]{1,0:T(8,128)(2,1)S(1)}, u32[]{:S(2)}, u32[]{:S(2)}) collective-permute-start(bf16[64,192]{1,0:T(8,128)(2,1)S(1)} %copy-done.13), channel_id=1, source_target_pairs={{0,1},{1,2},{2,3},{3,0},{4,5},{5,6},{6,7},{7,4},{8,9},{9,10},{10,1... | collective-permute-start | bytes 73736 | tf_op jit(solution)/shard_map/ppermute | solution.py:347
  107.0 10.3 %copy-start.7 = (f32[64,192]{1,0:T(8,128)}, f32[64,192]{1,0:T(8,128)S(1)}, u32[]{:S(2)}) copy-start(f32[64,192]{1,0:T(8,128)S(1)} %add_divide_fusion.own_ref) | copy-start | bytes 147460
  107.0 1.3 collective-permute-start.5
  108.4 9.0 %copy-start.9 = (f32[64,192]{1,0:T(8,128)}, f32[64,192]{1,0:T(8,128)S(1)}, u32[]{:S(2)}) copy-start(f32[64,192]{1,0:T(8,128)S(1)} %collective-permute-done.5.other_ref) | copy-start | bytes 147460
  117.3 0.8 copy-start.2
  121.2 41.7 %copy-start.6 = (bf16[2048,192]{1,0:T(8,128)(2,1)S(1)}, bf16[2048,192]{1,0:T(8,128)(2,1)}, u32[]{:S(2)}) copy-start(bf16[2048,192]{1,0:T(8,128)(2,1)} %get-tuple-element.15) | copy-start | bytes 2359300
  161.9 5.0 %copy-start = (bf16[32,160,128]{2,1,0:T(8,128)(2,1)}, bf16[32,160,128]{2,1,0:T(8,128)(2,1)S(1)}, u32[]{:S(2)}) copy-start(bf16[32,160,128]{2,1,0:T(8,128)(2,1)S(1)} %all_to_all.15.rows_ref) | copy-start | bytes 3932164
  161.9 17.0 %collective-permute-start.7 = (bf16[1728,128]{1,0:T(8,128)(2,1)S(1)}, bf16[1728,128]{1,0:T(8,128)(2,1)}, u32[]{:S(2)}, u32[]{:S(2)}) collective-permute-start(bf16[1728,128]{1,0:T(8,128)(2,1)S(1)} %bitcast.67), channel_id=1, source_target_pairs={{0,4},{4,0},{8,12},{12,8},{16,20},{20,16},{24,28},{28,24},{32,36},... | collective-permute-start | bytes 1327112 | tf_op jit(solution)/shard_map/ppermute | solution.py:33

commit v2 on v1

--- a/solution.py
+++ b/solution.py
@@ -4,6 +4,7 @@
 from jax.experimental import pallas as pl
 from jax.experimental.pallas import tpu as pltpu
 from jax.sharding import PartitionSpec as P
+
 
 HD = 64
 BF = jnp.bfloat16
@@ -31,6 +32,14 @@
 
 def core_swap(x):
     return lax.ppermute(x, "nodes", CORE_SWAP)
+
+
+def along(x, dx, dz):
+    pairs = []
+    for dev in range(2 * CHIPS):
+        at_x, at_z, core = dev // 16, dev // 2 % 8, dev % 2
+        pairs.append((dev, ((at_x + dx) % 4 * 8 + (at_z + dz) % 8) * 2 + core))
+    return lax.ppermute(x, "nodes", pairs)
 
 
 def chip_exchange(x):
@@ -87,7 +96,8 @@
     )(keys)
 
 
-def virtual_kernel(rows_ref, mix_ref, own_ref, other_ref):
+def virtual_kernel(rows_ref, mix_ref, *refs):
+    own_ref, other_ref = refs[-2:]
     mix = mix_ref[...]
     first = tn(mix, rows_ref[:, 0:32, :].reshape(1024, 128))
     second = tn(mix, rows_ref[:, 32:64, :].reshape(1024, 128))
@@ -98,14 +108,42 @@
     other_ref[:, 128:192] = both[64:128, 64:128]
 
 
-def mix_rows(rows, mix):
+def mix_rows(rows, mix, *after):
     part = jax.ShapeDtypeStruct((64, 192), F32)
-    return pl.pallas_call(virtual_kernel, out_shape=(part, part), name="mix_rows")(rows, mix)
+    whole = pl.BlockSpec(memory_space=pltpu.VMEM)
+    return pl.pallas_call(
+        virtual_kernel,
+        out_shape=(part, part),
+        in_specs=[whole, whole] + [pl.BlockSpec(memory_space=pl.ANY)] * len(after),
+        name="mix_rows",
+    )(rows, mix, *after)
+
+
+def project_kernel(tok_ref, wq_ref, wk_ref, wv_ref, q_ref, k_ref, v_ref):
+    tok = tok_ref[...]
+    q_ref[...] = nt(tok, wq_ref[...]).astype(BF)
+    k_ref[...] = nt(tok, wk_ref[...]).astype(BF)
+    v_ref[...] = nt(tok, wv_ref[...]).astype(BF)
+
+
+def project(tokens, wq, wk, wv):
+    out = jax.ShapeDtypeStruct((2048, 192), BF)
+    weight = pl.BlockSpec((192, 768), lambda i: (0, 0))
+    block = pl.BlockSpec((512, 192), lambda i: (i, 0))
+    return pl.pallas_call(
+        project_kernel,
+        out_shape=(out, out, out),
+        grid=(4,),
+        in_specs=[pl.BlockSpec((512, 768), lambda i: (i, 0)), weight, weight, weight],
+        out_specs=(block, block, block),
+        compiler_params=pltpu.CompilerParams(vmem_limit_bytes=VMEM_LIMIT),
+        name="project",
+    )(tokens, wq, wk, wv)
 
 
 def attend_kernel(
-    place_ref, tok_ref, grad_ref, virt_ref, wq_ref, wk_ref, wv_ref, wk4_ref, wv4_ref,
-    ctx_ref, dw_ref, vg0_ref, vg1_ref, vg2_ref, vg3_ref,
+    place_ref, tok_ref, q_ref, k_ref, v_ref, grad_ref, virt_ref, wk_ref, wv_ref, wk4_ref, wv4_ref,
+    ctx_ref, keep_ref, give_ref, vg0_ref, vg1_ref, vg2_ref, vg3_ref,
     acc_ref, kvirt_ref, vvirt_ref, dkvirt_ref, dvvirt_ref,
 ):
     step = pl.program_id(0)
@@ -122,9 +160,6 @@
         vvirt_ref[...] = nn(spread, nt(virt, wv_ref[...]).astype(BF)).astype(BF)
 
     tok = tok_ref[...]
-    queries = nt(tok, wq_ref[...]).astype(BF)
-    keys = nt(tok, wk_ref[...]).astype(BF)
-    values = nt(tok, wv_ref[...]).astype(BF)
     head_row = lax.broadcasted_iota(jnp.int32, (width, width), 0) // HD
     head_col = lax.broadcasted_iota(jnp.int32, (width, width), 1) // HD
     blocks = jnp.where(head_row == head_col, 1.0, 0.0).astype(BF)
@@ -140,9 +175,9 @@
     for i in range(GROUP):
         at = pl.multiple_of((step * GROUP + i) * 16, 16)
         span = slice(64 * i, 64 * i + 64)
-        key = jnp.concatenate([keys[span], kvirt_ref[pl.ds(at, 16), :]], axis=0)
-        value = jnp.concatenate([values[span], vvirt_ref[pl.ds(at, 16), :]], axis=0)
-        query = queries[span]
+        key = jnp.concatenate([k_ref[span, :], kvirt_ref[pl.ds(at, 16), :]], axis=0)
+        value = jnp.concatenate([v_ref[span, :], vvirt_ref[pl.ds(at, 16), :]], axis=0)
+        query = q_ref[span, :]
         grad = grad_ref[span, :]
         query_blocks = jnp.concatenate([query, query, query], axis=0) * blocks
         grad_blocks = jnp.concatenate([grad, grad, grad], axis=0) * blocks
@@ -188,18 +223,19 @@
                 for t in range(3):
                     keep = 3 * core + t
                     give = 3 * (1 - core) + t
-                    dw_ref[0, t] = acc_ref[:, 128 * keep : 128 * keep + 128]
-                    dw_ref[1, t] = acc_ref[:, 128 * give : 128 * give + 128]
-
-
-def attend(place, tokens, grads, virtual, wq, wk, wv, wk4, wv4):
+                    keep_ref[t] = acc_ref[:, 128 * keep : 128 * keep + 128]
+                    give_ref[t] = acc_ref[:, 128 * give : 128 * give + 128]
+
+
+def attend(place, tokens, q, k, v, grads, virtual, wk, wv, wk4, wv4):
     rows = 64 * GROUP
     steps = CENTRES // GROUP
     fixed2 = lambda i: (0, 0)
     fixed3 = lambda i: (0, 0, 0)
     out_shape = (
         jax.ShapeDtypeStruct((2048, 192), BF),
-        jax.ShapeDtypeStruct((2, 3, 576, 128), F32),
+        jax.ShapeDtypeStruct((3, 576, 128), F32),
+        jax.ShapeDtypeStruct((3, 576, 128), F32),
         jax.ShapeDtypeStruct((64, 192), F32),
         jax.ShapeDtypeStruct((64, 192), BF),
         jax.ShapeDtypeStruct((64, 192), BF),
@@ -207,6 +243,8 @@
     )
     small = pl.BlockSpec((64, 192), fixed2)
     weight = pl.BlockSpec((192, 768), fixed2)
+    head = pl.BlockSpec((rows, 192), lambda i: (i, 0))
+    half = pl.BlockSpec((3, 576, 128), fixed3)
     return pl.pallas_call(
         attend_kernel,
         out_shape=out_shape,
@@ -214,15 +252,14 @@
         in_specs=[
             pl.BlockSpec(memory_space=pltpu.SMEM),
             pl.BlockSpec((rows, 768), lambda i: (i, 0)),
-            pl.BlockSpec((rows, 192), lambda i: (i, 0)),
+            head, head, head, head,
             pl.BlockSpec((64, 768), fixed2),
-            weight, weight, weight,
+            weight, weight,
             pl.BlockSpec((4, 192, 192), fixed3),
             pl.BlockSpec((4, 192, 192), fixed3),
         ],
         out_specs=(
-            pl.BlockSpec((rows, 192), lambda i: (i, 0)),
-            pl.BlockSpec((2, 3, 576, 128), lambda i: (0, 0, 0, 0)),
+            head, half, half,
             small, small, small, small,
         ),
         scratch_shapes=[
@@ -234,10 +271,11 @@
         ],
         compiler_params=pltpu.CompilerParams(vmem_limit_bytes=VMEM_LIMIT),
         name="attend",
-    )(place, tokens, grads, virtual, wq, wk, wv, wk4, wv4)
-
-
-def spread_kernel(own_ref, other_ref, mix_ref, weights_ref, out_ref):
+    )(place, tokens, q, k, v, grads, virtual, wk, wv, wk4, wv4)
+
+
+def spread_kernel(own_ref, other_ref, mix_ref, pieces_ref, *refs):
+    out_ref, total_ref = refs[-2:]
     mix = mix_ref[...]
     zeros = jnp.zeros((64, 192), BF)
 
@@ -256,23 +294,53 @@
     out_ref[:, 32:64, :] = other[:, 0:128].reshape(CHIPS, 32, 128)
     out_ref[:, 64:96, 0:64] = own[:, 128:192].reshape(CHIPS, 32, 64)
     out_ref[:, 64:96, 64:128] = other[:, 128:192].reshape(CHIPS, 32, 64)
-    total = weights_ref[0].astype(F32)
+    total = pieces_ref[0].astype(F32)
     for chip in range(1, CHIPS):
-        total = total + weights_ref[chip].astype(F32)
-    total = total.astype(BF)
-    for chip in range(CHIPS):
-        out_ref[chip, 96:160, :] = total
-
-
-def spread(own, other, mix, weights):
+        total = total + pieces_ref[chip].astype(F32)
+    total_ref[...] = total.astype(BF)
+
+
+def spread(own, other, mix, pieces, *after):
+    whole = pl.BlockSpec(memory_space=pltpu.VMEM)
     return pl.pallas_call(
         spread_kernel,
-        out_shape=jax.ShapeDtypeStruct((CHIPS, 160, 128), BF),
+        out_shape=(
+            jax.ShapeDtypeStruct((CHIPS, 96, 128), BF),
+            jax.ShapeDtypeStruct((64, 128), BF),
+        ),
+        in_specs=[whole] * 4 + [pl.BlockSpec(memory_space=pl.ANY)] * len(after),
         name="spread",
-    )(own, other, mix, weights)
-
-
-def scatter_kernel(index_ref, rows_ref, out_ref, turned_ref):
+    )(own, other, mix, pieces, *after)
+
+
+def assemble_kernel(place_ref, mine_ref, theirs_ref, after_ref, *out_refs):
+    for piece in range(27):
+        dx = (place_ref[2] - piece // 8 + 4) % 4
+        dz = (place_ref[3] - piece % 8 + 8) % 8
+        out_ref = out_refs[(piece % 9) // 3]
+        rows = slice(64 * (piece % 3), 64 * (piece % 3) + 64)
+        mine = mine_ref[dx, dz].astype(F32)
+        theirs = theirs_ref[dx, dz].astype(F32)
+        low = place_ref[1] == 0
+        tile = 128 * (piece // 9)
+        out_ref[rows, tile : tile + 128] = jnp.where(low, mine, theirs)
+        out_ref[rows, 384 + tile : 512 + tile] = jnp.where(low, theirs, mine)
+
+
+def assemble(place, mine, theirs, after):
+    out = jax.ShapeDtypeStruct((192, 768), F32)
+    whole = pl.BlockSpec(memory_space=pltpu.VMEM)
+    return pl.pallas_call(
+        assemble_kernel,
+        out_shape=(out, out, out),
+        in_specs=[
+            pl.BlockSpec(memory_space=pltpu.SMEM), whole, whole, pl.BlockSpec(memory_space=pl.ANY)
+        ],
+        name="assemble",
+    )(place, mine, theirs, after)
+
+
+def scatter_kernel(index_ref, rows_ref, after_ref, out_ref, turned_ref):
     step = pl.program_id(0)
 
     @pl.when(step == 0)
@@ -294,7 +362,7 @@
     out_ref[...] = nt(turned_ref[...], select)
 
 
-def scatter_rows(index, rows):
+def scatter_rows(index, rows, after):
     return pl.pallas_call(
         scatter_kernel,
         out_shape=jax.ShapeDtypeStruct((192, 2048), F32),
@@ -302,18 +370,19 @@
         in_specs=[
             pl.BlockSpec((1, 2048), lambda i: (0, 0)),
             pl.BlockSpec((CHIPS, 96, 128), lambda i: (0, 0, 0)),
+            pl.BlockSpec(memory_space=pl.ANY),
         ],
         out_specs=pl.BlockSpec((192, 256), lambda i: (0, i)),
         scratch_shapes=[pltpu.VMEM((192, 2048), BF)],
         compiler_params=pltpu.CompilerParams(vmem_limit_bytes=VMEM_LIMIT),
         name="scatter_rows",
-    )(index, rows)
-
-
-def body(tokens, w_query, w_key, w_value, grad_out, owned_cls, send_rows, neigh_slot, neigh_count):
-    core = lax.axis_index("nodes") % 2
-    own_mp = lax.axis_index("mp")
-    place = jnp.stack([own_mp, core]).astype(jnp.int32)
+    )(index, rows, after)
+
+
+def layer(tokens, w_query, w_key, w_value, grad_out, owned_cls, send_rows, neigh_slot, neigh_count):
+    node = lax.axis_index("nodes")
+    core = node % 2
+    place = jnp.stack([lax.axis_index("mp"), core, node // 16, node // 2 % 8]).astype(jnp.int32)
 
     asked = send_rows.reshape(8, 4, 2, 32)
     asked = jnp.where(core == 0, asked, asked[:, :, ::-1])
@@ -333,36 +402,36 @@
     wk4 = w_key.reshape(192, 4, 192).transpose(1, 0, 2)
     wv4 = w_value.reshape(192, 4, 192).transpose(1, 0, 2)
 
+    flat = tokens.reshape(2048, 768)
+    q, k, v = project(flat, w_query, w_key, w_value)
+
     fetched = chip_exchange(sent)
-    own_part, other_part = mix_rows(fetched, mix)
+    own_part, other_part = mix_rows(fetched, mix, q, k, v, heads, wk4, wv4)
     divisor = counts.astype(F32)
     local = ((own_part + core_swap(other_part)) / divisor).astype(BF)
     virtual = lax.all_gather(local, "mp", axis=1, tiled=True)
 
-    ctx, dw, vg0, vg1, vg2, vg3 = attend(
-        place, tokens.reshape(2048, 768), heads, virtual, w_query, w_key, w_value, wk4, wv4
+    ctx, keep, give, vg0, vg1, vg2, vg3 = attend(
+        place, flat, q, k, v, heads, virtual, w_key, w_value, wk4, wv4
     )
     context = ctx.reshape(32, 64, 3, 64).transpose(0, 2, 1, 3).reshape(32, 3, 4096)
 
     around = lambda x, d: lax.ppermute(x, "mp", [(i, (i + d) % 4) for i in range(4)])
     moved = [around(vg, d + 1) for d, vg in enumerate((vg1, vg2, vg3))]
-    half = dw[0] + core_swap(dw[1])
-    half = half.astype(BF).reshape(1728, 128)
-    padded = jnp.pad(half, ((0, 2048 - 1728), (0, 0))).reshape(CHIPS, 64, 128)
-    pieces = chip_exchange(padded)
+    half = (keep + core_swap(give)).astype(BF).reshape(27, 64, 128)
+    pieces = chip_exchange(jnp.pad(half, ((0, CHIPS - 27), (0, 0), (0, 0))))
 
     shared = (vg0 + moved[0].astype(F32) + moved[1].astype(F32) + moved[2].astype(F32)) / divisor
-    other_shared = core_swap(shared)
-    outgoing = spread(shared, other_shared, mix, pieces)
+    outgoing, total = spread(
+        shared, core_swap(shared), mix, pieces, context.transpose(1, 0, 2)
+    )
     arrived = chip_exchange(outgoing)
-
-    mine = arrived[:, 96:160].reshape(2048, 128)[:1728]
+    row = jnp.stack([total] + [along(total, 0, d) for d in range(1, 8)])
+    mine = jnp.stack([row] + [along(row, d, 0) for d in range(1, 4)])
     theirs = core_swap(mine)
-    grad_cls = scatter_rows(index.reshape(1, 2048), arrived)
-    first = jnp.where(core == 0, mine, theirs).reshape(3, 576, 128)
-    second = jnp.where(core == 0, theirs, mine).reshape(3, 576, 128)
-    grads = jnp.concatenate([first, second], axis=0).transpose(1, 0, 2).reshape(576, 768).astype(F32)
-    return (context, grads[0:192], grads[192:384], grads[384:576], grad_cls)
+    grad_cls = scatter_rows(index.reshape(1, 2048), arrived, mine)
+    grad_query, grad_key, grad_value = assemble(place, mine, theirs, grad_cls)
+    return (context, grad_query, grad_key, grad_value, grad_cls)
 
 
 def solution(mesh):
@@ -384,4 +453,4 @@
         P("mp", None),
         P("mp", "nodes"),
     )
-    return jax.shard_map(body, mesh=mesh, in_specs=in_specs, out_specs=out_specs, check_vma=False)
+    return jax.shard_map(layer, mesh=mesh, in_specs=in_specs, out_specs=out_specs, check_vma=False)

time: 185 us -> 182 us (0.984)
  blocking collectives: 53 us -> 12.2 us
  starting transfers between devices: 21.4 us -> 45.9 us
  waiting for transfers between devices: 31.7 us -> 44.2 us
  local copies, waits for them, and re-layouts: 27.7 us -> 20.7 us
  Pallas kernels: 45.3 us -> 51 us
    all_to_all x1 -> x0, blocking collectives: 40.7 us -> none  [chip_exchange(): lax.all_to_all(x, 'nodes', split_axis=0, concat_axis=0, tiled=True, axis_...]
    ppermute x3 -> x13, waiting for transfers between devices: 1.63 us -> 31.3 us  [the longest x10 29.4 us: along(): return lax.ppermute(x, 'nodes', pairs)]
    all_to_all x2 -> x3, waiting for transfers between devices: 26.4 us -> 9.39 us  [chip_exchange(): lax.all_to_all(x, 'nodes', split_axis=0, concat_axis=0, tiled=True, axis_...]
    ppermute x3 -> x13, starting transfers between devices: 4.78 us -> 21.6 us  [the longest x10 16.8 us: along(): return lax.ppermute(x, 'nodes', pairs)]
    pallas_call x2 -> x4, Pallas kernels: 5.32 us -> 13.7 us  [the longest x1 5.98 us: project(): pl.pallas_call(project_kernel, out_shape=(out, out, out), grid=(4,), in_s...]
    all_to_all x2 -> x3, starting transfers between devices: 16.2 us -> 24 us  [chip_exchange(): lax.all_to_all(x, 'nodes', split_axis=0, concat_axis=0, tiled=True, axis_...]
    pallas_call x1, Pallas kernels: 23.5 us -> 20.8 us  [attend(): pl.pallas_call(attend_kernel, out_shape=out_shape, grid=(steps,), in_spec...]
    slice x4 -> x0, local copies, waits for them, and re-layouts: 2.6 us -> none  [the longest x3 2.56 us: body(): return (context, grads[0:192], grads[192:384], grads[384:576], grad_cls)]
  transfers between devices with their start and end apart: 10 -> 21, of which waited for: 6 -> 11; matrix products, arithmetic and copies ran while one was open for 11% -> 10% of each run, Pallas kernels for 5% -> 9%
where the time goes in v2:
time: 182 us; the launch traced here: 179 us
  Pallas kernels  51 us (28%)
  starting transfers between devices  45.9 us (25%)
  waiting for transfers between devices  44.2 us (24%)
  local copies, waits for them, and re-layouts  20.7 us (11%)
  blocking collectives  12.2 us (7%)
  other arithmetic  3.68 us (2%)
    ppermute x10, waiting for transfers between devices, along(): return lax.ppermute(x, 'nodes', pairs)  29.4 us
    all_to_all x3, starting transfers between devices, chip_exchange(): lax.all_to_all(x, 'nodes', split_axis=0, concat_axis=0, tiled=True, axis_...  24 us
    pallas_call x1, Pallas kernels, attend(): pl.pallas_call(attend_kernel, out_shape=out_shape, grid=(steps,), in_spec...  20.8 us
    ppermute x10, starting transfers between devices, along(): return lax.ppermute(x, 'nodes', pairs)  16.8 us
    all_gather x1, blocking collectives, layer(): virtual = lax.all_gather(local, 'mp', axis=1, tiled=True)  12.2 us
    all_to_all x3, waiting for transfers between devices, chip_exchange(): lax.all_to_all(x, 'nodes', split_axis=0, concat_axis=0, tiled=True, axis_...  9.39 us
    pallas_call x1, Pallas kernels, gather_rows(): pl.pallas_call(gather_kernel, out_shape=jax.ShapeDtypeStruct((CHIPS, 96,...  6.7 us
    pallas_call x1, Pallas kernels, scatter_rows(): pl.pallas_call(scatter_kernel, out_shape=jax.ShapeDtypeStruct((192, 2048)...  6.67 us
  transfers between devices with their start and end apart: 21, of which 11 were waited for; matrix products, arithmetic and copies ran while one was open for 10% of the time, Pallas kernels for 9%

profile of v2, /device:TPU:8, one launch (start us, length us, event | category | flops | bytes accessed | tf_op | source)
XLA Modules:
  0.0 178.7 jit_solution(17057396188966104054)
XLA Ops:
  0.6 0.8 copy.34
  1.6 0.7 reshape.56.index_ref
  2.3 6.7 %gather_rows.1 = bf16[32,96,128]{2,1,0:T(8,128)(2,1)} custom-call(s32[8,1,256]{2,1,0:T(1,128)} %reshape.56.index_ref, bf16[192,2048]{1,0:T(8,128)(2,1)} %table_ref.1), custom_call_target="tpu_custom_call" | custom-call | tf_op jit(solution)/shard_map/gather_rows/pallas_call | solution.py:68
  9.0 11.6 %all-to-all-start = ((bf16[32,96,128]{2,1,0:T(8,128)(2,1)}), bf16[32,96,128]{2,1,0:T(8,128)(2,1)}, u32[]{:S(2)}, u32[]{:S(2)}) async-start(bf16[32,96,128]{2,1,0:T(8,128)(2,1)} %gather_rows.1), calls=%async_computation | async-start | bytes 1572864 | tf_op jit(solution)/shard_map/all_to_all | solution.py:46
  20.6 0.1 copy.36
  20.7 0.1 lt.22
  20.8 0.1 collective-permute-start
  20.9 0.4 reshape.58
  21.3 0.4 reshape.59
  21.7 1.0 copy_bitcast_fusion
  22.7 2.5 %reshape.53 = bf16[32,3,64,64]{3,2,0,1:T(8,128)(2,1)S(1)} reshape(bf16[32,3,4096]{2,0,1:T(8,128)(2,1)} %param.13) | data formatting | bytes 1572864 | tf_op jit(solution)/shard_map/reshape | solution.py:401
  25.2 1.4 copy.33
  26.6 1.3 reshape.54
  27.9 1.3 copy.42.refs_3_.grad_ref
  29.2 6.0 %project.1 = (bf16[2048,192]{1,0:T(8,128)(2,1)}, bf16[2048,192]{1,0:T(8,128)(2,1)}, bf16[2048,192]{1,0:T(8,128)(2,1)}) custom-call(bf16[2048,768]{1,0:T(8,128)(2,1)} %bitcast.58, bf16[192,768]{1,0:T(8,128)(2,1)} %wq_ref.1, bf16[192,768]{1,0:T(8,128)(2,1)} %wk_ref.3, bf16[192,768]{1,0:T(8,128)(2,1)} %wv_ref.3), custom_call_target="tpu_custom_call" | custom-call | tf_op jit(solution)/shard_map/project/pallas_call | solution.py:133
  35.2 0.7 select_bitcast_fusion.1.key_ref
  35.9 3.1 %make_mixing.1.mix_ref = bf16[1024,128]{1,0:T(8,128)(2,1)} custom-call(s32[32,128]{1,0:T(8,128)} %select_bitcast_fusion.1.key_ref), custom_call_target="tpu_custom_call" | custom-call | tf_op jit(solution)/shard_map/make_mixing/pallas_call | solution.py:92
  39.0 4.9 %all-to-all-done.rows_ref = bf16[32,96,128]{2,1,0:T(8,128)(2,1)} async-done(((bf16[32,96,128]{2,1,0:T(8,128)(2,1)}), bf16[32,96,128]{2,1,0:T(8,128)(2,1)}, u32[]{:S(2)}, u32[]{:S(2)}) %all-to-all-start) | async-done | bytes 786464 | tf_op jit(solution)/shard_map/all_to_all | solution.py:46
  43.9 2.3 %mix_rows.1 = (f32[64,192]{1,0:T(8,128)}, f32[64,192]{1,0:T(8,128)}) custom-call(bf16[32,96,128]{2,1,0:T(8,128)(2,1)} %all-to-all-done.rows_ref, bf16[1024,128]{1,0:T(8,128)(2,1)} %make_mixing.1.mix_ref, bf16[2048,192]{1,0:T(8,128)(2,1)} %get-tuple-element.22.refs_0_.q_ref, bf16[2048,192]{1,0:T(8,128)(2,1)} %get-tuple-element.23.refs_1_.k_ref, ...), custom_call_target="tpu_custom_call" | custom-call | tf_op jit(solution)/shard_map/mix_rows/pallas_call | solution.py:114
  46.2 0.6 pad_add_fusion.1.place_ref
  46.8 0.9 collective-permute-done.1
  47.7 0.9 fusion
  48.6 12.2 %all-gather = bf16[4,192,64]{1,2,0:T(8,128)(2,1)S(1)} all-gather(bf16[1,192,64]{1,2,0:T(8,128)(2,1)S(1)} %fusion), channel_id=1, replica_groups=mesh['nodes'=64,'mp'=4] {'mp'}, dimensions={0}, use_global_device_ids=true | all-gather | bytes 122880 | tf_op jit(solution)/shard_map/all_gather | solution.py:412
  60.8 0.1 copy.41
  60.9 0.8 reshape.64
  61.7 20.8 %attend.1 = (bf16[2048,192]{1,0:T(8,128)(2,1)}, f32[3,576,128]{2,1,0:T(8,128)}, f32[3,576,128]{2,1,0:T(8,128)}, f32[64,192]{1,0:T(8,128)}, bf16[64,192]{1,0:T(8,...) custom-call(s32[4]{0:T(128)} %pad_add_fusion.1.place_ref, bf16[2048,768]{1,0:T(8,128)(2,1)} %bitcast.59, ...), custom_call_target="tpu_custom_call" | custom-call | tf_op jit(solution)/shard_map/attend/pallas_call | solution.py:248
  82.5 0.1 collective-permute-start.6
  82.6 2.6 %collective-permute-done.6 = f32[3,576,128]{2,1,0:T(8,128)S(1)} collective-permute-done((f32[3,576,128]{2,1,0:T(8,128)}, f32[3,576,128]{2,1,0:T(8,128)S(1)}, u32[]{:S(2)}, u32[]{:S(2)}) %collective-permute-start.6) | collective-permute-done | bytes 884768 | tf_op jit(solution)/shard_map/ppermute | solution.py:34
  85.3 1.3 add_convert_fusion
  86.6 0.9 pad.4
  87.4 5.4 %all-to-all-start.1 = ((bf16[32,64,128]{2,1,0:T(8,128)(2,1)}), bf16[32,64,128]{2,1,0:T(8,128)(2,1)}, u32[]{:S(2)}, u32[]{:S(2)}) async-start(bf16[32,64,128]{2,1,0:T(8,128)(2,1)} %pad.4), calls=%async_computation.1 | async-start | bytes 1048576 | tf_op jit(solution)/shard_map/all_to_all | solution.py:46
  93.0 2.6 %collective-permute-start.3 = (bf16[64,192]{1,0:T(8,128)(2,1)S(1)}, bf16[64,192]{1,0:T(8,128)(2,1)S(1)}, u32[]{:S(2)}, u32[]{:S(2)}) collective-permute-start(bf16[64,192]{1,0:T(8,128)(2,1)S(1)} %copy-done.13), channel_id=1, source_target_pairs={{0,2},{1,3},{2,0},{3,1},{4,6},{5,7},{6,4},{7,5},{8,10},{9,11},{10,... | collective-permute-start | bytes 73736 | tf_op jit(solution)/shard_map/ppermute | solution.py:419
  95.6 2.0 %collective-permute-start.4 = (bf16[64,192]{1,0:T(8,128)(2,1)S(1)}, bf16[64,192]{1,0:T(8,128)(2,1)S(1)}, u32[]{:S(2)}, u32[]{:S(2)}) collective-permute-start(bf16[64,192]{1,0:T(8,128)(2,1)S(1)} %copy-done.12), channel_id=1, source_target_pairs={{0,3},{1,0},{2,1},{3,2},{4,7},{5,4},{6,5},{7,6},{8,11},{9,8},{10,9... | collective-permute-start | bytes 73736 | tf_op jit(solution)/shard_map/ppermute | solution.py:419
  97.6 0.8 collective-permute-done.3
  98.5 1.1 collective-permute-done.4
  99.6 0.1 collective-permute-start.5
  99.7 0.5 copy.43
  100.2 1.6 reshape.60
  101.9 1.4 copy.44
  103.3 2.0 %reshape.61 = bf16[32,3,4096]{2,0,1:T(8,128)(2,1)} reshape(bf16[32,3,64,64]{3,2,0,1:T(8,128)(2,1)S(1)} %copy.44) | data formatting | bytes 1572864 | tf_op jit(solution)/shard_map/reshape | solution.py:417
  105.4 4.5 %all-to-all-done.1.pieces_ref = bf16[32,64,128]{2,1,0:T(8,128)(2,1)} async-done(((bf16[32,64,128]{2,1,0:T(8,128)(2,1)}), bf16[32,64,128]{2,1,0:T(8,128)(2,1)}, u32[]{:S(2)}, u32[]{:S(2)}) %all-to-all-start.1) | async-done | bytes 524320 | tf_op jit(solution)/shard_map/all_to_all | solution.py:46
  109.9 2.8 %spread.1 = (bf16[32,96,128]{2,1,0:T(8,128)(2,1)}, bf16[64,128]{1,0:T(8,128)(2,1)}) custom-call(f32[64,192]{1,0:T(8,128)} %copy-done.6, f32[64,192]{1,0:T(8,128)} %copy-done.8, bf16[1024,128]{1,0:T(8,128)(2,1)} %make_mixing.1.mix_ref, bf16[32,64,128]{2,1,0:T(8,128)(2,1)} %all-to-all-done.1.pieces_ref, bf16[3,32,4096]{2,1,0:T(8,128)(2,1)} %bitcast.62), custom_call_target="tpu_custom_call" | custom-call | tf_op jit(solution)/shard_map/spread/pallas_call | solution.py:305
  112.7 1.4 collective-permute-start.13
  114.1 1.4 collective-permute-start.12
  115.5 3.7 %collective-permute-start.11 = (bf16[64,128]{1,0:T(8,128)(2,1)}, bf16[64,128]{1,0:T(8,128)(2,1)S(1)}, u32[]{:S(2)}, u32[]{:S(2)}) collective-permute-start(bf16[64,128]{1,0:T(8,128)(2,1)} %get-tuple-element.34), channel_id=1, source_target_pairs={{0,40},{4,44},{8,48},{12,52},{16,56},{20,60},{24,0},{28,4},{32,8},... | collective-permute-start | bytes 49160 | tf_op jit(solution)/shard_map/ppermute | solution.py:42
  119.2 2.6 %collective-permute-start.10 = (bf16[64,128]{1,0:T(8,128)(2,1)}, bf16[64,128]{1,0:T(8,128)(2,1)S(1)}, u32[]{:S(2)}, u32[]{:S(2)}) collective-permute-start(bf16[64,128]{1,0:T(8,128)(2,1)} %get-tuple-element.34), channel_id=1, source_target_pairs={{0,32},{4,36},{8,40},{12,44},{16,48},{20,52},{24,56},{28,60},{32,0... | collective-permute-start | bytes 49160 | tf_op jit(solution)/shard_map/ppermute | solution.py:42
  121.9 0.2 collective-permute-start.7
  122.1 0.8 constant_dynamic-update-slice_fusion.7
  122.8 7.0 %all-to-all-start.2 = ((bf16[32,96,128]{2,1,0:T(8,128)(2,1)}), bf16[32,96,128]{2,1,0:T(8,128)(2,1)S(1)}, u32[]{:S(2)}, u32[]{:S(2)}) async-start(bf16[32,96,128]{2,1,0:T(8,128)(2,1)} %get-tuple-element.35), calls=%async_computation.2 | async-start | bytes 1572864 | tf_op jit(solution)/shard_map/all_to_all | solution.py:46
  129.9 2.8 %collective-permute-start.8 = (bf16[64,128]{1,0:T(8,128)(2,1)S(1)}, bf16[64,128]{1,0:T(8,128)(2,1)S(1)}, u32[]{:S(2)}, u32[]{:S(2)}) collective-permute-start(bf16[64,128]{1,0:T(8,128)(2,1)S(1)} %copy-done.10), channel_id=1, source_target_pairs={{0,16},{4,20},{8,24},{12,28},{16,32},{20,36},{24,40},{28,44},{32,4... | collective-permute-start | bytes 49160 | tf_op jit(solution)/shard_map/ppermute | solution.py:42
  132.6 16.5 %collective-permute-done.8 = bf16[64,128]{1,0:T(8,128)(2,1)S(1)} collective-permute-done((bf16[64,128]{1,0:T(8,128)(2,1)S(1)}, bf16[64,128]{1,0:T(8,128)(2,1)S(1)}, u32[]{:S(2)}, u32[]{:S(2)}) %collective-permute-start.8) | collective-permute-done | bytes 16416 | tf_op jit(solution)/shard_map/ppermute | solution.py:42
  149.1 6.7 %collective-permute-done.9 = bf16[64,128]{1,0:T(8,128)(2,1)S(1)} collective-permute-done((bf16[64,128]{1,0:T(8,128)(2,1)S(1)}, bf16[64,128]{1,0:T(8,128)(2,1)S(1)}, u32[]{:S(2)}, u32[]{:S(2)}) %collective-permute-start.9) | collective-permute-done | bytes 16416 | tf_op jit(solution)/shard_map/ppermute | solution.py:42
  155.9 3.0 %collective-permute-start.16 = (bf16[8,64,128]{2,1,0:T(8,128)(2,1)S(1)}, bf16[8,64,128]{2,1,0:T(8,128)(2,1)S(1)}, u32[]{:S(2)}, u32[]{:S(2)}) collective-permute-start(bf16[8,64,128]{2,1,0:T(8,128)(2,1)S(1)} %constant_dynamic-update-slice_fusion), channel_id=1, source_target_pairs={{0,192},{4,196},{8,200},{12,204},{16,208},{20,212},{24,216},{28,22... | collective-permute-start | bytes 393224 | tf_op jit(solution)/shard_map/ppermute | solution.py:42
  159.0 0.8 collective-permute-start.15
  159.8 0.9 collective-permute-start.14
  160.6 2.3 %collective-permute-done.16 = bf16[8,64,128]{2,1,0:T(8,128)(2,1)S(1)} collective-permute-done((bf16[8,64,128]{2,1,0:T(8,128)(2,1)S(1)}, bf16[8,64,128]{2,1,0:T(8,128)(2,1)S(1)}, u32[]{:S(2)}, u32[]{:S(2)}) %collective-permute-start.16) | collective-permute-done | bytes 131104 | tf_op jit(solution)/shard_map/ppermute | solution.py:42
  162.9 2.6 %collective-permute-done.15 = bf16[8,64,128]{2,1,0:T(8,128)(2,1)S(1)} collective-permute-done((bf16[8,64,128]{2,1,0:T(8,128)(2,1)S(1)}, bf16[8,64,128]{2,1,0:T(8,128)(2,1)S(1)}, u32[]{:S(2)}, u32[]{:S(2)}) %collective-permute-start.15) | collective-permute-done | bytes 131104 | tf_op jit(solution)/shard_map/ppermute | solution.py:42
  165.6 1.3 collective-permute-done.14
  166.9 0.1 collective-permute-start.17
  167.0 0.7 reshape_reshape.3.index_ref
  167.7 0.9 copy-done.1
  168.6 6.7 %scatter_rows.1.after_ref = f32[192,2048]{1,0:T(8,128)} custom-call(s32[1,2048]{1,0:T(1,128)} %reshape_reshape.3.index_ref, bf16[32,96,128]{2,1,0:T(8,128)(2,1)} %copy-done.1, bf16[4,8,64,128]{3,2,1,0:T(8,128)(2,1)} %copy-done), custom_call_target="tpu_custom_call" | custom-call | tf_op jit(solution)/shard_map/scatter_rows/pallas_call | solution.py:366
  175.3 0.8 copy-done.5
  176.1 2.5 %assemble.1 = (f32[192,768]{1,0:T(8,128)}, f32[192,768]{1,0:T(8,128)}, f32[192,768]{1,0:T(8,128)}) custom-call(s32[4]{0:T(128)} %pad_add_fusion.1.place_ref, bf16[4,8,64,128]{3,2,1,0:T(8,128)(2,1)} %copy-done, bf16[4,8,64,128]{3,2,1,0:T(8,128)(2,1)} %copy-done.5, f32[192,2048]{1,0:T(8,128)} %scatter_rows.1.after_ref), custom_call_target="tpu_custom_call" | custom-call | tf_op jit(solution)/shard_map/assemble/pallas_call | solution.py:333
  (56 shorter events, 0.6 us)
Async XLA Ops:
  2.3 18.3 %copy-start.9 = (s32[32,2,32]{2,1,0:T(2,128)S(1)}, s32[32,2,32]{2,1,0:T(2,128)}, u32[]{:S(2)}) copy-start(s32[32,2,32]{2,1,0:T(2,128)} %param.16) | copy-start | bytes 24580
  2.3 18.3 %copy-start.11 = (s32[32,2]{0,1:T(2,128)S(1)}, s32[32,2]{0,1:T(2,128)}, u32[]{:S(2)}) copy-start(s32[32,2]{0,1:T(2,128)} %param.17) | copy-start | bytes 772
  2.3 18.7 %copy-start.2 = (bf16[192,768]{1,0:T(8,128)(2,1)S(1)}, bf16[192,768]{1,0:T(8,128)(2,1)}, u32[]{:S(2)}) copy-start(bf16[192,768]{1,0:T(8,128)(2,1)} %wk_ref.3) | copy-start | bytes 884740
  9.0 12.3 %copy-start.3 = (bf16[192,768]{1,0:T(8,128)(2,1)S(1)}, bf16[192,768]{1,0:T(8,128)(2,1)}, u32[]{:S(2)}) copy-start(bf16[192,768]{1,0:T(8,128)(2,1)} %wv_ref.3) | copy-start | bytes 884740
  9.0 34.9 %all-to-all-start = ((bf16[32,96,128]{2,1,0:T(8,128)(2,1)}), bf16[32,96,128]{2,1,0:T(8,128)(2,1)}, u32[]{:S(2)}, u32[]{:S(2)}) async-start(bf16[32,96,128]{2,1,0:T(8,128)(2,1)} %gather_rows.1), calls=%async_computation | async-start | bytes 1572864 | tf_op jit(solution)/shard_map/all_to_all | solution.py:46
  20.8 14.3 %collective-permute-start = (s32[64,32]{0,1:T(8,128)S(1)}, s32[64,32]{0,1:T(8,128)S(1)}, u32[]{:S(2)}, u32[]{:S(2)}) collective-permute-start(s32[64,32]{0,1:T(8,128)S(1)} %fusion.1), channel_id=1, source_target_pairs={{0,4},{4,0},{8,12},{12,8},{16,20},{20,16},{24,28},{28,24},{32,36},... | collective-permute-start | bytes 24584 | tf_op jit(solution)/shard_map/ppermute | solution.py:34
  46.2 1.5 collective-permute-start.1
  82.5 2.7 %collective-permute-start.6 = (f32[3,576,128]{2,1,0:T(8,128)}, f32[3,576,128]{2,1,0:T(8,128)S(1)}, u32[]{:S(2)}, u32[]{:S(2)}) collective-permute-start(f32[3,576,128]{2,1,0:T(8,128)} %get-tuple-element.33), channel_id=1, source_target_pairs={{0,4},{4,0},{8,12},{12,8},{16,20},{20,16},{24,28},{28,24},{32,36},... | collective-permute-start | bytes 2654216 | tf_op jit(solution)/shard_map/ppermute | solution.py:34
  85.2 7.6 %copy-start.14 = (bf16[64,192]{1,0:T(8,128)(2,1)S(1)}, bf16[64,192]{1,0:T(8,128)(2,1)}, u32[]{:S(2)}) copy-start(bf16[64,192]{1,0:T(8,128)(2,1)} %get-tuple-element.29) | copy-start | bytes 73732
  85.3 7.7 %copy-start.13 = (bf16[64,192]{1,0:T(8,128)(2,1)S(1)}, bf16[64,192]{1,0:T(8,128)(2,1)}, u32[]{:S(2)}) copy-start(bf16[64,192]{1,0:T(8,128)(2,1)} %get-tuple-element.30) | copy-start | bytes 73732
  85.3 10.3 %copy-start.12 = (bf16[64,192]{1,0:T(8,128)(2,1)S(1)}, bf16[64,192]{1,0:T(8,128)(2,1)}, u32[]{:S(2)}) copy-start(bf16[64,192]{1,0:T(8,128)(2,1)} %get-tuple-element.31) | copy-start | bytes 73732
  85.3 14.3 %copy-start.7 = (f32[64,192]{1,0:T(8,128)S(1)}, f32[64,192]{1,0:T(8,128)}, u32[]{:S(2)}) copy-start(f32[64,192]{1,0:T(8,128)} %get-tuple-element.28) | copy-start | bytes 147460
  86.6 13.2 %copy-start.4 = (bf16[2048,192]{1,0:T(8,128)(2,1)S(1)}, bf16[2048,192]{1,0:T(8,128)(2,1)}, u32[]{:S(2)}) copy-start(bf16[2048,192]{1,0:T(8,128)(2,1)} %get-tuple-element.27) | copy-start | bytes 2359300
  87.4 22.4 %all-to-all-start.1 = ((bf16[32,64,128]{2,1,0:T(8,128)(2,1)}), bf16[32,64,128]{2,1,0:T(8,128)(2,1)}, u32[]{:S(2)}, u32[]{:S(2)}) async-start(bf16[32,64,128]{2,1,0:T(8,128)(2,1)} %pad.4), calls=%async_computation.1 | async-start | bytes 1048576 | tf_op jit(solution)/shard_map/all_to_all | solution.py:46
  92.9 4.8 %collective-permute-start.2 = (bf16[64,192]{1,0:T(8,128)(2,1)S(1)}, bf16[64,192]{1,0:T(8,128)(2,1)S(1)}, u32[]{:S(2)}, u32[]{:S(2)}) collective-permute-start(bf16[64,192]{1,0:T(8,128)(2,1)S(1)} %copy-done.14), channel_id=1, source_target_pairs={{0,1},{1,2},{2,3},{3,0},{4,5},{5,6},{6,7},{7,4},{8,9},{9,10},{10,1... | collective-permute-start | bytes 73736 | tf_op jit(solution)/shard_map/ppermute | solution.py:419
  93.0 5.5 %collective-permute-start.3 = (bf16[64,192]{1,0:T(8,128)(2,1)S(1)}, bf16[64,192]{1,0:T(8,128)(2,1)S(1)}, u32[]{:S(2)}, u32[]{:S(2)}) collective-permute-start(bf16[64,192]{1,0:T(8,128)(2,1)S(1)} %copy-done.13), channel_id=1, source_target_pairs={{0,2},{1,3},{2,0},{3,1},{4,6},{5,7},{6,4},{7,5},{8,10},{9,11},{10,... | collective-permute-start | bytes 73736 | tf_op jit(solution)/shard_map/ppermute | solution.py:419
  95.6 3.9 %collective-permute-start.4 = (bf16[64,192]{1,0:T(8,128)(2,1)S(1)}, bf16[64,192]{1,0:T(8,128)(2,1)S(1)}, u32[]{:S(2)}, u32[]{:S(2)}) collective-permute-start(bf16[64,192]{1,0:T(8,128)(2,1)S(1)} %copy-done.12), channel_id=1, source_target_pairs={{0,3},{1,0},{2,1},{3,2},{4,7},{5,4},{6,5},{7,6},{8,11},{9,8},{10,9... | collective-permute-start | bytes 73736 | tf_op jit(solution)/shard_map/ppermute | solution.py:419
  99.6 2.3 %copy-start.6 = (f32[64,192]{1,0:T(8,128)}, f32[64,192]{1,0:T(8,128)S(1)}, u32[]{:S(2)}) copy-start(f32[64,192]{1,0:T(8,128)S(1)} %add_divide_fusion.own_ref) | copy-start | bytes 147460
  99.6 5.8 %collective-permute-start.5 = (f32[64,192]{1,0:T(8,128)S(1)}, f32[64,192]{1,0:T(8,128)S(1)}, u32[]{:S(2)}, u32[]{:S(2)}) collective-permute-start(f32[64,192]{1,0:T(8,128)S(1)} %add_divide_fusion.own_ref), channel_id=1, source_target_pairs={{0,4},{4,0},{8,12},{12,8},{16,20},{20,16},{24,28},{28,24},{32,36},... | collective-permute-start | bytes 147464 | tf_op jit(solution)/shard_map/ppermute | solution.py:34
  105.4 4.5 %copy-start.8 = (f32[64,192]{1,0:T(8,128)}, f32[64,192]{1,0:T(8,128)S(1)}, u32[]{:S(2)}) copy-start(f32[64,192]{1,0:T(8,128)S(1)} %collective-permute-done.5.other_ref) | copy-start | bytes 147460
  112.7 17.2 %copy-start.10 = (bf16[64,128]{1,0:T(8,128)(2,1)S(1)}, bf16[64,128]{1,0:T(8,128)(2,1)}, u32[]{:S(2)}) copy-start(bf16[64,128]{1,0:T(8,128)(2,1)} %get-tuple-element.34) | copy-start | bytes 49156
  112.7 43.2 %collective-permute-start.13 = (bf16[64,128]{1,0:T(8,128)(2,1)}, bf16[64,128]{1,0:T(8,128)(2,1)S(1)}, u32[]{:S(2)}, u32[]{:S(2)}) collective-permute-start(bf16[64,128]{1,0:T(8,128)(2,1)} %get-tuple-element.34), channel_id=1, source_target_pairs={{0,56},{4,60},{8,0},{12,4},{16,8},{20,12},{24,16},{28,20},{32,24},... | collective-permute-start | bytes 49160 | tf_op jit(solution)/shard_map/ppermute | solution.py:42
  114.1 41.8 %collective-permute-start.12 = (bf16[64,128]{1,0:T(8,128)(2,1)}, bf16[64,128]{1,0:T(8,128)(2,1)S(1)}, u32[]{:S(2)}, u32[]{:S(2)}) collective-permute-start(bf16[64,128]{1,0:T(8,128)(2,1)} %get-tuple-element.34), channel_id=1, source_target_pairs={{0,48},{4,52},{8,56},{12,60},{16,0},{20,4},{24,8},{28,12},{32,16},... | collective-permute-start | bytes 49160 | tf_op jit(solution)/shard_map/ppermute | solution.py:42
  115.5 40.4 %collective-permute-start.11 = (bf16[64,128]{1,0:T(8,128)(2,1)}, bf16[64,128]{1,0:T(8,128)(2,1)S(1)}, u32[]{:S(2)}, u32[]{:S(2)}) collective-permute-start(bf16[64,128]{1,0:T(8,128)(2,1)} %get-tuple-element.34), channel_id=1, source_target_pairs={{0,40},{4,44},{8,48},{12,52},{16,56},{20,60},{24,0},{28,4},{32,8},... | collective-permute-start | bytes 49160 | tf_op jit(solution)/shard_map/ppermute | solution.py:42
  119.2 36.6 %collective-permute-start.10 = (bf16[64,128]{1,0:T(8,128)(2,1)}, bf16[64,128]{1,0:T(8,128)(2,1)S(1)}, u32[]{:S(2)}, u32[]{:S(2)}) collective-permute-start(bf16[64,128]{1,0:T(8,128)(2,1)} %get-tuple-element.34), channel_id=1, source_target_pairs={{0,32},{4,36},{8,40},{12,44},{16,48},{20,52},{24,56},{28,60},{32,0... | collective-permute-start | bytes 49160 | tf_op jit(solution)/shard_map/ppermute | solution.py:42
  121.9 8.0 %collective-permute-start.7 = (bf16[64,128]{1,0:T(8,128)(2,1)}, bf16[64,128]{1,0:T(8,128)(2,1)S(1)}, u32[]{:S(2)}, u32[]{:S(2)}) collective-permute-start(bf16[64,128]{1,0:T(8,128)(2,1)} %get-tuple-element.34), channel_id=1, source_target_pairs={{0,8},{4,12},{8,16},{12,20},{16,24},{20,28},{24,32},{28,36},{32,40... | collective-permute-start | bytes 49160 | tf_op jit(solution)/shard_map/ppermute | solution.py:42
  122.8 44.9 %all-to-all-start.2 = ((bf16[32,96,128]{2,1,0:T(8,128)(2,1)}), bf16[32,96,128]{2,1,0:T(8,128)(2,1)S(1)}, u32[]{:S(2)}, u32[]{:S(2)}) async-start(bf16[32,96,128]{2,1,0:T(8,128)(2,1)} %get-tuple-element.35), calls=%async_computation.2 | async-start | bytes 1572864 | tf_op jit(solution)/shard_map/all_to_all | solution.py:46
  129.9 19.2 %collective-permute-start.8 = (bf16[64,128]{1,0:T(8,128)(2,1)S(1)}, bf16[64,128]{1,0:T(8,128)(2,1)S(1)}, u32[]{:S(2)}, u32[]{:S(2)}) collective-permute-start(bf16[64,128]{1,0:T(8,128)(2,1)S(1)} %copy-done.10), channel_id=1, source_target_pairs={{0,16},{4,20},{8,24},{12,28},{16,32},{20,36},{24,40},{28,44},{32,4... | collective-permute-start | bytes 49160 | tf_op jit(solution)/shard_map/ppermute | solution.py:42
  149.1 6.7 %collective-permute-start.9 = (bf16[64,128]{1,0:T(8,128)(2,1)S(1)}, bf16[64,128]{1,0:T(8,128)(2,1)S(1)}, u32[]{:S(2)}, u32[]{:S(2)}) collective-permute-start(bf16[64,128]{1,0:T(8,128)(2,1)S(1)} %copy-done.10), channel_id=1, source_target_pairs={{0,24},{4,28},{8,32},{12,36},{16,40},{20,44},{24,48},{28,52},{32,5... | collective-permute-start | bytes 49160 | tf_op jit(solution)/shard_map/ppermute | solution.py:42
  155.9 7.0 %collective-permute-start.16 = (bf16[8,64,128]{2,1,0:T(8,128)(2,1)S(1)}, bf16[8,64,128]{2,1,0:T(8,128)(2,1)S(1)}, u32[]{:S(2)}, u32[]{:S(2)}) collective-permute-start(bf16[8,64,128]{2,1,0:T(8,128)(2,1)S(1)} %constant_dynamic-update-slice_fusion), channel_id=1, source_target_pairs={{0,192},{4,196},{8,200},{12,204},{16,208},{20,212},{24,216},{28,22... | collective-permute-start | bytes 393224 | tf_op jit(solution)/shard_map/ppermute | solution.py:42
  159.0 6.6 %collective-permute-start.15 = (bf16[8,64,128]{2,1,0:T(8,128)(2,1)S(1)}, bf16[8,64,128]{2,1,0:T(8,128)(2,1)S(1)}, u32[]{:S(2)}, u32[]{:S(2)}) collective-permute-start(bf16[8,64,128]{2,1,0:T(8,128)(2,1)S(1)} %constant_dynamic-update-slice_fusion), channel_id=1, source_target_pairs={{0,128},{4,132},{8,136},{12,140},{16,144},{20,148},{24,152},{28,15... | collective-permute-start | bytes 393224 | tf_op jit(solution)/shard_map/ppermute | solution.py:42
  159.8 7.1 %collective-permute-start.14 = (bf16[8,64,128]{2,1,0:T(8,128)(2,1)S(1)}, bf16[8,64,128]{2,1,0:T(8,128)(2,1)S(1)}, u32[]{:S(2)}, u32[]{:S(2)}) collective-permute-start(bf16[8,64,128]{2,1,0:T(8,128)(2,1)S(1)} %constant_dynamic-update-slice_fusion), channel_id=1, source_target_pairs={{0,64},{4,68},{8,72},{12,76},{16,80},{20,84},{24,88},{28,92},{32,9... | collective-permute-start | bytes 393224 | tf_op jit(solution)/shard_map/ppermute | solution.py:42
  166.9 0.8 copy-start
  166.9 8.4 %collective-permute-start.17 = (bf16[4,8,64,128]{3,2,1,0:T(8,128)(2,1)S(1)}, bf16[4,8,64,128]{3,2,1,0:T(8,128)(2,1)S(1)}, u32[]{:S(2)}, u32[]{:S(2)}) collective-permute-start(bf16[4,8,64,128]{3,2,1,0:T(8,128)(2,1)S(1)} %pad_maximum_fusion.after_ref.mine_ref), channel_id=1, source_target_pairs={{0,4},{4,0},{8,12},{12,8},{16,20},{20,16},{24,28},{28,24},{32,36},... | collective-permute-start | bytes 1572872 | tf_op jit(solution)/shard_map/ppermute | solution.py:34
  167.7 0.9 copy-start.1
  175.3 0.8 copy-start.5

commit v3 on v2

--- a/solution.py
+++ b/solution.py
@@ -11,7 +11,7 @@
 F32 = jnp.float32
 CHIPS = 32
 CENTRES = 32
-GROUP = 4
+GROUP = 8
 VMEM_LIMIT = 60 * 1024 * 1024
 
 XZ_GROUPS = [[chip * 2 + core for chip in range(CHIPS)] for core in range(2)]
@@ -81,11 +81,12 @@
 
 def mixing_kernel(key_ref, out_ref):
     for block in range(8):
-        slot = lax.broadcasted_iota(jnp.int32, (128, 128), 0) + 128 * block
-        total = jnp.zeros((128, 128), F32)
+        slot = lax.broadcasted_iota(jnp.int16, (128, 128), 0)
+        key = (key_ref[...] - 128 * block).astype(jnp.int16)
+        total = jnp.zeros((128, 128), BF)
         for k in range(32):
-            total = total + jnp.where(slot == key_ref[k : k + 1, :], 1.0, 0.0)
-        out_ref[128 * block : 128 * block + 128, :] = total.astype(BF)
+            total = total + jnp.where(slot == key[k : k + 1, :], jnp.ones((), BF), jnp.zeros((), BF))
+        out_ref[128 * block : 128 * block + 128, :] = total
 
 
 def make_mixing(keys):
@@ -217,14 +218,17 @@
         for d, ref in enumerate((vg0_ref, vg1_ref, vg2_ref, vg3_ref)):
             at = (own + d) % 4
             ref[...] = (nn(dk, wk4_ref[at]) + nn(dv, wv4_ref[at])).astype(ref.dtype)
+        keep_ref[1728:, :] = jnp.zeros((320, 128), F32)
+        give_ref[1728:, :] = jnp.zeros((320, 128), BF)
         for core in range(2):
             @pl.when(place_ref[1] == core)
             def _():
                 for t in range(3):
                     keep = 3 * core + t
                     give = 3 * (1 - core) + t
-                    keep_ref[t] = acc_ref[:, 128 * keep : 128 * keep + 128]
-                    give_ref[t] = acc_ref[:, 128 * give : 128 * give + 128]
+                    rows = slice(576 * t, 576 * t + 576)
+                    keep_ref[rows, :] = acc_ref[:, 128 * keep : 128 * keep + 128]
+                    give_ref[rows, :] = acc_ref[:, 128 * give : 128 * give + 128].astype(BF)
 
 
 def attend(place, tokens, q, k, v, grads, virtual, wk, wv, wk4, wv4):
@@ -234,8 +238,8 @@
     fixed3 = lambda i: (0, 0, 0)
     out_shape = (
         jax.ShapeDtypeStruct((2048, 192), BF),
-        jax.ShapeDtypeStruct((3, 576, 128), F32),
-        jax.ShapeDtypeStruct((3, 576, 128), F32),
+        jax.ShapeDtypeStruct((2048, 128), F32),
+        jax.ShapeDtypeStruct((2048, 128), BF),
         jax.ShapeDtypeStruct((64, 192), F32),
         jax.ShapeDtypeStruct((64, 192), BF),
         jax.ShapeDtypeStruct((64, 192), BF),
@@ -244,7 +248,7 @@
     small = pl.BlockSpec((64, 192), fixed2)
     weight = pl.BlockSpec((192, 768), fixed2)
     head = pl.BlockSpec((rows, 192), lambda i: (i, 0))
-    half = pl.BlockSpec((3, 576, 128), fixed3)
+    half = pl.BlockSpec((2048, 128), fixed2)
     return pl.pallas_call(
         attend_kernel,
         out_shape=out_shape,
@@ -274,8 +278,7 @@
     )(place, tokens, q, k, v, grads, virtual, wk, wv, wk4, wv4)
 
 
-def spread_kernel(own_ref, other_ref, mix_ref, pieces_ref, *refs):
-    out_ref, total_ref = refs[-2:]
+def spread_kernel(own_ref, other_ref, mix_ref, out_ref):
     mix = mix_ref[...]
     zeros = jnp.zeros((64, 192), BF)
 
@@ -294,26 +297,37 @@
     out_ref[:, 32:64, :] = other[:, 0:128].reshape(CHIPS, 32, 128)
     out_ref[:, 64:96, 0:64] = own[:, 128:192].reshape(CHIPS, 32, 64)
     out_ref[:, 64:96, 64:128] = other[:, 128:192].reshape(CHIPS, 32, 64)
+
+
+def spread(own, other, mix):
+    whole = pl.BlockSpec(memory_space=pltpu.VMEM)
+    return pl.pallas_call(
+        spread_kernel,
+        out_shape=jax.ShapeDtypeStruct((CHIPS, 96, 128), BF),
+        in_specs=[whole] * 3,
+        name="spread",
+    )(own, other, mix)
+
+
+def total_kernel(pieces_ref, *refs):
+    out_ref = refs[-1]
     total = pieces_ref[0].astype(F32)
     for chip in range(1, CHIPS):
         total = total + pieces_ref[chip].astype(F32)
-    total_ref[...] = total.astype(BF)
-
-
-def spread(own, other, mix, pieces, *after):
-    whole = pl.BlockSpec(memory_space=pltpu.VMEM)
-    return pl.pallas_call(
-        spread_kernel,
-        out_shape=(
-            jax.ShapeDtypeStruct((CHIPS, 96, 128), BF),
-            jax.ShapeDtypeStruct((64, 128), BF),
-        ),
-        in_specs=[whole] * 4 + [pl.BlockSpec(memory_space=pl.ANY)] * len(after),
-        name="spread",
-    )(own, other, mix, pieces, *after)
-
-
-def assemble_kernel(place_ref, mine_ref, theirs_ref, after_ref, *out_refs):
+    out_ref[...] = total.astype(BF)
+
+
+def sum_pieces(pieces, *after):
+    return pl.pallas_call(
+        total_kernel,
+        out_shape=jax.ShapeDtypeStruct((64, 128), BF),
+        in_specs=[pl.BlockSpec(memory_space=pltpu.VMEM)]
+        + [pl.BlockSpec(memory_space=pl.ANY)] * len(after),
+        name="sum_pieces",
+    )(pieces, *after)
+
+
+def assemble(place_ref, mine_ref, theirs_ref, out_refs):
     for piece in range(27):
         dx = (place_ref[2] - piece // 8 + 4) % 4
         dz = (place_ref[3] - piece % 8 + 8) % 8
@@ -327,24 +341,15 @@
         out_ref[rows, 384 + tile : 512 + tile] = jnp.where(low, theirs, mine)
 
 
-def assemble(place, mine, theirs, after):
-    out = jax.ShapeDtypeStruct((192, 768), F32)
-    whole = pl.BlockSpec(memory_space=pltpu.VMEM)
-    return pl.pallas_call(
-        assemble_kernel,
-        out_shape=(out, out, out),
-        in_specs=[
-            pl.BlockSpec(memory_space=pltpu.SMEM), whole, whole, pl.BlockSpec(memory_space=pl.ANY)
-        ],
-        name="assemble",
-    )(place, mine, theirs, after)
-
-
-def scatter_kernel(index_ref, rows_ref, after_ref, out_ref, turned_ref):
+def scatter_kernel(
+    place_ref, index_ref, rows_ref, mine_ref, theirs_ref,
+    out_ref, wq_ref, wk_ref, wv_ref, turned_ref,
+):
     step = pl.program_id(0)
 
     @pl.when(step == 0)
     def _():
+        assemble(place_ref, mine_ref, theirs_ref, (wq_ref, wk_ref, wv_ref))
         for g in range(8):
             chips = slice(4 * g, 4 * g + 4)
             first = rows_ref[chips, 0:32, :].reshape(128, 128).astype(F32).T.astype(BF)
@@ -362,21 +367,28 @@
     out_ref[...] = nt(turned_ref[...], select)
 
 
-def scatter_rows(index, rows, after):
+def scatter_rows(place, index, rows, mine, theirs):
+    weight = jax.ShapeDtypeStruct((192, 768), F32)
+    weight_block = pl.BlockSpec((192, 768), lambda i: (0, 0))
+    piece_block = pl.BlockSpec((4, 8, 64, 128), lambda i: (0, 0, 0, 0))
     return pl.pallas_call(
         scatter_kernel,
-        out_shape=jax.ShapeDtypeStruct((192, 2048), F32),
+        out_shape=(jax.ShapeDtypeStruct((192, 2048), F32), weight, weight, weight),
         grid=(8,),
         in_specs=[
+            pl.BlockSpec(memory_space=pltpu.SMEM),
             pl.BlockSpec((1, 2048), lambda i: (0, 0)),
             pl.BlockSpec((CHIPS, 96, 128), lambda i: (0, 0, 0)),
-            pl.BlockSpec(memory_space=pl.ANY),
+            piece_block,
+            piece_block,
         ],
-        out_specs=pl.BlockSpec((192, 256), lambda i: (0, i)),
+        out_specs=(
+            pl.BlockSpec((192, 256), lambda i: (0, i)), weight_block, weight_block, weight_block
+        ),
         scratch_shapes=[pltpu.VMEM((192, 2048), BF)],
         compiler_params=pltpu.CompilerParams(vmem_limit_bytes=VMEM_LIMIT),
         name="scatter_rows",
-    )(index, rows, after)
+    )(place, index, rows, mine, theirs)
 
 
 def layer(tokens, w_query, w_key, w_value, grad_out, owned_cls, send_rows, neigh_slot, neigh_count):
@@ -418,19 +430,21 @@
 
     around = lambda x, d: lax.ppermute(x, "mp", [(i, (i + d) % 4) for i in range(4)])
     moved = [around(vg, d + 1) for d, vg in enumerate((vg1, vg2, vg3))]
-    half = (keep + core_swap(give)).astype(BF).reshape(27, 64, 128)
-    pieces = chip_exchange(jnp.pad(half, ((0, CHIPS - 27), (0, 0), (0, 0))))
+    half = (keep + core_swap(give).astype(F32)).astype(BF)
+    pieces = chip_exchange(half.reshape(CHIPS, 64, 128))
 
     shared = (vg0 + moved[0].astype(F32) + moved[1].astype(F32) + moved[2].astype(F32)) / divisor
-    outgoing, total = spread(
-        shared, core_swap(shared), mix, pieces, context.transpose(1, 0, 2)
-    )
+    outgoing = spread(shared, core_swap(shared), mix)
+    total = sum_pieces(pieces, outgoing, context.transpose(1, 0, 2))
     arrived = chip_exchange(outgoing)
-    row = jnp.stack([total] + [along(total, 0, d) for d in range(1, 8)])
+    near = jnp.stack([total] + [along(total, 0, d) for d in range(1, 4)])
+    across = along(near, 0, 4)
+    row = jnp.concatenate([near, across], axis=0)
     mine = jnp.stack([row] + [along(row, d, 0) for d in range(1, 4)])
     theirs = core_swap(mine)
-    grad_cls = scatter_rows(index.reshape(1, 2048), arrived, mine)
-    grad_query, grad_key, grad_value = assemble(place, mine, theirs, grad_cls)
+    grad_cls, grad_query, grad_key, grad_value = scatter_rows(
+        place, index.reshape(1, 2048), arrived, mine, theirs
+    )
     return (context, grad_query, grad_key, grad_value, grad_cls)
 
 

time: 182 us -> 173 us (0.951)
  the two profiles are of different devices: /device:TPU:8 before, /device:TPU:1 now
where the time goes in v3:
time: 173 us; the launch traced here: 172 us
  starting transfers between devices  60 us (35%)
  Pallas kernels  48.3 us (28%)
  waiting for transfers between devices  27.9 us (16%)
  local copies, waits for them, and re-layouts  19.5 us (11%)
  blocking collectives  9.64 us (6%)
  other arithmetic  5.39 us (3%)
    all_to_all x3, starting transfers between devices, chip_exchange(): lax.all_to_all(x, 'nodes', split_axis=0, concat_axis=0, tiled=True, axis_...  26.2 us
    ppermute x7, waiting for transfers between devices, along(): return lax.ppermute(x, 'nodes', pairs)  20.9 us
    pallas_call x1, Pallas kernels, attend(): pl.pallas_call(attend_kernel, out_shape=out_shape, grid=(steps,), in_spec...  19.4 us
    ppermute x5, starting transfers between devices, core_swap(): return lax.ppermute(x, 'nodes', CORE_SWAP)  16.4 us
    ppermute x7, starting transfers between devices, along(): return lax.ppermute(x, 'nodes', pairs)  13.9 us
    all_gather x1, blocking collectives, layer(): virtual = lax.all_gather(local, 'mp', axis=1, tiled=True)  9.64 us
    pallas_call x1, Pallas kernels, scatter_rows(): pl.pallas_call(scatter_kernel, out_shape=(jax.ShapeDtypeStruct((192, 2048...  7.23 us
    pallas_call x1, Pallas kernels, gather_rows(): pl.pallas_call(gather_kernel, out_shape=jax.ShapeDtypeStruct((CHIPS, 96,...  6.69 us
  transfers between devices with their start and end apart: 18, of which 13 were waited for; matrix products, arithmetic and copies ran while one was open for 10% of the time, Pallas kernels for 7%

profile of v3, /device:TPU:1, one launch (start us, length us, event | category | flops | bytes accessed | tf_op | source)
XLA Modules:
  0.0 171.6 jit_solution(11513894993270014155)
XLA Ops:
  0.6 0.8 copy.34
  1.6 0.7 reshape.56.index_ref
  2.3 6.7 %gather_rows.1 = bf16[32,96,128]{2,1,0:T(8,128)(2,1)} custom-call(s32[8,1,256]{2,1,0:T(1,128)} %reshape.56.index_ref, bf16[192,2048]{1,0:T(8,128)(2,1)} %table_ref.1), custom_call_target="tpu_custom_call" | custom-call | tf_op jit(solution)/shard_map/gather_rows/pallas_call | solution.py:68
  9.0 12.1 %all-to-all-start = ((bf16[32,96,128]{2,1,0:T(8,128)(2,1)}), bf16[32,96,128]{2,1,0:T(8,128)(2,1)}, u32[]{:S(2)}, u32[]{:S(2)}) async-start(bf16[32,96,128]{2,1,0:T(8,128)(2,1)} %gather_rows.1), calls=%async_computation | async-start | bytes 1572864 | tf_op jit(solution)/shard_map/all_to_all | solution.py:46
  21.2 0.1 lt.22
  21.4 1.0 collective-permute-start
  22.4 0.4 reshape.58
  22.8 0.4 reshape.59
  23.2 1.0 copy_bitcast_fusion
  24.1 2.5 %reshape.53 = bf16[32,3,64,64]{3,2,0,1:T(8,128)(2,1)S(1)} reshape(bf16[32,3,4096]{2,0,1:T(8,128)(2,1)} %param.13) | data formatting | bytes 1572864 | tf_op jit(solution)/shard_map/reshape | solution.py:413
  26.7 1.4 copy.33
  28.1 1.3 reshape.54
  29.4 1.3 copy.42.refs_3_.grad_ref
  30.7 6.0 %project.1 = (bf16[2048,192]{1,0:T(8,128)(2,1)}, bf16[2048,192]{1,0:T(8,128)(2,1)}, bf16[2048,192]{1,0:T(8,128)(2,1)}) custom-call(bf16[2048,768]{1,0:T(8,128)(2,1)} %bitcast.50, bf16[192,768]{1,0:T(8,128)(2,1)} %wq_ref.1, bf16[192,768]{1,0:T(8,128)(2,1)} %wk_ref.3, bf16[192,768]{1,0:T(8,128)(2,1)} %wv_ref.3), custom_call_target="tpu_custom_call" | custom-call | tf_op jit(solution)/shard_map/project/pallas_call | solution.py:134
  36.6 0.7 select_bitcast_fusion.1.key_ref
  37.3 2.3 %make_mixing.1.mix_ref = bf16[1024,128]{1,0:T(8,128)(2,1)} custom-call(s32[32,128]{1,0:T(8,128)} %select_bitcast_fusion.1.key_ref), custom_call_target="tpu_custom_call" | custom-call | tf_op jit(solution)/shard_map/make_mixing/pallas_call | solution.py:93
  39.6 0.8 all-to-all-done.rows_ref
  40.4 2.3 %mix_rows.1 = (f32[64,192]{1,0:T(8,128)}, f32[64,192]{1,0:T(8,128)}) custom-call(bf16[32,96,128]{2,1,0:T(8,128)(2,1)} %all-to-all-done.rows_ref, bf16[1024,128]{1,0:T(8,128)(2,1)} %make_mixing.1.mix_ref, bf16[2048,192]{1,0:T(8,128)(2,1)} %get-tuple-element.21.refs_0_.q_ref, bf16[2048,192]{1,0:T(8,128)(2,1)} %get-tuple-element.22.refs_1_.k_ref, ...), custom_call_target="tpu_custom_call" | custom-call | tf_op jit(solution)/shard_map/mix_rows/pallas_call | solution.py:115
  42.7 4.9 %collective-permute-start.1 = (f32[64,192]{1,0:T(8,128)}, f32[64,192]{1,0:T(8,128)S(1)}, u32[]{:S(2)}, u32[]{:S(2)}) collective-permute-start(f32[64,192]{1,0:T(8,128)} %get-tuple-element.25), channel_id=1, source_target_pairs={{0,4},{4,0},{8,12},{12,8},{16,20},{20,16},{24,28},{28,24},{32,36},... | collective-permute-start | bytes 147464 | tf_op jit(solution)/shard_map/ppermute | solution.py:34
  47.7 0.7 pad_add_fusion.1.place_ref
  48.3 0.5 collective-permute-done.1
  48.8 0.9 fusion
  49.7 9.6 %all-gather = bf16[4,192,64]{1,2,0:T(8,128)(2,1)S(1)} all-gather(bf16[1,192,64]{1,2,0:T(8,128)(2,1)S(1)} %fusion), channel_id=1, replica_groups=mesh['nodes'=64,'mp'=4] {'mp'}, dimensions={0}, use_global_device_ids=true | all-gather | bytes 122880 | tf_op jit(solution)/shard_map/all_gather | solution.py:424
  59.5 0.8 reshape.64
  60.2 19.4 %attend.1 = (bf16[2048,192]{1,0:T(8,128)(2,1)}, f32[2048,128]{1,0:T(8,128)}, bf16[2048,128]{1,0:T(8,128)(2,1)}, f32[64,192]{1,0:T(8,128)}, bf16[64,192]{1,0:T(8,...) custom-call(s32[4]{0:T(128)} %pad_add_fusion.1.place_ref, bf16[2048,768]{1,0:T(8,128)(2,1)} %bitcast.51, ...), custom_call_target="tpu_custom_call" | custom-call | tf_op jit(solution)/shard_map/attend/pallas_call | solution.py:252
  79.7 3.5 %collective-permute-start.6 = (bf16[2048,128]{1,0:T(8,128)(2,1)}, bf16[2048,128]{1,0:T(8,128)(2,1)S(1)}, u32[]{:S(2)}, u32[]{:S(2)}) collective-permute-start(bf16[2048,128]{1,0:T(8,128)(2,1)} %get-tuple-element.32), channel_id=1, source_target_pairs={{0,4},{4,0},{8,12},{12,8},{16,20},{20,16},{24,28},{28,24},{32,36},... | collective-permute-start | bytes 1572872 | tf_op jit(solution)/shard_map/ppermute | solution.py:34
  83.2 1.7 %collective-permute-done.6 = bf16[2048,128]{1,0:T(8,128)(2,1)S(1)} collective-permute-done((bf16[2048,128]{1,0:T(8,128)(2,1)}, bf16[2048,128]{1,0:T(8,128)(2,1)S(1)}, u32[]{:S(2)}, u32[]{:S(2)}) %collective-permute-start.6) | collective-permute-done | bytes 524320 | tf_op jit(solution)/shard_map/ppermute | solution.py:34
  84.9 2.2 %add_convert_fusion = bf16[2048,128]{1,0:T(8,128)(2,1)} fusion(f32[2048,128]{1,0:T(8,128)} %get-tuple-element.31, bf16[2048,128]{1,0:T(8,128)(2,1)S(1)} %collective-permute-done.6), kind=kLoop, calls=%fused_computation | loop fusion | flops 786432 | bytes 2097152 | tf_op jit(solution)/shard_map/convert_element_type | solution.py:433
  87.2 4.6 %all-to-all-start.2 = ((bf16[32,64,128]{2,1,0:T(8,128)(2,1)}), bf16[32,64,128]{2,1,0:T(8,128)(2,1)}, u32[]{:S(2)}, u32[]{:S(2)}) async-start(bf16[32,64,128]{2,1,0:T(8,128)(2,1)} %bitcast.16), calls=%async_computation.2 | async-start | bytes 1048576 | tf_op jit(solution)/shard_map/all_to_all | solution.py:46
  91.8 1.1 collective-permute-start.2
  92.9 2.4 %collective-permute-start.3 = (bf16[64,192]{1,0:T(8,128)(2,1)S(1)}, bf16[64,192]{1,0:T(8,128)(2,1)S(1)}, u32[]{:S(2)}, u32[]{:S(2)}) collective-permute-start(bf16[64,192]{1,0:T(8,128)(2,1)S(1)} %copy-done.12), channel_id=1, source_target_pairs={{0,2},{1,3},{2,0},{3,1},{4,6},{5,7},{6,4},{7,5},{8,10},{9,11},{10,... | collective-permute-start | bytes 73736 | tf_op jit(solution)/shard_map/ppermute | solution.py:431
  95.3 0.1 collective-permute-start.4
  95.4 0.5 collective-permute-done.2
  95.9 1.6 collective-permute-done.3
  97.4 1.0 collective-permute-done.4
  98.6 2.0 %collective-permute-start.5 = (f32[64,192]{1,0:T(8,128)S(1)}, f32[64,192]{1,0:T(8,128)S(1)}, u32[]{:S(2)}, u32[]{:S(2)}) collective-permute-start(f32[64,192]{1,0:T(8,128)S(1)} %add_divide_fusion.own_ref), channel_id=1, source_target_pairs={{0,4},{4,0},{8,12},{12,8},{16,20},{20,16},{24,28},{28,24},{32,36},... | collective-permute-start | bytes 147464 | tf_op jit(solution)/shard_map/ppermute | solution.py:34
  100.6 0.5 copy.43
  101.1 1.6 reshape.60
  102.7 1.4 copy.44
  104.2 2.0 %reshape.61 = bf16[32,3,4096]{2,0,1:T(8,128)(2,1)} reshape(bf16[32,3,64,64]{3,2,0,1:T(8,128)(2,1)S(1)} %copy.44) | data formatting | bytes 1572864 | tf_op jit(solution)/shard_map/reshape | solution.py:429
  106.2 0.6 copy-done.8
  106.9 2.7 %spread.1.refs_0_ = bf16[32,96,128]{2,1,0:T(8,128)(2,1)} custom-call(f32[64,192]{1,0:T(8,128)} %copy-done.6, f32[64,192]{1,0:T(8,128)} %copy-done.8, bf16[1024,128]{1,0:T(8,128)(2,1)} %make_mixing.1.mix_ref), custom_call_target="tpu_custom_call" | custom-call | tf_op jit(solution)/shard_map/spread/pallas_call | solution.py:304
  109.6 9.4 %all-to-all-start.1 = ((bf16[32,96,128]{2,1,0:T(8,128)(2,1)}), bf16[32,96,128]{2,1,0:T(8,128)(2,1)S(1)}, u32[]{:S(2)}, u32[]{:S(2)}) async-start(bf16[32,96,128]{2,1,0:T(8,128)(2,1)} %spread.1.refs_0_), calls=%async_computation.1 | async-start | bytes 1572864 | tf_op jit(solution)/shard_map/all_to_all | solution.py:46
  119.0 1.7 %sum_pieces.1 = bf16[64,128]{1,0:T(8,128)(2,1)} custom-call(bf16[32,64,128]{2,1,0:T(8,128)(2,1)} %all-to-all-done.2.pieces_ref, bf16[32,96,128]{2,1,0:T(8,128)(2,1)} %spread.1.refs_0_, bf16[3,32,4096]{2,1,0:T(8,128)(2,1)} %bitcast.54), custom_call_target="tpu_custom_call" | custom-call | tf_op jit(solution)/shard_map/sum_pieces/pallas_call | solution.py:321
  120.7 3.0 %collective-permute-start.9 = (bf16[64,128]{1,0:T(8,128)(2,1)}, bf16[64,128]{1,0:T(8,128)(2,1)S(1)}, u32[]{:S(2)}, u32[]{:S(2)}) collective-permute-start(bf16[64,128]{1,0:T(8,128)(2,1)} %sum_pieces.1), channel_id=1, source_target_pairs={{0,24},{4,28},{8,32},{12,36},{16,40},{20,44},{24,48},{28,52},{32,5... | collective-permute-start | bytes 49160 | tf_op jit(solution)/shard_map/ppermute | solution.py:42
  123.7 2.4 %collective-permute-start.8 = (bf16[64,128]{1,0:T(8,128)(2,1)}, bf16[64,128]{1,0:T(8,128)(2,1)S(1)}, u32[]{:S(2)}, u32[]{:S(2)}) collective-permute-start(bf16[64,128]{1,0:T(8,128)(2,1)} %sum_pieces.1), channel_id=1, source_target_pairs={{0,16},{4,20},{8,24},{12,28},{16,32},{20,36},{24,40},{28,44},{32,4... | collective-permute-start | bytes 49160 | tf_op jit(solution)/shard_map/ppermute | solution.py:42
  126.1 0.3 collective-permute-start.7
  126.4 0.8 constant_dynamic-update-slice_fusion.4
  127.2 11.8 %collective-permute-done.9 = bf16[64,128]{1,0:T(8,128)(2,1)S(1)} collective-permute-done((bf16[64,128]{1,0:T(8,128)(2,1)}, bf16[64,128]{1,0:T(8,128)(2,1)S(1)}, u32[]{:S(2)}, u32[]{:S(2)}) %collective-permute-start.9) | collective-permute-done | bytes 16416 | tf_op jit(solution)/shard_map/ppermute | solution.py:42
  139.0 0.8 collective-permute-done.8
  139.8 0.7 pad_maximum_fusion.1
  140.5 4.4 %collective-permute-start.10 = (bf16[4,64,128]{2,1,0:T(8,128)(2,1)S(1)}, bf16[4,64,128]{2,1,0:T(8,128)(2,1)S(1)}, u32[]{:S(2)}, u32[]{:S(2)}) collective-permute-start(bf16[4,64,128]{2,1,0:T(8,128)(2,1)S(1)} %pad_maximum_fusion.1), channel_id=1, source_target_pairs={{0,32},{4,36},{8,40},{12,44},{16,48},{20,52},{24,56},{28,60},{32,0... | collective-permute-start | bytes 196616 | tf_op jit(solution)/shard_map/ppermute | solution.py:42
  145.0 2.7 %collective-permute-done.10 = bf16[4,64,128]{2,1,0:T(8,128)(2,1)S(1)} collective-permute-done((bf16[4,64,128]{2,1,0:T(8,128)(2,1)S(1)}, bf16[4,64,128]{2,1,0:T(8,128)(2,1)S(1)}, u32[]{:S(2)}, u32[]{:S(2)}) %collective-permute-start.10) | collective-permute-done | bytes 65568 | tf_op jit(solution)/shard_map/ppermute | solution.py:42
  147.6 2.7 %collective-permute-start.13 = (bf16[8,64,128]{2,1,0:T(8,128)(2,1)S(1)}, bf16[8,64,128]{2,1,0:T(8,128)(2,1)S(1)}, u32[]{:S(2)}, u32[]{:S(2)}) collective-permute-start(bf16[8,64,128]{2,1,0:T(8,128)(2,1)S(1)} %constant_dynamic-update-slice_fusion), channel_id=1, source_target_pairs={{0,192},{4,196},{8,200},{12,204},{16,208},{20,212},{24,216},{28,22... | collective-permute-start | bytes 393224 | tf_op jit(solution)/shard_map/ppermute | solution.py:42
  150.3 0.5 collective-permute-start.12
  150.8 0.6 collective-permute-start.11
  151.4 2.2 %collective-permute-done.13 = bf16[8,64,128]{2,1,0:T(8,128)(2,1)S(1)} collective-permute-done((bf16[8,64,128]{2,1,0:T(8,128)(2,1)S(1)}, bf16[8,64,128]{2,1,0:T(8,128)(2,1)S(1)}, u32[]{:S(2)}, u32[]{:S(2)}) %collective-permute-start.13) | collective-permute-done | bytes 131104 | tf_op jit(solution)/shard_map/ppermute | solution.py:42
  153.6 2.1 %collective-permute-done.12 = bf16[8,64,128]{2,1,0:T(8,128)(2,1)S(1)} collective-permute-done((bf16[8,64,128]{2,1,0:T(8,128)(2,1)S(1)}, bf16[8,64,128]{2,1,0:T(8,128)(2,1)S(1)}, u32[]{:S(2)}, u32[]{:S(2)}) %collective-permute-start.12) | collective-permute-done | bytes 131104 | tf_op jit(solution)/shard_map/ppermute | solution.py:42
  155.7 1.3 collective-permute-done.11
  157.1 4.9 %collective-permute-start.14 = (bf16[4,8,64,128]{3,2,1,0:T(8,128)(2,1)S(1)}, bf16[4,8,64,128]{3,2,1,0:T(8,128)(2,1)S(1)}, u32[]{:S(2)}, u32[]{:S(2)}) collective-permute-start(bf16[4,8,64,128]{3,2,1,0:T(8,128)(2,1)S(1)} %pad_maximum_fusion.mine_ref), channel_id=1, source_target_pairs={{0,4},{4,0},{8,12},{12,8},{16,20},{20,16},{24,28},{28,24},{32,36},... | collective-permute-start | bytes 1572872 | tf_op jit(solution)/shard_map/ppermute | solution.py:34
  162.0 0.7 reshape_reshape.3.index_ref
  162.7 0.8 collective-permute-done.14.theirs_ref
  163.6 0.8 copy-done.5
  164.4 7.2 %scatter_rows.1 = (f32[192,2048]{1,0:T(8,128)}, f32[192,768]{1,0:T(8,128)}, f32[192,768]{1,0:T(8,128)}, f32[192,768]{1,0:T(8,128)}) custom-call(s32[4]{0:T(128)} %pad_add_fusion.1.place_ref, s32[1,2048]{1,0:T(1,128)} %reshape_reshape.3.index_ref, bf16[32,96,128]{2,1,0:T(8,128)(2,1)} %copy-done, bf16[4,8,64,128]{3,2,1,0:T(8,128)(2,1)} %copy-done.3, ...), custom_call_target="tpu_custom_call" | custom-call | tf_op jit(solution)/shard_map/scatter_rows/pallas_call | solution.py:374
  (45 shorter events, 0.7 us)
Async XLA Ops:
  2.3 18.8 %copy-start.9 = (s32[32,2,32]{2,1,0:T(2,128)S(1)}, s32[32,2,32]{2,1,0:T(2,128)}, u32[]{:S(2)}) copy-start(s32[32,2,32]{2,1,0:T(2,128)} %param.16) | copy-start | bytes 24580
  2.3 18.9 %copy-start.10 = (s32[32,2]{0,1:T(2,128)S(1)}, s32[32,2]{0,1:T(2,128)}, u32[]{:S(2)}) copy-start(s32[32,2]{0,1:T(2,128)} %param.17) | copy-start | bytes 772
  2.3 20.1 %copy-start.1 = (bf16[192,768]{1,0:T(8,128)(2,1)S(1)}, bf16[192,768]{1,0:T(8,128)(2,1)}, u32[]{:S(2)}) copy-start(bf16[192,768]{1,0:T(8,128)(2,1)} %wk_ref.3) | copy-start | bytes 884740
  9.0 13.8 %copy-start.2 = (bf16[192,768]{1,0:T(8,128)(2,1)S(1)}, bf16[192,768]{1,0:T(8,128)(2,1)}, u32[]{:S(2)}) copy-start(bf16[192,768]{1,0:T(8,128)(2,1)} %wv_ref.3) | copy-start | bytes 884740
  9.0 31.5 %all-to-all-start = ((bf16[32,96,128]{2,1,0:T(8,128)(2,1)}), bf16[32,96,128]{2,1,0:T(8,128)(2,1)}, u32[]{:S(2)}, u32[]{:S(2)}) async-start(bf16[32,96,128]{2,1,0:T(8,128)(2,1)} %gather_rows.1), calls=%async_computation | async-start | bytes 1572864 | tf_op jit(solution)/shard_map/all_to_all | solution.py:46
  21.4 15.3 %collective-permute-start = (s32[64,32]{0,1:T(8,128)S(1)}, s32[64,32]{0,1:T(8,128)S(1)}, u32[]{:S(2)}, u32[]{:S(2)}) collective-permute-start(s32[64,32]{0,1:T(8,128)S(1)} %fusion.1), channel_id=1, source_target_pairs={{0,4},{4,0},{8,12},{12,8},{16,20},{20,16},{24,28},{28,24},{32,36},... | collective-permute-start | bytes 24584 | tf_op jit(solution)/shard_map/ppermute | solution.py:34
  42.7 6.0 %collective-permute-start.1 = (f32[64,192]{1,0:T(8,128)}, f32[64,192]{1,0:T(8,128)S(1)}, u32[]{:S(2)}, u32[]{:S(2)}) collective-permute-start(f32[64,192]{1,0:T(8,128)} %get-tuple-element.25), channel_id=1, source_target_pairs={{0,4},{4,0},{8,12},{12,8},{16,20},{20,16},{24,28},{28,24},{32,36},... | collective-permute-start | bytes 147464 | tf_op jit(solution)/shard_map/ppermute | solution.py:34
  79.7 5.2 %collective-permute-start.6 = (bf16[2048,128]{1,0:T(8,128)(2,1)}, bf16[2048,128]{1,0:T(8,128)(2,1)S(1)}, u32[]{:S(2)}, u32[]{:S(2)}) collective-permute-start(bf16[2048,128]{1,0:T(8,128)(2,1)} %get-tuple-element.32), channel_id=1, source_target_pairs={{0,4},{4,0},{8,12},{12,8},{16,20},{20,16},{24,28},{28,24},{32,36},... | collective-permute-start | bytes 1572872 | tf_op jit(solution)/shard_map/ppermute | solution.py:34
  84.9 6.9 %copy-start.13 = (bf16[64,192]{1,0:T(8,128)(2,1)S(1)}, bf16[64,192]{1,0:T(8,128)(2,1)}, u32[]{:S(2)}) copy-start(bf16[64,192]{1,0:T(8,128)(2,1)} %get-tuple-element.28) | copy-start | bytes 73732
  84.9 7.9 %copy-start.12 = (bf16[64,192]{1,0:T(8,128)(2,1)S(1)}, bf16[64,192]{1,0:T(8,128)(2,1)}, u32[]{:S(2)}) copy-start(bf16[64,192]{1,0:T(8,128)(2,1)} %get-tuple-element.29) | copy-start | bytes 73732
  84.9 10.3 %copy-start.11 = (bf16[64,192]{1,0:T(8,128)(2,1)S(1)}, bf16[64,192]{1,0:T(8,128)(2,1)}, u32[]{:S(2)}) copy-start(bf16[64,192]{1,0:T(8,128)(2,1)} %get-tuple-element.30) | copy-start | bytes 73732
  84.9 13.5 %copy-start.7 = (f32[64,192]{1,0:T(8,128)S(1)}, f32[64,192]{1,0:T(8,128)}, u32[]{:S(2)}) copy-start(f32[64,192]{1,0:T(8,128)} %get-tuple-element.27) | copy-start | bytes 147460
  84.9 15.7 %copy-start.4 = (bf16[2048,192]{1,0:T(8,128)(2,1)S(1)}, bf16[2048,192]{1,0:T(8,128)(2,1)}, u32[]{:S(2)}) copy-start(bf16[2048,192]{1,0:T(8,128)(2,1)} %get-tuple-element.26) | copy-start | bytes 2359300
  87.2 22.4 %all-to-all-start.2 = ((bf16[32,64,128]{2,1,0:T(8,128)(2,1)}), bf16[32,64,128]{2,1,0:T(8,128)(2,1)}, u32[]{:S(2)}, u32[]{:S(2)}) async-start(bf16[32,64,128]{2,1,0:T(8,128)(2,1)} %bitcast.16), calls=%async_computation.2 | async-start | bytes 1048576 | tf_op jit(solution)/shard_map/all_to_all | solution.py:46
  91.8 4.1 %collective-permute-start.2 = (bf16[64,192]{1,0:T(8,128)(2,1)S(1)}, bf16[64,192]{1,0:T(8,128)(2,1)S(1)}, u32[]{:S(2)}, u32[]{:S(2)}) collective-permute-start(bf16[64,192]{1,0:T(8,128)(2,1)S(1)} %copy-done.13), channel_id=1, source_target_pairs={{0,1},{1,2},{2,3},{3,0},{4,5},{5,6},{6,7},{7,4},{8,9},{9,10},{10,1... | collective-permute-start | bytes 73736 | tf_op jit(solution)/shard_map/ppermute | solution.py:431
  92.9 4.6 %collective-permute-start.3 = (bf16[64,192]{1,0:T(8,128)(2,1)S(1)}, bf16[64,192]{1,0:T(8,128)(2,1)S(1)}, u32[]{:S(2)}, u32[]{:S(2)}) collective-permute-start(bf16[64,192]{1,0:T(8,128)(2,1)S(1)} %copy-done.12), channel_id=1, source_target_pairs={{0,2},{1,3},{2,0},{3,1},{4,6},{5,7},{6,4},{7,5},{8,10},{9,11},{10,... | collective-permute-start | bytes 73736 | tf_op jit(solution)/shard_map/ppermute | solution.py:431
  95.3 3.2 %collective-permute-start.4 = (bf16[64,192]{1,0:T(8,128)(2,1)S(1)}, bf16[64,192]{1,0:T(8,128)(2,1)S(1)}, u32[]{:S(2)}, u32[]{:S(2)}) collective-permute-start(bf16[64,192]{1,0:T(8,128)(2,1)S(1)} %copy-done.11), channel_id=1, source_target_pairs={{0,3},{1,0},{2,1},{3,2},{4,7},{5,4},{6,5},{7,6},{8,11},{9,8},{10,9... | collective-permute-start | bytes 73736 | tf_op jit(solution)/shard_map/ppermute | solution.py:431
  98.6 4.2 %copy-start.6 = (f32[64,192]{1,0:T(8,128)}, f32[64,192]{1,0:T(8,128)S(1)}, u32[]{:S(2)}) copy-start(f32[64,192]{1,0:T(8,128)S(1)} %add_divide_fusion.own_ref) | copy-start | bytes 147460
  98.6 7.7 %collective-permute-start.5 = (f32[64,192]{1,0:T(8,128)S(1)}, f32[64,192]{1,0:T(8,128)S(1)}, u32[]{:S(2)}, u32[]{:S(2)}) collective-permute-start(f32[64,192]{1,0:T(8,128)S(1)} %add_divide_fusion.own_ref), channel_id=1, source_target_pairs={{0,4},{4,0},{8,12},{12,8},{16,20},{20,16},{24,28},{28,24},{32,36},... | collective-permute-start | bytes 147464 | tf_op jit(solution)/shard_map/ppermute | solution.py:34
  106.2 0.6 copy-start.8
  109.6 53.2 %all-to-all-start.1 = ((bf16[32,96,128]{2,1,0:T(8,128)(2,1)}), bf16[32,96,128]{2,1,0:T(8,128)(2,1)S(1)}, u32[]{:S(2)}, u32[]{:S(2)}) async-start(bf16[32,96,128]{2,1,0:T(8,128)(2,1)} %spread.1.refs_0_), calls=%async_computation.1 | async-start | bytes 1572864 | tf_op jit(solution)/shard_map/all_to_all | solution.py:46
  120.7 18.2 %collective-permute-start.9 = (bf16[64,128]{1,0:T(8,128)(2,1)}, bf16[64,128]{1,0:T(8,128)(2,1)S(1)}, u32[]{:S(2)}, u32[]{:S(2)}) collective-permute-start(bf16[64,128]{1,0:T(8,128)(2,1)} %sum_pieces.1), channel_id=1, source_target_pairs={{0,24},{4,28},{8,32},{12,36},{16,40},{20,44},{24,48},{28,52},{32,5... | collective-permute-start | bytes 49160 | tf_op jit(solution)/shard_map/ppermute | solution.py:42
  123.7 16.0 %collective-permute-start.8 = (bf16[64,128]{1,0:T(8,128)(2,1)}, bf16[64,128]{1,0:T(8,128)(2,1)S(1)}, u32[]{:S(2)}, u32[]{:S(2)}) collective-permute-start(bf16[64,128]{1,0:T(8,128)(2,1)} %sum_pieces.1), channel_id=1, source_target_pairs={{0,16},{4,20},{8,24},{12,28},{16,32},{20,36},{24,40},{28,44},{32,4... | collective-permute-start | bytes 49160 | tf_op jit(solution)/shard_map/ppermute | solution.py:42
  126.1 13.6 %collective-permute-start.7 = (bf16[64,128]{1,0:T(8,128)(2,1)}, bf16[64,128]{1,0:T(8,128)(2,1)S(1)}, u32[]{:S(2)}, u32[]{:S(2)}) collective-permute-start(bf16[64,128]{1,0:T(8,128)(2,1)} %sum_pieces.1), channel_id=1, source_target_pairs={{0,8},{4,12},{8,16},{12,20},{16,24},{20,28},{24,32},{28,36},{32,40... | collective-permute-start | bytes 49160 | tf_op jit(solution)/shard_map/ppermute | solution.py:42
  140.5 7.1 %collective-permute-start.10 = (bf16[4,64,128]{2,1,0:T(8,128)(2,1)S(1)}, bf16[4,64,128]{2,1,0:T(8,128)(2,1)S(1)}, u32[]{:S(2)}, u32[]{:S(2)}) collective-permute-start(bf16[4,64,128]{2,1,0:T(8,128)(2,1)S(1)} %pad_maximum_fusion.1), channel_id=1, source_target_pairs={{0,32},{4,36},{8,40},{12,44},{16,48},{20,52},{24,56},{28,60},{32,0... | collective-permute-start | bytes 196616 | tf_op jit(solution)/shard_map/ppermute | solution.py:42
  147.6 6.0 %collective-permute-start.13 = (bf16[8,64,128]{2,1,0:T(8,128)(2,1)S(1)}, bf16[8,64,128]{2,1,0:T(8,128)(2,1)S(1)}, u32[]{:S(2)}, u32[]{:S(2)}) collective-permute-start(bf16[8,64,128]{2,1,0:T(8,128)(2,1)S(1)} %constant_dynamic-update-slice_fusion), channel_id=1, source_target_pairs={{0,192},{4,196},{8,200},{12,204},{16,208},{20,212},{24,216},{28,22... | collective-permute-start | bytes 393224 | tf_op jit(solution)/shard_map/ppermute | solution.py:42
  150.3 5.4 %collective-permute-start.12 = (bf16[8,64,128]{2,1,0:T(8,128)(2,1)S(1)}, bf16[8,64,128]{2,1,0:T(8,128)(2,1)S(1)}, u32[]{:S(2)}, u32[]{:S(2)}) collective-permute-start(bf16[8,64,128]{2,1,0:T(8,128)(2,1)S(1)} %constant_dynamic-update-slice_fusion), channel_id=1, source_target_pairs={{0,128},{4,132},{8,136},{12,140},{16,144},{20,148},{24,152},{28,15... | collective-permute-start | bytes 393224 | tf_op jit(solution)/shard_map/ppermute | solution.py:42
  150.8 6.2 %collective-permute-start.11 = (bf16[8,64,128]{2,1,0:T(8,128)(2,1)S(1)}, bf16[8,64,128]{2,1,0:T(8,128)(2,1)S(1)}, u32[]{:S(2)}, u32[]{:S(2)}) collective-permute-start(bf16[8,64,128]{2,1,0:T(8,128)(2,1)S(1)} %constant_dynamic-update-slice_fusion), channel_id=1, source_target_pairs={{0,64},{4,68},{8,72},{12,76},{16,80},{20,84},{24,88},{28,92},{32,9... | collective-permute-start | bytes 393224 | tf_op jit(solution)/shard_map/ppermute | solution.py:42
  157.1 6.5 %copy-start.3 = (bf16[4,8,64,128]{3,2,1,0:T(8,128)(2,1)}, bf16[4,8,64,128]{3,2,1,0:T(8,128)(2,1)S(1)}, u32[]{:S(2)}) copy-start(bf16[4,8,64,128]{3,2,1,0:T(8,128)(2,1)S(1)} %pad_maximum_fusion.mine_ref) | copy-start | bytes 1572868
  157.1 6.4 %collective-permute-start.14 = (bf16[4,8,64,128]{3,2,1,0:T(8,128)(2,1)S(1)}, bf16[4,8,64,128]{3,2,1,0:T(8,128)(2,1)S(1)}, u32[]{:S(2)}, u32[]{:S(2)}) collective-permute-start(bf16[4,8,64,128]{3,2,1,0:T(8,128)(2,1)S(1)} %pad_maximum_fusion.mine_ref), channel_id=1, source_target_pairs={{0,4},{4,0},{8,12},{12,8},{16,20},{20,16},{24,28},{28,24},{32,36},... | collective-permute-start | bytes 1572872 | tf_op jit(solution)/shard_map/ppermute | solution.py:34
  162.7 0.9 copy-start
  163.6 0.8 copy-start.5

commit v4 on v3

--- a/solution.py
+++ b/solution.py
@@ -172,6 +172,7 @@
             lane < 64, full[0:64], jnp.where(lane < 128, full[64:128], full[128:192])
         )
 
+    empty = jnp.zeros((HD, HD), BF)
     dqs, dks, dvs = [], [], []
     for i in range(GROUP):
         at = pl.multiple_of((step * GROUP + i) * 16, 16)
@@ -179,9 +180,16 @@
         key = jnp.concatenate([k_ref[span, :], kvirt_ref[pl.ds(at, 16), :]], axis=0)
         value = jnp.concatenate([v_ref[span, :], vvirt_ref[pl.ds(at, 16), :]], axis=0)
         query = q_ref[span, :]
-        grad = grad_ref[span, :]
+        first, second, third = grad_ref[0, span, :], grad_ref[1, span, :], grad_ref[2, span, :]
         query_blocks = jnp.concatenate([query, query, query], axis=0) * blocks
-        grad_blocks = jnp.concatenate([grad, grad, grad], axis=0) * blocks
+        grad_blocks = jnp.concatenate(
+            [
+                jnp.concatenate([first, empty, empty], axis=1),
+                jnp.concatenate([empty, second, empty], axis=1),
+                jnp.concatenate([empty, empty, third], axis=1),
+            ],
+            axis=0,
+        )
         scores = jnp.where(valid, nt(key, query_blocks) * 0.125, -1e30)
         top = jnp.max(scores, axis=0, keepdims=True)
         powers = jnp.exp(scores - top)
@@ -191,7 +199,10 @@
         prob_grads = nt(value, grad_blocks)
         inner = jnp.sum(prob_grads * probs, axis=0, keepdims=True)
         score_low = (probs * (prob_grads - inner) * 0.125).astype(BF)
-        ctx_ref[span, :] = heads_of(tn(low, value)).astype(BF)
+        mixed = tn(low, value)
+        for h in range(3):
+            part = slice(HD * h, HD * h + HD)
+            ctx_ref[h, span, :] = mixed[part, part].astype(BF)
         dq = heads_of(tn(score_low, key)).astype(BF)
         dv = nn(low, grad_blocks).astype(BF)
         dk = nn(score_low, query_blocks).astype(BF)
@@ -237,7 +248,7 @@
     fixed2 = lambda i: (0, 0)
     fixed3 = lambda i: (0, 0, 0)
     out_shape = (
-        jax.ShapeDtypeStruct((2048, 192), BF),
+        jax.ShapeDtypeStruct((3, 2048, HD), BF),
         jax.ShapeDtypeStruct((2048, 128), F32),
         jax.ShapeDtypeStruct((2048, 128), BF),
         jax.ShapeDtypeStruct((64, 192), F32),
@@ -248,6 +259,7 @@
     small = pl.BlockSpec((64, 192), fixed2)
     weight = pl.BlockSpec((192, 768), fixed2)
     head = pl.BlockSpec((rows, 192), lambda i: (i, 0))
+    by_head = pl.BlockSpec((3, rows, HD), lambda i: (0, i, 0))
     half = pl.BlockSpec((2048, 128), fixed2)
     return pl.pallas_call(
         attend_kernel,
@@ -256,14 +268,14 @@
         in_specs=[
             pl.BlockSpec(memory_space=pltpu.SMEM),
             pl.BlockSpec((rows, 768), lambda i: (i, 0)),
-            head, head, head, head,
+            head, head, head, by_head,
             pl.BlockSpec((64, 768), fixed2),
             weight, weight,
             pl.BlockSpec((4, 192, 192), fixed3),
             pl.BlockSpec((4, 192, 192), fixed3),
         ],
         out_specs=(
-            head, half, half,
+            by_head, half, half,
             small, small, small, small,
         ),
         scratch_shapes=[
@@ -410,7 +422,7 @@
     keys = jnp.where(here, (all_slots >> 6) * 32 + (all_slots & 31), -1).T
     mix = make_mixing(keys)
 
-    heads = grad_out.reshape(32, 3, 64, 64).transpose(0, 2, 1, 3).reshape(2048, 192)
+    heads = grad_out.transpose(1, 0, 2).reshape(3, 2048, HD)
     wk4 = w_key.reshape(192, 4, 192).transpose(1, 0, 2)
     wv4 = w_value.reshape(192, 4, 192).transpose(1, 0, 2)
 
@@ -426,7 +438,7 @@
     ctx, keep, give, vg0, vg1, vg2, vg3 = attend(
         place, flat, q, k, v, heads, virtual, w_key, w_value, wk4, wv4
     )
-    context = ctx.reshape(32, 64, 3, 64).transpose(0, 2, 1, 3).reshape(32, 3, 4096)
+    context = ctx.reshape(3, 32, 4096).transpose(1, 0, 2)
 
     around = lambda x, d: lax.ppermute(x, "mp", [(i, (i + d) % 4) for i in range(4)])
     moved = [around(vg, d + 1) for d, vg in enumerate((vg1, vg2, vg3))]

time: 173 us -> 169 us (0.977)
  the two profiles are of different devices: /device:TPU:1 before, /device:TPU:8 now
where the time goes in v4:
time: 169 us; the launch traced here: 166 us
  Pallas kernels  48 us (28%)
  waiting for transfers between devices  45.3 us (27%)
  starting transfers between devices  41.4 us (24%)
  local copies, waits for them, and re-layouts  12.9 us (8%)
  blocking collectives  12.2 us (7%)
  other arithmetic  5.36 us (3%)
    ppermute x7, waiting for transfers between devices, along(): return lax.ppermute(x, 'nodes', pairs)  24.9 us
    all_to_all x3, starting transfers between devices, chip_exchange(): lax.all_to_all(x, 'nodes', split_axis=0, concat_axis=0, tiled=True, axis_...  21.9 us
    pallas_call x1, Pallas kernels, attend(): pl.pallas_call(attend_kernel, out_shape=out_shape, grid=(steps,), in_spec...  19.1 us
    all_to_all x3, waiting for transfers between devices, chip_exchange(): lax.all_to_all(x, 'nodes', split_axis=0, concat_axis=0, tiled=True, axis_...  14.3 us
    ppermute x7, starting transfers between devices, along(): return lax.ppermute(x, 'nodes', pairs)  14.3 us
    all_gather x1, blocking collectives, layer(): virtual = lax.all_gather(local, 'mp', axis=1, tiled=True)  12.2 us
    pallas_call x1, Pallas kernels, scatter_rows(): pl.pallas_call(scatter_kernel, out_shape=(jax.ShapeDtypeStruct((192, 2048...  7.22 us
    pallas_call x1, Pallas kernels, gather_rows(): pl.pallas_call(gather_kernel, out_shape=jax.ShapeDtypeStruct((CHIPS, 96,...  6.7 us
  transfers between devices with their start and end apart: 18, of which 13 were waited for; matrix products, arithmetic and copies ran while one was open for 6% of the time, Pallas kernels for 8%

profile of v4, /device:TPU:8, one launch (start us, length us, event | category | flops | bytes accessed | tf_op | source)
XLA Modules:
  0.0 166.1 jit_solution(10502848224011983692)
XLA Ops:
  0.6 0.8 copy.26
  1.4 0.1 rev.3
  1.6 0.7 reshape.49.index_ref
  2.3 6.7 %gather_rows.1 = bf16[32,96,128]{2,1,0:T(8,128)(2,1)} custom-call(s32[8,1,256]{2,1,0:T(1,128)} %reshape.49.index_ref, bf16[192,2048]{1,0:T(8,128)(2,1)} %table_ref.1), custom_call_target="tpu_custom_call" | custom-call | tf_op jit(solution)/shard_map/gather_rows/pallas_call | solution.py:68
  9.0 11.4 %all-to-all-start = ((bf16[32,96,128]{2,1,0:T(8,128)(2,1)}), bf16[32,96,128]{2,1,0:T(8,128)(2,1)S(1)}, u32[]{:S(2)}, u32[]{:S(2)}) async-start(bf16[32,96,128]{2,1,0:T(8,128)(2,1)} %gather_rows.1), calls=%async_computation | async-start | bytes 1572864 | tf_op jit(solution)/shard_map/all_to_all | solution.py:46
  20.4 0.1 copy.29
  20.5 0.1 copy.28
  20.6 0.1 lt.22
  20.7 0.1 collective-permute-start
  20.8 0.4 reshape.51
  21.2 0.4 reshape.52
  21.6 1.0 copy_bitcast_fusion
  22.6 2.6 %reshape.47.refs_3_.grad_ref = bf16[3,2048,64]{2,1,0:T(8,128)(2,1)} reshape(bf16[3,32,4096]{2,1,0:T(8,128)(2,1)S(1)} %bitcast.40) | data formatting | bytes 1572864 | tf_op jit(solution)/shard_map/reshape | solution.py:425
  25.1 6.0 %project.1 = (bf16[2048,192]{1,0:T(8,128)(2,1)}, bf16[2048,192]{1,0:T(8,128)(2,1)}, bf16[2048,192]{1,0:T(8,128)(2,1)}) custom-call(bf16[2048,768]{1,0:T(8,128)(2,1)} %bitcast.37, bf16[192,768]{1,0:T(8,128)(2,1)} %wq_ref.1, bf16[192,768]{1,0:T(8,128)(2,1)} %wk_ref.3, bf16[192,768]{1,0:T(8,128)(2,1)} %wv_ref.3), custom_call_target="tpu_custom_call" | custom-call | tf_op jit(solution)/shard_map/project/pallas_call | solution.py:134
  31.1 0.7 select_bitcast_fusion.1.key_ref
  31.8 2.3 %make_mixing.1.mix_ref = bf16[1024,128]{1,0:T(8,128)(2,1)} custom-call(s32[32,128]{1,0:T(8,128)} %select_bitcast_fusion.1.key_ref), custom_call_target="tpu_custom_call" | custom-call | tf_op jit(solution)/shard_map/make_mixing/pallas_call | solution.py:93
  34.1 9.7 %all-to-all-done.rows_ref = bf16[32,96,128]{2,1,0:T(8,128)(2,1)S(1)} async-done(((bf16[32,96,128]{2,1,0:T(8,128)(2,1)}), bf16[32,96,128]{2,1,0:T(8,128)(2,1)S(1)}, u32[]{:S(2)}, u32[]{:S(2)}) %all-to-all-start) | async-done | bytes 786464 | tf_op jit(solution)/shard_map/all_to_all | solution.py:46
  43.8 0.9 copy-done
  44.7 2.3 %mix_rows.1 = (f32[64,192]{1,0:T(8,128)}, f32[64,192]{1,0:T(8,128)}) custom-call(bf16[32,96,128]{2,1,0:T(8,128)(2,1)} %copy-done, bf16[1024,128]{1,0:T(8,128)(2,1)} %make_mixing.1.mix_ref, bf16[2048,192]{1,0:T(8,128)(2,1)} %get-tuple-element.21.refs_0_.q_ref, bf16[2048,192]{1,0:T(8,128)(2,1)} %get-tuple-element.22.refs_1_.k_ref, ...), custom_call_target="tpu_custom_call" | custom-call | tf_op jit(solution)/shard_map/mix_rows/pallas_call | solution.py:115
  47.0 0.6 pad_add_fusion.1.place_ref
  47.6 0.9 collective-permute-done.1
  48.4 0.9 fusion
  49.4 12.2 %all-gather = bf16[4,192,64]{1,2,0:T(8,128)(2,1)S(1)} all-gather(bf16[1,192,64]{1,2,0:T(8,128)(2,1)S(1)} %fusion), channel_id=1, replica_groups=mesh['nodes'=64,'mp'=4] {'mp'}, dimensions={0}, use_global_device_ids=true | all-gather | bytes 122880 | tf_op jit(solution)/shard_map/all_gather | solution.py:436
  61.6 0.1 copy.32
  61.7 0.8 reshape.56
  62.5 19.1 %attend.1 = (bf16[3,2048,64]{2,1,0:T(8,128)(2,1)}, f32[2048,128]{1,0:T(8,128)}, bf16[2048,128]{1,0:T(8,128)(2,1)}, f32[64,192]{1,0:T(8,128)}, bf16[64,192]{1,0:T...) custom-call(s32[4]{0:T(128)} %pad_add_fusion.1.place_ref, bf16[2048,768]{1,0:T(8,128)(2,1)} %bitcast.38, ...), custom_call_target="tpu_custom_call" | custom-call | tf_op jit(solution)/shard_map/attend/pallas_call | solution.py:264
  81.6 0.1 collective-permute-start.6
  81.7 2.1 %collective-permute-done.6 = bf16[2048,128]{1,0:T(8,128)(2,1)S(1)} collective-permute-done((bf16[2048,128]{1,0:T(8,128)(2,1)}, bf16[2048,128]{1,0:T(8,128)(2,1)S(1)}, u32[]{:S(2)}, u32[]{:S(2)}) %collective-permute-start.6) | collective-permute-done | bytes 524320 | tf_op jit(solution)/shard_map/ppermute | solution.py:34
  83.8 2.2 %add_convert_fusion = bf16[2048,128]{1,0:T(8,128)(2,1)} fusion(f32[2048,128]{1,0:T(8,128)} %get-tuple-element.31, bf16[2048,128]{1,0:T(8,128)(2,1)S(1)} %collective-permute-done.6), kind=kLoop, calls=%fused_computation | loop fusion | flops 786432 | bytes 2097152 | tf_op jit(solution)/shard_map/convert_element_type | solution.py:445
  86.1 4.8 %all-to-all-start.2 = ((bf16[32,64,128]{2,1,0:T(8,128)(2,1)}), bf16[32,64,128]{2,1,0:T(8,128)(2,1)S(1)}, u32[]{:S(2)}, u32[]{:S(2)}) async-start(bf16[32,64,128]{2,1,0:T(8,128)(2,1)} %bitcast.16), calls=%async_computation.2 | async-start | bytes 1048576 | tf_op jit(solution)/shard_map/all_to_all | solution.py:46
  90.8 0.2 collective-permute-start.2
  91.1 2.7 %collective-permute-start.3 = (bf16[64,192]{1,0:T(8,128)(2,1)S(1)}, bf16[64,192]{1,0:T(8,128)(2,1)S(1)}, u32[]{:S(2)}, u32[]{:S(2)}) collective-permute-start(bf16[64,192]{1,0:T(8,128)(2,1)S(1)} %copy-done.15), channel_id=1, source_target_pairs={{0,2},{1,3},{2,0},{3,1},{4,6},{5,7},{6,4},{7,5},{8,10},{9,11},{10,... | collective-permute-start | bytes 73736 | tf_op jit(solution)/shard_map/ppermute | solution.py:443
  93.7 1.9 %collective-permute-start.4 = (bf16[64,192]{1,0:T(8,128)(2,1)S(1)}, bf16[64,192]{1,0:T(8,128)(2,1)S(1)}, u32[]{:S(2)}, u32[]{:S(2)}) collective-permute-start(bf16[64,192]{1,0:T(8,128)(2,1)S(1)} %copy-done.14), channel_id=1, source_target_pairs={{0,3},{1,0},{2,1},{3,2},{4,7},{5,4},{6,5},{7,6},{8,11},{9,8},{10,9... | collective-permute-start | bytes 73736 | tf_op jit(solution)/shard_map/ppermute | solution.py:443
  95.6 1.0 collective-permute-done.3
  96.6 1.0 collective-permute-done.4
  97.7 0.1 add_divide_fusion.own_ref
  97.8 0.1 collective-permute-start.5
  97.9 2.0 %reshape.53.refs_1_ = bf16[3,32,4096]{2,1,0:T(8,128)(2,1)} reshape(bf16[3,2048,64]{2,1,0:T(8,128)(2,1)S(1)} %copy-done.6) | data formatting | bytes 1572864 | tf_op jit(solution)/shard_map/reshape | solution.py:441
  99.9 0.6 copy-done.11
  100.6 2.7 %spread.1.refs_0_ = bf16[32,96,128]{2,1,0:T(8,128)(2,1)} custom-call(f32[64,192]{1,0:T(8,128)} %copy-done.9, f32[64,192]{1,0:T(8,128)} %copy-done.11, bf16[1024,128]{1,0:T(8,128)(2,1)} %make_mixing.1.mix_ref), custom_call_target="tpu_custom_call" | custom-call | tf_op jit(solution)/shard_map/spread/pallas_call | solution.py:316
  103.2 4.6 %all-to-all-done.2.pieces_ref = bf16[32,64,128]{2,1,0:T(8,128)(2,1)S(1)} async-done(((bf16[32,64,128]{2,1,0:T(8,128)(2,1)}), bf16[32,64,128]{2,1,0:T(8,128)(2,1)S(1)}, u32[]{:S(2)}, u32[]{:S(2)}) %all-to-all-start.2) | async-done | bytes 524320 | tf_op jit(solution)/shard_map/all_to_all | solution.py:46
  107.9 5.7 %all-to-all-start.1 = ((bf16[32,96,128]{2,1,0:T(8,128)(2,1)}), bf16[32,96,128]{2,1,0:T(8,128)(2,1)S(1)}, u32[]{:S(2)}, u32[]{:S(2)}) async-start(bf16[32,96,128]{2,1,0:T(8,128)(2,1)} %spread.1.refs_0_), calls=%async_computation.1 | async-start | bytes 1572864 | tf_op jit(solution)/shard_map/all_to_all | solution.py:46
  113.6 1.7 %sum_pieces.1 = bf16[64,128]{1,0:T(8,128)(2,1)} custom-call(bf16[32,64,128]{2,1,0:T(8,128)(2,1)} %copy-done.4, bf16[32,96,128]{2,1,0:T(8,128)(2,1)} %spread.1.refs_0_, bf16[3,32,4096]{2,1,0:T(8,128)(2,1)} %reshape.53.refs_1_), custom_call_target="tpu_custom_call" | custom-call | tf_op jit(solution)/shard_map/sum_pieces/pallas_call | solution.py:333
  115.4 3.6 %collective-permute-start.9 = (bf16[64,128]{1,0:T(8,128)(2,1)}, bf16[64,128]{1,0:T(8,128)(2,1)S(1)}, u32[]{:S(2)}, u32[]{:S(2)}) collective-permute-start(bf16[64,128]{1,0:T(8,128)(2,1)} %sum_pieces.1), channel_id=1, source_target_pairs={{0,24},{4,28},{8,32},{12,36},{16,40},{20,44},{24,48},{28,52},{32,5... | collective-permute-start | bytes 49160 | tf_op jit(solution)/shard_map/ppermute | solution.py:42
  118.9 2.7 %collective-permute-start.8 = (bf16[64,128]{1,0:T(8,128)(2,1)}, bf16[64,128]{1,0:T(8,128)(2,1)S(1)}, u32[]{:S(2)}, u32[]{:S(2)}) collective-permute-start(bf16[64,128]{1,0:T(8,128)(2,1)} %sum_pieces.1), channel_id=1, source_target_pairs={{0,16},{4,20},{8,24},{12,28},{16,32},{20,36},{24,40},{28,44},{32,4... | collective-permute-start | bytes 49160 | tf_op jit(solution)/shard_map/ppermute | solution.py:42
  121.6 0.6 collective-permute-start.7
  122.2 0.8 constant_dynamic-update-slice_fusion.4
  122.9 12.9 %collective-permute-done.9 = bf16[64,128]{1,0:T(8,128)(2,1)S(1)} collective-permute-done((bf16[64,128]{1,0:T(8,128)(2,1)}, bf16[64,128]{1,0:T(8,128)(2,1)S(1)}, u32[]{:S(2)}, u32[]{:S(2)}) %collective-permute-start.9) | collective-permute-done | bytes 16416 | tf_op jit(solution)/shard_map/ppermute | solution.py:42
  135.8 0.3 collective-permute-done.8
  136.1 0.7 pad_maximum_fusion.1
  136.9 3.1 %collective-permute-start.10 = (bf16[4,64,128]{2,1,0:T(8,128)(2,1)S(1)}, bf16[4,64,128]{2,1,0:T(8,128)(2,1)S(1)}, u32[]{:S(2)}, u32[]{:S(2)}) collective-permute-start(bf16[4,64,128]{2,1,0:T(8,128)(2,1)S(1)} %pad_maximum_fusion.1), channel_id=1, source_target_pairs={{0,32},{4,36},{8,40},{12,44},{16,48},{20,52},{24,56},{28,60},{32,0... | collective-permute-start | bytes 196616 | tf_op jit(solution)/shard_map/ppermute | solution.py:42
  139.9 5.5 %collective-permute-done.10 = bf16[4,64,128]{2,1,0:T(8,128)(2,1)S(1)} collective-permute-done((bf16[4,64,128]{2,1,0:T(8,128)(2,1)S(1)}, bf16[4,64,128]{2,1,0:T(8,128)(2,1)S(1)}, u32[]{:S(2)}, u32[]{:S(2)}) %collective-permute-start.10) | collective-permute-done | bytes 65568 | tf_op jit(solution)/shard_map/ppermute | solution.py:42
  145.4 2.7 %collective-permute-start.13 = (bf16[8,64,128]{2,1,0:T(8,128)(2,1)S(1)}, bf16[8,64,128]{2,1,0:T(8,128)(2,1)S(1)}, u32[]{:S(2)}, u32[]{:S(2)}) collective-permute-start(bf16[8,64,128]{2,1,0:T(8,128)(2,1)S(1)} %constant_dynamic-update-slice_fusion), channel_id=1, source_target_pairs={{0,192},{4,196},{8,200},{12,204},{16,208},{20,212},{24,216},{28,22... | collective-permute-start | bytes 393224 | tf_op jit(solution)/shard_map/ppermute | solution.py:42
  148.1 0.8 collective-permute-start.12
  148.9 0.9 collective-permute-start.11
  149.8 2.3 %collective-permute-done.13 = bf16[8,64,128]{2,1,0:T(8,128)(2,1)S(1)} collective-permute-done((bf16[8,64,128]{2,1,0:T(8,128)(2,1)S(1)}, bf16[8,64,128]{2,1,0:T(8,128)(2,1)S(1)}, u32[]{:S(2)}, u32[]{:S(2)}) %collective-permute-start.13) | collective-permute-done | bytes 131104 | tf_op jit(solution)/shard_map/ppermute | solution.py:42
  152.1 2.6 %collective-permute-done.12 = bf16[8,64,128]{2,1,0:T(8,128)(2,1)S(1)} collective-permute-done((bf16[8,64,128]{2,1,0:T(8,128)(2,1)S(1)}, bf16[8,64,128]{2,1,0:T(8,128)(2,1)S(1)}, u32[]{:S(2)}, u32[]{:S(2)}) %collective-permute-start.12) | collective-permute-done | bytes 131104 | tf_op jit(solution)/shard_map/ppermute | solution.py:42
  154.7 1.3 collective-permute-done.11
  156.0 0.1 pad_maximum_fusion.mine_ref
  156.1 0.1 collective-permute-start.14
  156.2 0.7 reshape_reshape.3.index_ref
  156.9 1.2 collective-permute-done.14.theirs_ref
  158.1 0.8 copy-done.8
  158.9 7.2 %scatter_rows.1 = (f32[192,2048]{1,0:T(8,128)}, f32[192,768]{1,0:T(8,128)}, f32[192,768]{1,0:T(8,128)}, f32[192,768]{1,0:T(8,128)}) custom-call(s32[4]{0:T(128)} %pad_add_fusion.1.place_ref, s32[1,2048]{1,0:T(1,128)} %reshape_reshape.3.index_ref, bf16[32,96,128]{2,1,0:T(8,128)(2,1)} %copy-done.1, bf16[4,8,64,128]{3,2,1,0:T(8,128)(2,1)} %copy-done.5, ...), custom_call_target="tpu_custom_call" | custom-call | tf_op jit(solution)/shard_map/scatter_rows/pallas_call | solution.py:386
  (45 shorter events, 0.2 us)
Async XLA Ops:
  2.3 18.2 %copy-start.12 = (s32[32,2,32]{2,1,0:T(2,128)S(1)}, s32[32,2,32]{2,1,0:T(2,128)}, u32[]{:S(2)}) copy-start(s32[32,2,32]{2,1,0:T(2,128)} %param.16) | copy-start | bytes 24580
  2.3 18.2 %copy-start.13 = (s32[32,2]{0,1:T(2,128)S(1)}, s32[32,2]{0,1:T(2,128)}, u32[]{:S(2)}) copy-start(s32[32,2]{0,1:T(2,128)} %param.17) | copy-start | bytes 772
  2.3 18.6 %copy-start.2 = (bf16[192,768]{1,0:T(8,128)(2,1)S(1)}, bf16[192,768]{1,0:T(8,128)(2,1)}, u32[]{:S(2)}) copy-start(bf16[192,768]{1,0:T(8,128)(2,1)} %wk_ref.3) | copy-start | bytes 884740
  9.0 12.2 %copy-start.3 = (bf16[192,768]{1,0:T(8,128)(2,1)S(1)}, bf16[192,768]{1,0:T(8,128)(2,1)}, u32[]{:S(2)}) copy-start(bf16[192,768]{1,0:T(8,128)(2,1)} %wv_ref.3) | copy-start | bytes 884740
  9.0 34.8 %all-to-all-start = ((bf16[32,96,128]{2,1,0:T(8,128)(2,1)}), bf16[32,96,128]{2,1,0:T(8,128)(2,1)S(1)}, u32[]{:S(2)}, u32[]{:S(2)}) async-start(bf16[32,96,128]{2,1,0:T(8,128)(2,1)} %gather_rows.1), calls=%async_computation | async-start | bytes 1572864 | tf_op jit(solution)/shard_map/all_to_all | solution.py:46
  20.4 2.1 %copy-start.7 = (bf16[32,3,4096]{2,0,1:T(8,128)(2,1)S(1)}, bf16[32,3,4096]{2,0,1:T(8,128)(2,1)}, u32[]{:S(2)}) copy-start(bf16[32,3,4096]{2,0,1:T(8,128)(2,1)} %param.13) | copy-start | bytes 2359300
  20.7 10.4 %collective-permute-start = (s32[64,32]{0,1:T(8,128)S(1)}, s32[64,32]{0,1:T(8,128)S(1)}, u32[]{:S(2)}, u32[]{:S(2)}) collective-permute-start(s32[64,32]{0,1:T(8,128)S(1)} %fusion.1), channel_id=1, source_target_pairs={{0,4},{4,0},{8,12},{12,8},{16,20},{20,16},{24,28},{28,24},{32,36},... | collective-permute-start | bytes 24584 | tf_op jit(solution)/shard_map/ppermute | solution.py:34
  43.8 0.9 copy-start
  47.0 1.5 collective-permute-start.1
  81.6 2.2 %collective-permute-start.6 = (bf16[2048,128]{1,0:T(8,128)(2,1)}, bf16[2048,128]{1,0:T(8,128)(2,1)S(1)}, u32[]{:S(2)}, u32[]{:S(2)}) collective-permute-start(bf16[2048,128]{1,0:T(8,128)(2,1)} %get-tuple-element.32), channel_id=1, source_target_pairs={{0,4},{4,0},{8,12},{12,8},{16,20},{20,16},{24,28},{28,24},{32,36},... | collective-permute-start | bytes 1572872 | tf_op jit(solution)/shard_map/ppermute | solution.py:34
  83.8 7.0 %copy-start.16 = (bf16[64,192]{1,0:T(8,128)(2,1)S(1)}, bf16[64,192]{1,0:T(8,128)(2,1)}, u32[]{:S(2)}) copy-start(bf16[64,192]{1,0:T(8,128)(2,1)} %get-tuple-element.28) | copy-start | bytes 73732
  83.8 7.3 %copy-start.15 = (bf16[64,192]{1,0:T(8,128)(2,1)S(1)}, bf16[64,192]{1,0:T(8,128)(2,1)}, u32[]{:S(2)}) copy-start(bf16[64,192]{1,0:T(8,128)(2,1)} %get-tuple-element.29) | copy-start | bytes 73732
  83.8 9.9 %copy-start.14 = (bf16[64,192]{1,0:T(8,128)(2,1)S(1)}, bf16[64,192]{1,0:T(8,128)(2,1)}, u32[]{:S(2)}) copy-start(bf16[64,192]{1,0:T(8,128)(2,1)} %get-tuple-element.30) | copy-start | bytes 73732
  83.8 13.8 %copy-start.10 = (f32[64,192]{1,0:T(8,128)S(1)}, f32[64,192]{1,0:T(8,128)}, u32[]{:S(2)}) copy-start(f32[64,192]{1,0:T(8,128)} %get-tuple-element.27) | copy-start | bytes 147460
  83.8 14.0 %copy-start.6 = (bf16[3,2048,64]{2,1,0:T(8,128)(2,1)S(1)}, bf16[3,2048,64]{2,1,0:T(8,128)(2,1)}, u32[]{:S(2)}) copy-start(bf16[3,2048,64]{2,1,0:T(8,128)(2,1)} %get-tuple-element.26) | copy-start | bytes 2359300
  86.1 21.8 %all-to-all-start.2 = ((bf16[32,64,128]{2,1,0:T(8,128)(2,1)}), bf16[32,64,128]{2,1,0:T(8,128)(2,1)S(1)}, u32[]{:S(2)}, u32[]{:S(2)}) async-start(bf16[32,64,128]{2,1,0:T(8,128)(2,1)} %bitcast.16), calls=%async_computation.2 | async-start | bytes 1048576 | tf_op jit(solution)/shard_map/all_to_all | solution.py:46
  90.8 4.8 %collective-permute-start.2 = (bf16[64,192]{1,0:T(8,128)(2,1)S(1)}, bf16[64,192]{1,0:T(8,128)(2,1)S(1)}, u32[]{:S(2)}, u32[]{:S(2)}) collective-permute-start(bf16[64,192]{1,0:T(8,128)(2,1)S(1)} %copy-done.16), channel_id=1, source_target_pairs={{0,1},{1,2},{2,3},{3,0},{4,5},{5,6},{6,7},{7,4},{8,9},{9,10},{10,1... | collective-permute-start | bytes 73736 | tf_op jit(solution)/shard_map/ppermute | solution.py:443
  91.1 5.6 %collective-permute-start.3 = (bf16[64,192]{1,0:T(8,128)(2,1)S(1)}, bf16[64,192]{1,0:T(8,128)(2,1)S(1)}, u32[]{:S(2)}, u32[]{:S(2)}) collective-permute-start(bf16[64,192]{1,0:T(8,128)(2,1)S(1)} %copy-done.15), channel_id=1, source_target_pairs={{0,2},{1,3},{2,0},{3,1},{4,6},{5,7},{6,4},{7,5},{8,10},{9,11},{10,... | collective-permute-start | bytes 73736 | tf_op jit(solution)/shard_map/ppermute | solution.py:443
  93.7 3.9 %collective-permute-start.4 = (bf16[64,192]{1,0:T(8,128)(2,1)S(1)}, bf16[64,192]{1,0:T(8,128)(2,1)S(1)}, u32[]{:S(2)}, u32[]{:S(2)}) collective-permute-start(bf16[64,192]{1,0:T(8,128)(2,1)S(1)} %copy-done.14), channel_id=1, source_target_pairs={{0,3},{1,0},{2,1},{3,2},{4,7},{5,4},{6,5},{7,6},{8,11},{9,8},{10,9... | collective-permute-start | bytes 73736 | tf_op jit(solution)/shard_map/ppermute | solution.py:443
  97.7 2.2 %copy-start.9 = (f32[64,192]{1,0:T(8,128)}, f32[64,192]{1,0:T(8,128)S(1)}, u32[]{:S(2)}) copy-start(f32[64,192]{1,0:T(8,128)S(1)} %add_divide_fusion.own_ref) | copy-start | bytes 147460
  97.8 2.2 %collective-permute-start.5 = (f32[64,192]{1,0:T(8,128)S(1)}, f32[64,192]{1,0:T(8,128)S(1)}, u32[]{:S(2)}, u32[]{:S(2)}) collective-permute-start(f32[64,192]{1,0:T(8,128)S(1)} %add_divide_fusion.own_ref), channel_id=1, source_target_pairs={{0,4},{4,0},{8,12},{12,8},{16,20},{20,16},{24,28},{28,24},{32,36},... | collective-permute-start | bytes 147464 | tf_op jit(solution)/shard_map/ppermute | solution.py:34
  99.9 0.6 copy-start.11
  107.9 5.8 %copy-start.4 = (bf16[32,64,128]{2,1,0:T(8,128)(2,1)}, bf16[32,64,128]{2,1,0:T(8,128)(2,1)S(1)}, u32[]{:S(2)}) copy-start(bf16[32,64,128]{2,1,0:T(8,128)(2,1)S(1)} %all-to-all-done.2.pieces_ref) | copy-start | bytes 1572868
  107.9 49.0 %all-to-all-start.1 = ((bf16[32,96,128]{2,1,0:T(8,128)(2,1)}), bf16[32,96,128]{2,1,0:T(8,128)(2,1)S(1)}, u32[]{:S(2)}, u32[]{:S(2)}) async-start(bf16[32,96,128]{2,1,0:T(8,128)(2,1)} %spread.1.refs_0_), calls=%async_computation.1 | async-start | bytes 1572864 | tf_op jit(solution)/shard_map/all_to_all | solution.py:46
  115.4 20.5 %collective-permute-start.9 = (bf16[64,128]{1,0:T(8,128)(2,1)}, bf16[64,128]{1,0:T(8,128)(2,1)S(1)}, u32[]{:S(2)}, u32[]{:S(2)}) collective-permute-start(bf16[64,128]{1,0:T(8,128)(2,1)} %sum_pieces.1), channel_id=1, source_target_pairs={{0,24},{4,28},{8,32},{12,36},{16,40},{20,44},{24,48},{28,52},{32,5... | collective-permute-start | bytes 49160 | tf_op jit(solution)/shard_map/ppermute | solution.py:42
  118.9 17.2 %collective-permute-start.8 = (bf16[64,128]{1,0:T(8,128)(2,1)}, bf16[64,128]{1,0:T(8,128)(2,1)S(1)}, u32[]{:S(2)}, u32[]{:S(2)}) collective-permute-start(bf16[64,128]{1,0:T(8,128)(2,1)} %sum_pieces.1), channel_id=1, source_target_pairs={{0,16},{4,20},{8,24},{12,28},{16,32},{20,36},{24,40},{28,44},{32,4... | collective-permute-start | bytes 49160 | tf_op jit(solution)/shard_map/ppermute | solution.py:42
  121.6 14.5 %collective-permute-start.7 = (bf16[64,128]{1,0:T(8,128)(2,1)}, bf16[64,128]{1,0:T(8,128)(2,1)S(1)}, u32[]{:S(2)}, u32[]{:S(2)}) collective-permute-start(bf16[64,128]{1,0:T(8,128)(2,1)} %sum_pieces.1), channel_id=1, source_target_pairs={{0,8},{4,12},{8,16},{12,20},{16,24},{20,28},{24,32},{28,36},{32,40... | collective-permute-start | bytes 49160 | tf_op jit(solution)/shard_map/ppermute | solution.py:42
  136.9 8.5 %collective-permute-start.10 = (bf16[4,64,128]{2,1,0:T(8,128)(2,1)S(1)}, bf16[4,64,128]{2,1,0:T(8,128)(2,1)S(1)}, u32[]{:S(2)}, u32[]{:S(2)}) collective-permute-start(bf16[4,64,128]{2,1,0:T(8,128)(2,1)S(1)} %pad_maximum_fusion.1), channel_id=1, source_target_pairs={{0,32},{4,36},{8,40},{12,44},{16,48},{20,52},{24,56},{28,60},{32,0... | collective-permute-start | bytes 196616 | tf_op jit(solution)/shard_map/ppermute | solution.py:42
  145.4 6.6 %collective-permute-start.13 = (bf16[8,64,128]{2,1,0:T(8,128)(2,1)S(1)}, bf16[8,64,128]{2,1,0:T(8,128)(2,1)S(1)}, u32[]{:S(2)}, u32[]{:S(2)}) collective-permute-start(bf16[8,64,128]{2,1,0:T(8,128)(2,1)S(1)} %constant_dynamic-update-slice_fusion), channel_id=1, source_target_pairs={{0,192},{4,196},{8,200},{12,204},{16,208},{20,212},{24,216},{28,22... | collective-permute-start | bytes 393224 | tf_op jit(solution)/shard_map/ppermute | solution.py:42
  148.1 6.6 %collective-permute-start.12 = (bf16[8,64,128]{2,1,0:T(8,128)(2,1)S(1)}, bf16[8,64,128]{2,1,0:T(8,128)(2,1)S(1)}, u32[]{:S(2)}, u32[]{:S(2)}) collective-permute-start(bf16[8,64,128]{2,1,0:T(8,128)(2,1)S(1)} %constant_dynamic-update-slice_fusion), channel_id=1, source_target_pairs={{0,128},{4,132},{8,136},{12,140},{16,144},{20,148},{24,152},{28,15... | collective-permute-start | bytes 393224 | tf_op jit(solution)/shard_map/ppermute | solution.py:42
  148.9 7.1 %collective-permute-start.11 = (bf16[8,64,128]{2,1,0:T(8,128)(2,1)S(1)}, bf16[8,64,128]{2,1,0:T(8,128)(2,1)S(1)}, u32[]{:S(2)}, u32[]{:S(2)}) collective-permute-start(bf16[8,64,128]{2,1,0:T(8,128)(2,1)S(1)} %constant_dynamic-update-slice_fusion), channel_id=1, source_target_pairs={{0,64},{4,68},{8,72},{12,76},{16,80},{20,84},{24,88},{28,92},{32,9... | collective-permute-start | bytes 393224 | tf_op jit(solution)/shard_map/ppermute | solution.py:42
  156.1 2.0 %copy-start.5 = (bf16[4,8,64,128]{3,2,1,0:T(8,128)(2,1)}, bf16[4,8,64,128]{3,2,1,0:T(8,128)(2,1)S(1)}, u32[]{:S(2)}) copy-start(bf16[4,8,64,128]{3,2,1,0:T(8,128)(2,1)S(1)} %pad_maximum_fusion.mine_ref) | copy-start | bytes 1572868
  156.1 2.0 %collective-permute-start.14 = (bf16[4,8,64,128]{3,2,1,0:T(8,128)(2,1)S(1)}, bf16[4,8,64,128]{3,2,1,0:T(8,128)(2,1)S(1)}, u32[]{:S(2)}, u32[]{:S(2)}) collective-permute-start(bf16[4,8,64,128]{3,2,1,0:T(8,128)(2,1)S(1)} %pad_maximum_fusion.mine_ref), channel_id=1, source_target_pairs={{0,4},{4,0},{8,12},{12,8},{16,20},{20,16},{24,28},{28,24},{32,36},... | collective-permute-start | bytes 1572872 | tf_op jit(solution)/shard_map/ppermute | solution.py:34
  156.9 1.2 copy-start.1
  158.1 0.8 copy-start.8

commit v5 on v4

--- a/solution.py
+++ b/solution.py
@@ -28,6 +28,10 @@
 
 def tn(a, b):
     return lax.dot_general(a, b, (((0,), (0,)), ((), ())), preferred_element_type=F32)
+
+
+def near(x):
+    return pltpu.with_memory_space_constraint(x, pltpu.VMEM)
 
 
 def core_swap(x):
@@ -117,7 +121,7 @@
         out_shape=(part, part),
         in_specs=[whole, whole] + [pl.BlockSpec(memory_space=pl.ANY)] * len(after),
         name="mix_rows",
-    )(rows, mix, *after)
+    )(near(rows), mix, *after)
 
 
 def project_kernel(tok_ref, wq_ref, wk_ref, wv_ref, q_ref, k_ref, v_ref):
@@ -336,7 +340,7 @@
         in_specs=[pl.BlockSpec(memory_space=pltpu.VMEM)]
         + [pl.BlockSpec(memory_space=pl.ANY)] * len(after),
         name="sum_pieces",
-    )(pieces, *after)
+    )(near(pieces), *after)
 
 
 def assemble(place_ref, mine_ref, theirs_ref, out_refs):
@@ -382,7 +386,7 @@
 def scatter_rows(place, index, rows, mine, theirs):
     weight = jax.ShapeDtypeStruct((192, 768), F32)
     weight_block = pl.BlockSpec((192, 768), lambda i: (0, 0))
-    piece_block = pl.BlockSpec((4, 8, 64, 128), lambda i: (0, 0, 0, 0))
+    whole = pl.BlockSpec(memory_space=pltpu.VMEM)
     return pl.pallas_call(
         scatter_kernel,
         out_shape=(jax.ShapeDtypeStruct((192, 2048), F32), weight, weight, weight),
@@ -390,9 +394,9 @@
         in_specs=[
             pl.BlockSpec(memory_space=pltpu.SMEM),
             pl.BlockSpec((1, 2048), lambda i: (0, 0)),
-            pl.BlockSpec((CHIPS, 96, 128), lambda i: (0, 0, 0)),
-            piece_block,
-            piece_block,
+            whole,
+            whole,
+            whole,
         ],
         out_specs=(
             pl.BlockSpec((192, 256), lambda i: (0, i)), weight_block, weight_block, weight_block
@@ -400,7 +404,7 @@
         scratch_shapes=[pltpu.VMEM((192, 2048), BF)],
         compiler_params=pltpu.CompilerParams(vmem_limit_bytes=VMEM_LIMIT),
         name="scatter_rows",
-    )(place, index, rows, mine, theirs)
+    )(place, index, near(rows), near(mine), near(theirs))
 
 
 def layer(tokens, w_query, w_key, w_value, grad_out, owned_cls, send_rows, neigh_slot, neigh_count):
@@ -449,9 +453,9 @@
     outgoing = spread(shared, core_swap(shared), mix)
     total = sum_pieces(pieces, outgoing, context.transpose(1, 0, 2))
     arrived = chip_exchange(outgoing)
-    near = jnp.stack([total] + [along(total, 0, d) for d in range(1, 4)])
-    across = along(near, 0, 4)
-    row = jnp.concatenate([near, across], axis=0)
+    close = jnp.stack([total] + [along(total, 0, d) for d in range(1, 4)])
+    across = along(close, 0, 4)
+    row = jnp.concatenate([close, across], axis=0)
     mine = jnp.stack([row] + [along(row, d, 0) for d in range(1, 4)])
     theirs = core_swap(mine)
     grad_cls, grad_query, grad_key, grad_value = scatter_rows(

time: 169 us -> 167 us (0.988)
  Pallas kernels: 48 us -> 46 us
  local copies, waits for them, and re-layouts: 12.9 us -> 11.2 us
    unnamed x41 -> x31, local copies, waits for them, and re-layouts: 4.79 us -> 3.11 us
  transfers between devices with their start and end apart: 18 -> 18, of which waited for: 13 -> 13; matrix products, arithmetic and copies ran while one was open for 6% -> 6% of each run, Pallas kernels for 8% -> 7%
where the time goes in v5:
time: 167 us; the launch traced here: 163 us
  waiting for transfers between devices  46.4 us (28%)
  Pallas kernels  46 us (28%)
  starting transfers between devices  41.4 us (25%)
  blocking collectives  12.2 us (7%)
  local copies, waits for them, and re-layouts  11.2 us (7%)
  other arithmetic  5.44 us (3%)
    ppermute x7, waiting for transfers between devices, along(): return lax.ppermute(x, 'nodes', pairs)  25.9 us
    all_to_all x3, starting transfers between devices, chip_exchange(): lax.all_to_all(x, 'nodes', split_axis=0, concat_axis=0, tiled=True, axis_...  21.9 us
    pallas_call x1, Pallas kernels, attend(): pl.pallas_call(attend_kernel, out_shape=out_shape, grid=(steps,), in_spec...  19.1 us
    all_to_all x3, waiting for transfers between devices, chip_exchange(): lax.all_to_all(x, 'nodes', split_axis=0, concat_axis=0, tiled=True, axis_...  14.3 us
    ppermute x7, starting transfers between devices, along(): return lax.ppermute(x, 'nodes', pairs)  14.3 us
    all_gather x1, blocking collectives, layer(): virtual = lax.all_gather(local, 'mp', axis=1, tiled=True)  12.2 us
    pallas_call x1, Pallas kernels, gather_rows(): pl.pallas_call(gather_kernel, out_shape=jax.ShapeDtypeStruct((CHIPS, 96,...  6.7 us
    pallas_call x1, Pallas kernels, scatter_rows(): pl.pallas_call(scatter_kernel, out_shape=(jax.ShapeDtypeStruct((192, 2048...  6.47 us
  transfers between devices with their start and end apart: 18, of which 13 were waited for; matrix products, arithmetic and copies ran while one was open for 6% of the time, Pallas kernels for 7%

profile of v5, /device:TPU:8, one launch (start us, length us, event | category | flops | bytes accessed | tf_op | source)
XLA Modules:
  0.0 163.4 jit_solution(7033180046701195729)
XLA Ops:
  0.6 0.8 copy.26
  1.4 0.1 rev.3
  1.6 0.7 reshape.49.index_ref
  2.3 6.7 %gather_rows.1 = bf16[32,96,128]{2,1,0:T(8,128)(2,1)} custom-call(s32[8,1,256]{2,1,0:T(1,128)} %reshape.49.index_ref, bf16[192,2048]{1,0:T(8,128)(2,1)} %table_ref.1), custom_call_target="tpu_custom_call" | custom-call | tf_op jit(solution)/shard_map/gather_rows/pallas_call | solution.py:72
  9.0 11.4 %all-to-all-start = ((bf16[32,96,128]{2,1,0:T(8,128)(2,1)}), bf16[32,96,128]{2,1,0:T(8,128)(2,1)S(1)}, u32[]{:S(2)}, u32[]{:S(2)}) async-start(bf16[32,96,128]{2,1,0:T(8,128)(2,1)} %gather_rows.1), calls=%async_computation | async-start | bytes 1572864 | tf_op jit(solution)/shard_map/all_to_all | solution.py:50
  20.4 0.0 copy-start.3
  20.4 0.1 copy.29
  20.5 0.1 copy.28
  20.6 0.1 lt.22
  20.7 0.1 collective-permute-start
  20.8 0.4 reshape.51
  21.2 0.4 reshape.52
  21.6 1.0 copy_bitcast_fusion
  22.6 2.6 %reshape.47.refs_3_.grad_ref = bf16[3,2048,64]{2,1,0:T(8,128)(2,1)} reshape(bf16[3,32,4096]{2,1,0:T(8,128)(2,1)S(1)} %bitcast.40) | data formatting | bytes 1572864 | tf_op jit(solution)/shard_map/reshape | solution.py:429
  25.1 6.0 %project.1 = (bf16[2048,192]{1,0:T(8,128)(2,1)}, bf16[2048,192]{1,0:T(8,128)(2,1)}, bf16[2048,192]{1,0:T(8,128)(2,1)}) custom-call(bf16[2048,768]{1,0:T(8,128)(2,1)} %bitcast.37, bf16[192,768]{1,0:T(8,128)(2,1)} %wq_ref.1, bf16[192,768]{1,0:T(8,128)(2,1)} %wk_ref.3, bf16[192,768]{1,0:T(8,128)(2,1)} %wv_ref.3), custom_call_target="tpu_custom_call" | custom-call | tf_op jit(solution)/shard_map/project/pallas_call | solution.py:138
  31.1 0.7 select_bitcast_fusion.1.key_ref
  31.8 2.3 %make_mixing.1.mix_ref = bf16[1024,128]{1,0:T(8,128)(2,1)} custom-call(s32[32,128]{1,0:T(8,128)} %select_bitcast_fusion.1.key_ref), custom_call_target="tpu_custom_call" | custom-call | tf_op jit(solution)/shard_map/make_mixing/pallas_call | solution.py:97
  34.1 9.7 %all-to-all-done.rows_ref = bf16[32,96,128]{2,1,0:T(8,128)(2,1)S(1)} async-done(((bf16[32,96,128]{2,1,0:T(8,128)(2,1)}), bf16[32,96,128]{2,1,0:T(8,128)(2,1)S(1)}, u32[]{:S(2)}, u32[]{:S(2)}) %all-to-all-start) | async-done | bytes 786464 | tf_op jit(solution)/shard_map/all_to_all | solution.py:50
  43.8 2.1 %mix_rows.1 = (f32[64,192]{1,0:T(8,128)}, f32[64,192]{1,0:T(8,128)}) custom-call(bf16[32,96,128]{2,1,0:T(8,128)(2,1)S(1)} %all-to-all-done.rows_ref, bf16[1024,128]{1,0:T(8,128)(2,1)} %make_mixing.1.mix_ref, bf16[2048,192]{1,0:T(8,128)(2,1)} %get-tuple-element.21.refs_0_.q_ref, bf16[2048,192]{1,0:T(8,128)(2,1)} %get-tuple-element.22.refs_1_.k_ref, ...), custom_call_target="tpu_custom_call" | custom-call | tf_op jit(solution)/shard_map/mix_rows/pallas_call | solution.py:119
  45.9 0.7 pad_add_fusion.1.place_ref
  46.5 0.8 collective-permute-done.1
  47.3 0.9 fusion
  48.2 12.2 %all-gather = bf16[4,192,64]{1,2,0:T(8,128)(2,1)S(1)} all-gather(bf16[1,192,64]{1,2,0:T(8,128)(2,1)S(1)} %fusion), channel_id=1, replica_groups=mesh['nodes'=64,'mp'=4] {'mp'}, dimensions={0}, use_global_device_ids=true | all-gather | bytes 122880 | tf_op jit(solution)/shard_map/all_gather | solution.py:440
  60.5 0.1 copy.32
  60.6 0.8 reshape.56
  61.4 19.1 %attend.1 = (bf16[3,2048,64]{2,1,0:T(8,128)(2,1)}, f32[2048,128]{1,0:T(8,128)}, bf16[2048,128]{1,0:T(8,128)(2,1)}, f32[64,192]{1,0:T(8,128)}, bf16[64,192]{1,0:T...) custom-call(s32[4]{0:T(128)} %pad_add_fusion.1.place_ref, bf16[2048,768]{1,0:T(8,128)(2,1)} %bitcast.38, ...), custom_call_target="tpu_custom_call" | custom-call | tf_op jit(solution)/shard_map/attend/pallas_call | solution.py:268
  80.5 0.1 collective-permute-start.6
  80.6 2.1 %collective-permute-done.6 = bf16[2048,128]{1,0:T(8,128)(2,1)S(1)} collective-permute-done((bf16[2048,128]{1,0:T(8,128)(2,1)}, bf16[2048,128]{1,0:T(8,128)(2,1)S(1)}, u32[]{:S(2)}, u32[]{:S(2)}) %collective-permute-start.6) | collective-permute-done | bytes 524320 | tf_op jit(solution)/shard_map/ppermute | solution.py:38
  82.7 2.2 %add_convert_fusion = bf16[2048,128]{1,0:T(8,128)(2,1)} fusion(f32[2048,128]{1,0:T(8,128)} %get-tuple-element.31, bf16[2048,128]{1,0:T(8,128)(2,1)S(1)} %collective-permute-done.6), kind=kLoop, calls=%fused_computation | loop fusion | flops 786432 | bytes 2097152 | tf_op jit(solution)/shard_map/convert_element_type | solution.py:449
  85.0 4.7 %all-to-all-start.2 = ((bf16[32,64,128]{2,1,0:T(8,128)(2,1)}), bf16[32,64,128]{2,1,0:T(8,128)(2,1)S(1)}, u32[]{:S(2)}, u32[]{:S(2)}) async-start(bf16[32,64,128]{2,1,0:T(8,128)(2,1)} %bitcast.16), calls=%async_computation.2 | async-start | bytes 1048576 | tf_op jit(solution)/shard_map/all_to_all | solution.py:50
  89.7 0.2 collective-permute-start.2
  89.9 2.7 %collective-permute-start.3 = (bf16[64,192]{1,0:T(8,128)(2,1)S(1)}, bf16[64,192]{1,0:T(8,128)(2,1)S(1)}, u32[]{:S(2)}, u32[]{:S(2)}) collective-permute-start(bf16[64,192]{1,0:T(8,128)(2,1)S(1)} %copy-done.10), channel_id=1, source_target_pairs={{0,2},{1,3},{2,0},{3,1},{4,6},{5,7},{6,4},{7,5},{8,10},{9,11},{10,... | collective-permute-start | bytes 73736 | tf_op jit(solution)/shard_map/ppermute | solution.py:447
  92.6 1.9 %collective-permute-start.4 = (bf16[64,192]{1,0:T(8,128)(2,1)S(1)}, bf16[64,192]{1,0:T(8,128)(2,1)S(1)}, u32[]{:S(2)}, u32[]{:S(2)}) collective-permute-start(bf16[64,192]{1,0:T(8,128)(2,1)S(1)} %copy-done.9), channel_id=1, source_target_pairs={{0,3},{1,0},{2,1},{3,2},{4,7},{5,4},{6,5},{7,6},{8,11},{9,8},{10,9... | collective-permute-start | bytes 73736 | tf_op jit(solution)/shard_map/ppermute | solution.py:447
  94.5 1.0 collective-permute-done.3
  95.5 1.0 collective-permute-done.4
  96.5 0.1 add_divide_fusion.own_ref
  96.6 0.0 copy-start.4
  96.6 0.1 collective-permute-start.5
  96.7 2.0 %reshape.53.refs_1_ = bf16[3,32,4096]{2,1,0:T(8,128)(2,1)} reshape(bf16[3,2048,64]{2,1,0:T(8,128)(2,1)S(1)} %copy-done.2) | data formatting | bytes 1572864 | tf_op jit(solution)/shard_map/reshape | solution.py:445
  98.8 0.6 copy-done.6
  99.4 2.7 %spread.1.refs_0_ = bf16[32,96,128]{2,1,0:T(8,128)(2,1)} custom-call(f32[64,192]{1,0:T(8,128)} %copy-done.4, f32[64,192]{1,0:T(8,128)} %copy-done.6, bf16[1024,128]{1,0:T(8,128)(2,1)} %make_mixing.1.mix_ref), custom_call_target="tpu_custom_call" | custom-call | tf_op jit(solution)/shard_map/spread/pallas_call | solution.py:320
  102.1 4.6 %all-to-all-done.2.pieces_ref = bf16[32,64,128]{2,1,0:T(8,128)(2,1)S(1)} async-done(((bf16[32,64,128]{2,1,0:T(8,128)(2,1)}), bf16[32,64,128]{2,1,0:T(8,128)(2,1)S(1)}, u32[]{:S(2)}, u32[]{:S(2)}) %all-to-all-start.2) | async-done | bytes 524320 | tf_op jit(solution)/shard_map/all_to_all | solution.py:50
  106.7 5.7 %all-to-all-start.1 = ((bf16[32,96,128]{2,1,0:T(8,128)(2,1)}), bf16[32,96,128]{2,1,0:T(8,128)(2,1)S(1)}, u32[]{:S(2)}, u32[]{:S(2)}) async-start(bf16[32,96,128]{2,1,0:T(8,128)(2,1)} %spread.1.refs_0_), calls=%async_computation.1 | async-start | bytes 1572864 | tf_op jit(solution)/shard_map/all_to_all | solution.py:50
  112.5 0.7 sum_pieces.1
  113.2 3.6 %collective-permute-start.9 = (bf16[64,128]{1,0:T(8,128)(2,1)}, bf16[64,128]{1,0:T(8,128)(2,1)S(1)}, u32[]{:S(2)}, u32[]{:S(2)}) collective-permute-start(bf16[64,128]{1,0:T(8,128)(2,1)} %sum_pieces.1), channel_id=1, source_target_pairs={{0,24},{4,28},{8,32},{12,36},{16,40},{20,44},{24,48},{28,52},{32,5... | collective-permute-start | bytes 49160 | tf_op jit(solution)/shard_map/ppermute | solution.py:46
  116.8 2.7 %collective-permute-start.8 = (bf16[64,128]{1,0:T(8,128)(2,1)}, bf16[64,128]{1,0:T(8,128)(2,1)S(1)}, u32[]{:S(2)}, u32[]{:S(2)}) collective-permute-start(bf16[64,128]{1,0:T(8,128)(2,1)} %sum_pieces.1), channel_id=1, source_target_pairs={{0,16},{4,20},{8,24},{12,28},{16,32},{20,36},{24,40},{28,44},{32,4... | collective-permute-start | bytes 49160 | tf_op jit(solution)/shard_map/ppermute | solution.py:46
  119.5 0.6 collective-permute-start.7
  120.0 0.8 constant_dynamic-update-slice_fusion.4
  120.8 13.9 %collective-permute-done.9 = bf16[64,128]{1,0:T(8,128)(2,1)S(1)} collective-permute-done((bf16[64,128]{1,0:T(8,128)(2,1)}, bf16[64,128]{1,0:T(8,128)(2,1)S(1)}, u32[]{:S(2)}, u32[]{:S(2)}) %collective-permute-start.9) | collective-permute-done | bytes 16416 | tf_op jit(solution)/shard_map/ppermute | solution.py:46
  134.7 0.3 collective-permute-done.8
  135.0 0.7 pad_maximum_fusion.1
  135.7 3.1 %collective-permute-start.10 = (bf16[4,64,128]{2,1,0:T(8,128)(2,1)S(1)}, bf16[4,64,128]{2,1,0:T(8,128)(2,1)S(1)}, u32[]{:S(2)}, u32[]{:S(2)}) collective-permute-start(bf16[4,64,128]{2,1,0:T(8,128)(2,1)S(1)} %pad_maximum_fusion.1), channel_id=1, source_target_pairs={{0,32},{4,36},{8,40},{12,44},{16,48},{20,52},{24,56},{28,60},{32,0... | collective-permute-start | bytes 196616 | tf_op jit(solution)/shard_map/ppermute | solution.py:46
  138.8 5.4 %collective-permute-done.10 = bf16[4,64,128]{2,1,0:T(8,128)(2,1)S(1)} collective-permute-done((bf16[4,64,128]{2,1,0:T(8,128)(2,1)S(1)}, bf16[4,64,128]{2,1,0:T(8,128)(2,1)S(1)}, u32[]{:S(2)}, u32[]{:S(2)}) %collective-permute-start.10) | collective-permute-done | bytes 65568 | tf_op jit(solution)/shard_map/ppermute | solution.py:46
  144.3 2.7 %collective-permute-start.13 = (bf16[8,64,128]{2,1,0:T(8,128)(2,1)S(1)}, bf16[8,64,128]{2,1,0:T(8,128)(2,1)S(1)}, u32[]{:S(2)}, u32[]{:S(2)}) collective-permute-start(bf16[8,64,128]{2,1,0:T(8,128)(2,1)S(1)} %constant_dynamic-update-slice_fusion), channel_id=1, source_target_pairs={{0,192},{4,196},{8,200},{12,204},{16,208},{20,212},{24,216},{28,22... | collective-permute-start | bytes 393224 | tf_op jit(solution)/shard_map/ppermute | solution.py:46
  147.0 0.8 collective-permute-start.12
  147.8 0.9 collective-permute-start.11
  148.7 2.3 %collective-permute-done.13 = bf16[8,64,128]{2,1,0:T(8,128)(2,1)S(1)} collective-permute-done((bf16[8,64,128]{2,1,0:T(8,128)(2,1)S(1)}, bf16[8,64,128]{2,1,0:T(8,128)(2,1)S(1)}, u32[]{:S(2)}, u32[]{:S(2)}) %collective-permute-start.13) | collective-permute-done | bytes 131104 | tf_op jit(solution)/shard_map/ppermute | solution.py:46
  150.9 2.6 %collective-permute-done.12 = bf16[8,64,128]{2,1,0:T(8,128)(2,1)S(1)} collective-permute-done((bf16[8,64,128]{2,1,0:T(8,128)(2,1)S(1)}, bf16[8,64,128]{2,1,0:T(8,128)(2,1)S(1)}, u32[]{:S(2)}, u32[]{:S(2)}) %collective-permute-start.12) | collective-permute-done | bytes 131104 | tf_op jit(solution)/shard_map/ppermute | solution.py:46
  153.6 1.3 collective-permute-done.11
  154.9 0.1 pad_maximum_fusion.mine_ref
  155.0 0.1 collective-permute-start.14
  155.1 0.7 reshape_reshape.3.index_ref
  155.8 1.2 collective-permute-done.14.theirs_ref
  157.0 6.5 %scatter_rows.1 = (f32[192,2048]{1,0:T(8,128)}, f32[192,768]{1,0:T(8,128)}, f32[192,768]{1,0:T(8,128)}, f32[192,768]{1,0:T(8,128)}) custom-call(s32[4]{0:T(128)} %pad_add_fusion.1.place_ref, s32[1,2048]{1,0:T(1,128)} %reshape_reshape.3.index_ref, bf16[32,96,128]{2,1,0:T(8,128)(2,1)S(1)} %all-to-all-done.1.rows_ref, ...), custom_call_target="tpu_custom_call" | custom-call | tf_op jit(solution)/shard_map/scatter_rows/pallas_call | solution.py:390
  (35 shorter events, 0.1 us)
Async XLA Ops:
  2.3 18.2 %copy-start.7 = (s32[32,2,32]{2,1,0:T(2,128)S(1)}, s32[32,2,32]{2,1,0:T(2,128)}, u32[]{:S(2)}) copy-start(s32[32,2,32]{2,1,0:T(2,128)} %param.16) | copy-start | bytes 24580
  2.3 18.2 %copy-start.8 = (s32[32,2]{0,1:T(2,128)S(1)}, s32[32,2]{0,1:T(2,128)}, u32[]{:S(2)}) copy-start(s32[32,2]{0,1:T(2,128)} %param.17) | copy-start | bytes 772
  2.3 18.6 %copy-start = (bf16[192,768]{1,0:T(8,128)(2,1)S(1)}, bf16[192,768]{1,0:T(8,128)(2,1)}, u32[]{:S(2)}) copy-start(bf16[192,768]{1,0:T(8,128)(2,1)} %wk_ref.3) | copy-start | bytes 884740
  9.0 12.2 %copy-start.1 = (bf16[192,768]{1,0:T(8,128)(2,1)S(1)}, bf16[192,768]{1,0:T(8,128)(2,1)}, u32[]{:S(2)}) copy-start(bf16[192,768]{1,0:T(8,128)(2,1)} %wv_ref.3) | copy-start | bytes 884740
  9.0 34.8 %all-to-all-start = ((bf16[32,96,128]{2,1,0:T(8,128)(2,1)}), bf16[32,96,128]{2,1,0:T(8,128)(2,1)S(1)}, u32[]{:S(2)}, u32[]{:S(2)}) async-start(bf16[32,96,128]{2,1,0:T(8,128)(2,1)} %gather_rows.1), calls=%async_computation | async-start | bytes 1572864 | tf_op jit(solution)/shard_map/all_to_all | solution.py:50
  20.4 2.1 %copy-start.3 = (bf16[32,3,4096]{2,0,1:T(8,128)(2,1)S(1)}, bf16[32,3,4096]{2,0,1:T(8,128)(2,1)}, u32[]{:S(2)}) copy-start(bf16[32,3,4096]{2,0,1:T(8,128)(2,1)} %param.13) | copy-start | bytes 2359300
  20.7 10.4 %collective-permute-start = (s32[64,32]{0,1:T(8,128)S(1)}, s32[64,32]{0,1:T(8,128)S(1)}, u32[]{:S(2)}, u32[]{:S(2)}) collective-permute-start(s32[64,32]{0,1:T(8,128)S(1)} %fusion.1), channel_id=1, source_target_pairs={{0,4},{4,0},{8,12},{12,8},{16,20},{20,16},{24,28},{28,24},{32,36},... | collective-permute-start | bytes 24584 | tf_op jit(solution)/shard_map/ppermute | solution.py:38
  45.9 1.5 collective-permute-start.1
  80.5 2.2 %collective-permute-start.6 = (bf16[2048,128]{1,0:T(8,128)(2,1)}, bf16[2048,128]{1,0:T(8,128)(2,1)S(1)}, u32[]{:S(2)}, u32[]{:S(2)}) collective-permute-start(bf16[2048,128]{1,0:T(8,128)(2,1)} %get-tuple-element.32), channel_id=1, source_target_pairs={{0,4},{4,0},{8,12},{12,8},{16,20},{20,16},{24,28},{28,24},{32,36},... | collective-permute-start | bytes 1572872 | tf_op jit(solution)/shard_map/ppermute | solution.py:38
  82.7 7.0 %copy-start.11 = (bf16[64,192]{1,0:T(8,128)(2,1)S(1)}, bf16[64,192]{1,0:T(8,128)(2,1)}, u32[]{:S(2)}) copy-start(bf16[64,192]{1,0:T(8,128)(2,1)} %get-tuple-element.28) | copy-start | bytes 73732
  82.7 7.2 %copy-start.10 = (bf16[64,192]{1,0:T(8,128)(2,1)S(1)}, bf16[64,192]{1,0:T(8,128)(2,1)}, u32[]{:S(2)}) copy-start(bf16[64,192]{1,0:T(8,128)(2,1)} %get-tuple-element.29) | copy-start | bytes 73732
  82.7 9.9 %copy-start.9 = (bf16[64,192]{1,0:T(8,128)(2,1)S(1)}, bf16[64,192]{1,0:T(8,128)(2,1)}, u32[]{:S(2)}) copy-start(bf16[64,192]{1,0:T(8,128)(2,1)} %get-tuple-element.30) | copy-start | bytes 73732
  82.7 13.8 %copy-start.5 = (f32[64,192]{1,0:T(8,128)S(1)}, f32[64,192]{1,0:T(8,128)}, u32[]{:S(2)}) copy-start(f32[64,192]{1,0:T(8,128)} %get-tuple-element.27) | copy-start | bytes 147460
  82.7 14.0 %copy-start.2 = (bf16[3,2048,64]{2,1,0:T(8,128)(2,1)S(1)}, bf16[3,2048,64]{2,1,0:T(8,128)(2,1)}, u32[]{:S(2)}) copy-start(bf16[3,2048,64]{2,1,0:T(8,128)(2,1)} %get-tuple-element.26) | copy-start | bytes 2359300
  85.0 21.8 %all-to-all-start.2 = ((bf16[32,64,128]{2,1,0:T(8,128)(2,1)}), bf16[32,64,128]{2,1,0:T(8,128)(2,1)S(1)}, u32[]{:S(2)}, u32[]{:S(2)}) async-start(bf16[32,64,128]{2,1,0:T(8,128)(2,1)} %bitcast.16), calls=%async_computation.2 | async-start | bytes 1048576 | tf_op jit(solution)/shard_map/all_to_all | solution.py:50
  89.7 4.8 %collective-permute-start.2 = (bf16[64,192]{1,0:T(8,128)(2,1)S(1)}, bf16[64,192]{1,0:T(8,128)(2,1)S(1)}, u32[]{:S(2)}, u32[]{:S(2)}) collective-permute-start(bf16[64,192]{1,0:T(8,128)(2,1)S(1)} %copy-done.11), channel_id=1, source_target_pairs={{0,1},{1,2},{2,3},{3,0},{4,5},{5,6},{6,7},{7,4},{8,9},{9,10},{10,1... | collective-permute-start | bytes 73736 | tf_op jit(solution)/shard_map/ppermute | solution.py:447
  89.9 5.6 %collective-permute-start.3 = (bf16[64,192]{1,0:T(8,128)(2,1)S(1)}, bf16[64,192]{1,0:T(8,128)(2,1)S(1)}, u32[]{:S(2)}, u32[]{:S(2)}) collective-permute-start(bf16[64,192]{1,0:T(8,128)(2,1)S(1)} %copy-done.10), channel_id=1, source_target_pairs={{0,2},{1,3},{2,0},{3,1},{4,6},{5,7},{6,4},{7,5},{8,10},{9,11},{10,... | collective-permute-start | bytes 73736 | tf_op jit(solution)/shard_map/ppermute | solution.py:447
  92.6 3.9 %collective-permute-start.4 = (bf16[64,192]{1,0:T(8,128)(2,1)S(1)}, bf16[64,192]{1,0:T(8,128)(2,1)S(1)}, u32[]{:S(2)}, u32[]{:S(2)}) collective-permute-start(bf16[64,192]{1,0:T(8,128)(2,1)S(1)} %copy-done.9), channel_id=1, source_target_pairs={{0,3},{1,0},{2,1},{3,2},{4,7},{5,4},{6,5},{7,6},{8,11},{9,8},{10,9... | collective-permute-start | bytes 73736 | tf_op jit(solution)/shard_map/ppermute | solution.py:447
  96.6 2.2 %copy-start.4 = (f32[64,192]{1,0:T(8,128)}, f32[64,192]{1,0:T(8,128)S(1)}, u32[]{:S(2)}) copy-start(f32[64,192]{1,0:T(8,128)S(1)} %add_divide_fusion.own_ref) | copy-start | bytes 147460
  96.6 2.2 %collective-permute-start.5 = (f32[64,192]{1,0:T(8,128)S(1)}, f32[64,192]{1,0:T(8,128)S(1)}, u32[]{:S(2)}, u32[]{:S(2)}) collective-permute-start(f32[64,192]{1,0:T(8,128)S(1)} %add_divide_fusion.own_ref), channel_id=1, source_target_pairs={{0,4},{4,0},{8,12},{12,8},{16,20},{20,16},{24,28},{28,24},{32,36},... | collective-permute-start | bytes 147464 | tf_op jit(solution)/shard_map/ppermute | solution.py:38
  98.8 0.6 copy-start.6
  106.7 49.0 %all-to-all-start.1 = ((bf16[32,96,128]{2,1,0:T(8,128)(2,1)}), bf16[32,96,128]{2,1,0:T(8,128)(2,1)S(1)}, u32[]{:S(2)}, u32[]{:S(2)}) async-start(bf16[32,96,128]{2,1,0:T(8,128)(2,1)} %spread.1.refs_0_), calls=%async_computation.1 | async-start | bytes 1572864 | tf_op jit(solution)/shard_map/all_to_all | solution.py:50
  113.2 21.5 %collective-permute-start.9 = (bf16[64,128]{1,0:T(8,128)(2,1)}, bf16[64,128]{1,0:T(8,128)(2,1)S(1)}, u32[]{:S(2)}, u32[]{:S(2)}) collective-permute-start(bf16[64,128]{1,0:T(8,128)(2,1)} %sum_pieces.1), channel_id=1, source_target_pairs={{0,24},{4,28},{8,32},{12,36},{16,40},{20,44},{24,48},{28,52},{32,5... | collective-permute-start | bytes 49160 | tf_op jit(solution)/shard_map/ppermute | solution.py:46
  116.8 18.2 %collective-permute-start.8 = (bf16[64,128]{1,0:T(8,128)(2,1)}, bf16[64,128]{1,0:T(8,128)(2,1)S(1)}, u32[]{:S(2)}, u32[]{:S(2)}) collective-permute-start(bf16[64,128]{1,0:T(8,128)(2,1)} %sum_pieces.1), channel_id=1, source_target_pairs={{0,16},{4,20},{8,24},{12,28},{16,32},{20,36},{24,40},{28,44},{32,4... | collective-permute-start | bytes 49160 | tf_op jit(solution)/shard_map/ppermute | solution.py:46
  119.5 15.6 %collective-permute-start.7 = (bf16[64,128]{1,0:T(8,128)(2,1)}, bf16[64,128]{1,0:T(8,128)(2,1)S(1)}, u32[]{:S(2)}, u32[]{:S(2)}) collective-permute-start(bf16[64,128]{1,0:T(8,128)(2,1)} %sum_pieces.1), channel_id=1, source_target_pairs={{0,8},{4,12},{8,16},{12,20},{16,24},{20,28},{24,32},{28,36},{32,40... | collective-permute-start | bytes 49160 | tf_op jit(solution)/shard_map/ppermute | solution.py:46
  135.7 8.5 %collective-permute-start.10 = (bf16[4,64,128]{2,1,0:T(8,128)(2,1)S(1)}, bf16[4,64,128]{2,1,0:T(8,128)(2,1)S(1)}, u32[]{:S(2)}, u32[]{:S(2)}) collective-permute-start(bf16[4,64,128]{2,1,0:T(8,128)(2,1)S(1)} %pad_maximum_fusion.1), channel_id=1, source_target_pairs={{0,32},{4,36},{8,40},{12,44},{16,48},{20,52},{24,56},{28,60},{32,0... | collective-permute-start | bytes 196616 | tf_op jit(solution)/shard_map/ppermute | solution.py:46
  144.3 6.7 %collective-permute-start.13 = (bf16[8,64,128]{2,1,0:T(8,128)(2,1)S(1)}, bf16[8,64,128]{2,1,0:T(8,128)(2,1)S(1)}, u32[]{:S(2)}, u32[]{:S(2)}) collective-permute-start(bf16[8,64,128]{2,1,0:T(8,128)(2,1)S(1)} %constant_dynamic-update-slice_fusion), channel_id=1, source_target_pairs={{0,192},{4,196},{8,200},{12,204},{16,208},{20,212},{24,216},{28,22... | collective-permute-start | bytes 393224 | tf_op jit(solution)/shard_map/ppermute | solution.py:46
  147.0 6.6 %collective-permute-start.12 = (bf16[8,64,128]{2,1,0:T(8,128)(2,1)S(1)}, bf16[8,64,128]{2,1,0:T(8,128)(2,1)S(1)}, u32[]{:S(2)}, u32[]{:S(2)}) collective-permute-start(bf16[8,64,128]{2,1,0:T(8,128)(2,1)S(1)} %constant_dynamic-update-slice_fusion), channel_id=1, source_target_pairs={{0,128},{4,132},{8,136},{12,140},{16,144},{20,148},{24,152},{28,15... | collective-permute-start | bytes 393224 | tf_op jit(solution)/shard_map/ppermute | solution.py:46
  147.8 7.1 %collective-permute-start.11 = (bf16[8,64,128]{2,1,0:T(8,128)(2,1)S(1)}, bf16[8,64,128]{2,1,0:T(8,128)(2,1)S(1)}, u32[]{:S(2)}, u32[]{:S(2)}) collective-permute-start(bf16[8,64,128]{2,1,0:T(8,128)(2,1)S(1)} %constant_dynamic-update-slice_fusion), channel_id=1, source_target_pairs={{0,64},{4,68},{8,72},{12,76},{16,80},{20,84},{24,88},{28,92},{32,9... | collective-permute-start | bytes 393224 | tf_op jit(solution)/shard_map/ppermute | solution.py:46
  155.0 2.0 %collective-permute-start.14 = (bf16[4,8,64,128]{3,2,1,0:T(8,128)(2,1)S(1)}, bf16[4,8,64,128]{3,2,1,0:T(8,128)(2,1)S(1)}, u32[]{:S(2)}, u32[]{:S(2)}) collective-permute-start(bf16[4,8,64,128]{3,2,1,0:T(8,128)(2,1)S(1)} %pad_maximum_fusion.mine_ref), channel_id=1, source_target_pairs={{0,4},{4,0},{8,12},{12,8},{16,20},{20,16},{24,28},{28,24},{32,36},... | collective-permute-start | bytes 1572872 | tf_op jit(solution)/shard_map/ppermute | solution.py:38
